TPU v7x, 32 devices: a whole 2x2x4 slice. The times are simulated.
32 devices in a mesh: dp: 2 (over core), seq: 4 (over y, x), heads: 4 (over z).
Axes of the slice: x: 2, y: 2, z: 4, core: 2. Of those that a mesh axis runs over, the one named last changes fastest.
Arguments:
- residual: bfloat16 [6, 1536, 1536], P('dp', ('seq', 'heads')), may hold values from -6 to 6
- out_grad: bfloat16 [6, 1536, 1536], P('dp', 'seq'), may hold values from -6 to 6
- lengths: int32 [6], P('dp'), may hold values from 384 to 1536, as said below
- attn_gain: bfloat16 [1536], replicated, may hold values from 0.25 to 1.75
- query_weight: bfloat16 [1536, 1536], P(None, 'heads'), may hold values from -0.21875 to 0.21875
- query_bias: bfloat16 [1536], P('heads'), may hold values from -4 to 4
- key_weight: bfloat16 [1536, 256], replicated, may hold values from -0.21875 to 0.21875
- key_bias: bfloat16 [256], replicated, may hold values from -4 to 4
- value_weight: bfloat16 [1536, 256], replicated, may hold values from -0.15625 to 0.15625
- value_bias: bfloat16 [256], replicated, may hold values from -4 to 4
- output_weight: bfloat16 [1536, 1536], P('heads'), may hold values from -0.4375 to 0.4375
- ffn_gain: bfloat16 [1536], replicated, may hold values from 0.25 to 1.75
- gate_weight: bfloat16 [1536, 8960], P(('dp', 'seq'), 'heads'), may hold values from -0.15625 to 0.15625
- up_weight: bfloat16 [1536, 8960], P(('dp', 'seq'), 'heads'), may hold values from -0.15625 to 0.15625
- down_weight: bfloat16 [8960, 1536], P('heads', ('dp', 'seq')), may hold values from -0.0625 to 0.0625
Outputs:
- block_out: bfloat16 [6, 1536, 1536], P('dp', ('seq', 'heads'))
- residual_grad: float32 [6, 1536, 1536], P('dp', ('seq', 'heads'))
- attn_gain_grad: float32 [1536], P(('dp', 'seq', 'heads'))
- query_weight_grad: float32 [1536, 1536], P(('dp', 'seq'), 'heads')
- query_bias_grad: float32 [1536], P('heads')
- key_weight_grad: float32 [1536, 256], P(('dp', 'seq'), 'heads')
- key_bias_grad: float32 [256], P('heads')
- value_weight_grad: float32 [1536, 256], P(('dp', 'seq'), 'heads')
- value_bias_grad: float32 [256], P('heads')
- output_weight_grad: float32 [1536, 1536], P('heads', ('dp', 'seq'))
- ffn_gain_grad: float32 [1536], P(('dp', 'seq', 'heads'))
- gate_weight_grad: float32 [1536, 8960], P(('dp', 'seq'), 'heads')
- up_weight_grad: float32 [1536, 8960], P(('dp', 'seq'), 'heads')
- down_weight_grad: float32 [8960, 1536], P('heads', ('dp', 'seq'))
Inputs may be any that keep to these rules, and one draw needn't show every extreme that they name: `lengths`: each row is valid up to its length and padded after it; at least one row has length exactly 1536.
All inputs are finite; a program needn't handle non-finite values.
Results may differ from a plain program's by a relative error of at most 0.019.
Values may be sent and summed in bfloat16 or wider, within the bound.
No kernel may reach another device: no remote copies, remote signals or barrier semaphores. Data moves between devices by JAX's collectives and lax.ppermute only.
A program may use at most 256 MiB of HBM per device.

v0:
```python
import jax
import jax.numpy as jnp
from jax import lax
from jax.sharding import PartitionSpec as P

H = 12
KVH = 2
HD = 128


epsilon = 1e-06
rope_base = 1000000.0
masked_value = -1000000000.0


def partner(value, axis, stride):
    mask = 2**stride
    pairs = [(source, source ^ mask) for source in range(lax.axis_size(axis))]
    return lax.ppermute(value, axis, pairs)


def rms_scale(values):
    return lax.rsqrt(jnp.mean(values * values, axis=-1, keepdims=True) + epsilon)


def rotate(values):
    middle = values.shape[-1] // 2
    return jnp.concatenate([-values[..., middle:], values[..., :middle]], axis=-1)


def angles(positions, head_size):
    inverse_freq = rope_base ** (
        -jnp.arange(0, head_size // 2, dtype=jnp.float32) * 2.0 / head_size
    )
    phase_grid = positions[:, None] * inverse_freq[None, :]
    phase_grid = jnp.concatenate([phase_grid, phase_grid], axis=-1)
    return (jnp.cos(phase_grid), jnp.sin(phase_grid))


def norm_back(upstream, normed, inv_rms, gain_row):
    scaled = upstream * gain_row
    return inv_rms * (scaled - normed * jnp.mean(scaled * normed, axis=-1, keepdims=True))


def local(
    residual,
    out_grad,
    lengths,
    attn_gain,
    query_weight,
    query_bias,
    key_weight,
    key_bias,
    value_weight,
    value_bias,
    output_weight,
    ffn_gain,
    gate_weight,
    up_weight,
    down_weight,
):
    row_count, own_len, model_width = residual.shape
    head_size = HD
    query_width = query_weight.shape[1]
    query_heads = query_width // head_size
    half_size = head_size // 2
    heads_index = lax.axis_index("heads")
    seq_index = lax.axis_index("seq")
    group_index = heads_index * query_heads // (H // KVH)
    side_index = heads_index % 2
    first_gain = attn_gain.astype(jnp.float32)
    second_gain = ffn_gain.astype(jnp.float32)
    key_group = lax.dynamic_slice_in_dim(key_weight, group_index * head_size, head_size, 1)
    value_group = lax.dynamic_slice_in_dim(value_weight, group_index * head_size, head_size, 1)
    key_shift = lax.dynamic_slice_in_dim(key_bias, group_index * head_size, head_size, 0).astype(
        jnp.float32
    )
    value_shift = lax.dynamic_slice_in_dim(
        value_bias, group_index * head_size, head_size, 0
    ).astype(jnp.float32)
    gathered = lax.all_gather(residual, "heads", axis=1, tiled=True)
    shard_len = gathered.shape[1]
    token_count = row_count * shard_len
    stream = gathered.astype(jnp.float32).reshape(token_count, model_width)
    first_scale = rms_scale(stream)
    first_normed = stream * first_scale
    first_input = (first_normed * first_gain).astype(jnp.bfloat16)
    query_pos = seq_index * shard_len + jnp.arange(shard_len, dtype=jnp.int32)
    cosine, sine = angles(query_pos.astype(jnp.float32), head_size)
    cos_query = cosine[None, :, None, :]
    sin_query = sine[None, :, None, :]
    cos_key = cosine[None]
    sin_key = sine[None]
    query_lin = (
        jnp.dot(first_input, query_weight, preferred_element_type=jnp.float32)
        + query_bias.astype(jnp.float32)
    ).reshape(row_count, shard_len, query_heads, head_size)
    query_rotated_rows = (query_lin * cos_query + rotate(query_lin) * sin_query).astype(
        jnp.bfloat16
    )
    key_lin = (
        jnp.dot(first_input, key_group, preferred_element_type=jnp.float32) + key_shift
    ).reshape(row_count, shard_len, head_size)
    key_rot = (key_lin * cos_key + rotate(key_lin) * sin_key).astype(jnp.bfloat16)
    value_own = (
        (jnp.dot(first_input, value_group, preferred_element_type=jnp.float32) + value_shift)
        .astype(jnp.bfloat16)
        .reshape(row_count, shard_len, head_size)
    )
    key_full_rows, value_full_rows = (
        lax.all_gather(key_rot, "seq", axis=1, tiled=True),
        lax.all_gather(value_own, "seq", axis=1, tiled=True),
    )
    key_pos = jnp.arange(key_full_rows.shape[1], dtype=jnp.int32)
    visible = (key_pos[None, None, :] <= query_pos[None, :, None]) & (
        key_pos[None, None, :] < lengths[:, None, None]
    )
    visible = visible[:, :, None, :]
    score_scale = head_size ** (-0.5)

    def masked_logits():
        unscaled_scores = jnp.einsum(
            "fvyl,fil->fvyi", query_rotated_rows, key_full_rows, preferred_element_type=jnp.float32
        )
        return jnp.where(visible, unscaled_scores * score_scale, masked_value)

    logits = masked_logits()
    peak = jnp.max(logits, axis=-1, keepdims=True)
    shifted_exp = jnp.exp(logits - peak)
    total = jnp.sum(shifted_exp, axis=-1, keepdims=True)
    probabilities_reduced = (shifted_exp / total).astype(jnp.bfloat16)
    log_total = peak + jnp.log(total)
    attended = (
        jnp.einsum(
            "iaeg,ign->iaen",
            probabilities_reduced,
            value_full_rows,
            preferred_element_type=jnp.float32,
        )
        .astype(jnp.bfloat16)
        .reshape(token_count, query_width)
    )
    attn_part = jnp.dot(attended, output_weight, preferred_element_type=jnp.float32)
    second_stream = stream + lax.psum(attn_part, "heads")
    second_scale = rms_scale(second_stream)
    second_normed = second_stream * second_scale
    second_input = (second_normed * second_gain).astype(jnp.bfloat16)
    gate_full, up_full, down_full = (
        lax.all_gather(gate_weight, ("dp", "seq"), axis=0, tiled=True),
        lax.all_gather(up_weight, ("dp", "seq"), axis=0, tiled=True),
        lax.all_gather(down_weight, ("dp", "seq"), axis=1, tiled=True),
    )
    gate_act = jnp.dot(second_input, gate_full, preferred_element_type=jnp.float32)
    up_act = jnp.dot(second_input, up_full, preferred_element_type=jnp.float32)
    sigmoid_gate = jax.nn.sigmoid(gate_act)
    silu_gate = jax.nn.silu(gate_act)
    hidden = (silu_gate * up_act).astype(jnp.bfloat16)
    ffn_part = jnp.dot(hidden, down_full, preferred_element_type=jnp.float32).reshape(
        row_count, shard_len, model_width
    )
    ffn_own = lax.psum_scatter(
        ffn_part.astype(jnp.bfloat16), "heads", scatter_dimension=1, tiled=True
    ).astype(jnp.float32)
    stream_own = lax.dynamic_slice_in_dim(
        second_stream.reshape(row_count, shard_len, model_width), heads_index * own_len, own_len, 1
    )
    block_out = (stream_own + ffn_own).astype(jnp.bfloat16)
    grad_flat = out_grad.reshape(token_count, model_width)
    grad_hidden = jnp.einsum("td,fd->tf", grad_flat, down_full, preferred_element_type=jnp.float32)
    grad_gate = (
        grad_hidden * up_act * sigmoid_gate * (1.0 + gate_act * (1.0 - sigmoid_gate))
    ).astype(jnp.bfloat16)
    grad_up = (grad_hidden * silu_gate).astype(jnp.bfloat16)
    down_grad = jnp.einsum("tf,td->fd", hidden, grad_flat, preferred_element_type=jnp.float32)
    gate_grad = jnp.einsum("td,tf->df", second_input, grad_gate, preferred_element_type=jnp.float32)
    up_grad = jnp.einsum("td,tf->df", second_input, grad_up, preferred_element_type=jnp.float32)
    second_back = jnp.einsum(
        "tf,df->td", grad_gate, gate_full, preferred_element_type=jnp.float32
    ) + jnp.einsum("tf,df->td", grad_up, up_full, preferred_element_type=jnp.float32)
    second_gain_term = jnp.sum(second_back * second_normed, axis=0)
    second_spread = norm_back(second_back, second_normed, second_scale, second_gain)
    grad_stream = grad_flat.astype(jnp.float32) + lax.psum(second_spread, "heads")
    grad_attn = grad_stream.astype(jnp.bfloat16)
    output_grad = jnp.einsum("tq,td->qd", attended, grad_attn, preferred_element_type=jnp.float32)
    attended_output_gradient = (
        jnp.einsum("td,qd->tq", grad_attn, output_weight, preferred_element_type=jnp.float32)
        .astype(jnp.bfloat16)
        .reshape(row_count, shard_len, query_heads, head_size)
    )
    probs = jnp.exp(masked_logits() - log_total)
    grad_probs = jnp.einsum(
        "fvyl,fil->fvyi",
        attended_output_gradient,
        value_full_rows,
        preferred_element_type=jnp.float32,
    )
    logits_gradient = (
        probs * (grad_probs - jnp.sum(probs * grad_probs, axis=-1, keepdims=True)) * score_scale
    ).astype(jnp.bfloat16)
    grad_query_rot = jnp.einsum(
        "iaeg,ign->iaen", logits_gradient, key_full_rows, preferred_element_type=jnp.float32
    )
    grad_key_all = jnp.einsum(
        "lnya,lnyz->laz", logits_gradient, query_rotated_rows, preferred_element_type=jnp.float32
    )
    grad_value_all = jnp.einsum(
        "lnya,lnyz->laz",
        probs.astype(jnp.bfloat16),
        attended_output_gradient,
        preferred_element_type=jnp.float32,
    )
    grad_query = (
        (grad_query_rot * cos_query - rotate(grad_query_rot) * sin_query)
        .astype(jnp.bfloat16)
        .reshape(token_count, query_width)
    )
    key_value_own = (
        lax.psum_scatter(grad_key_all, "seq", scatter_dimension=1, tiled=True),
        lax.psum_scatter(grad_value_all, "seq", scatter_dimension=1, tiled=True),
    )
    pair_stack = jnp.stack(key_value_own)
    pair_stack = pair_stack + partner(pair_stack, "heads", 0)
    grad_key_rot = pair_stack[0]
    grad_key = (
        (grad_key_rot * cos_key - rotate(grad_key_rot) * sin_key)
        .astype(jnp.bfloat16)
        .reshape(token_count, head_size)
    )
    grad_value = pair_stack[1].astype(jnp.bfloat16).reshape(token_count, head_size)
    grad_key_half = lax.dynamic_slice_in_dim(grad_key, side_index * half_size, half_size, 1)
    grad_value_half = lax.dynamic_slice_in_dim(grad_value, side_index * half_size, half_size, 1)
    key_half = lax.dynamic_slice_in_dim(key_group, side_index * half_size, half_size, 1)
    value_half = lax.dynamic_slice_in_dim(value_group, side_index * half_size, half_size, 1)
    query_grad = jnp.einsum(
        "td,tq->dq", first_input, grad_query, preferred_element_type=jnp.float32
    )
    key_grad = jnp.einsum(
        "td,tq->dq", first_input, grad_key_half, preferred_element_type=jnp.float32
    )
    value_grad = jnp.einsum(
        "td,tq->dq", first_input, grad_value_half, preferred_element_type=jnp.float32
    )
    first_back = jnp.einsum(
        "tq,dq->td", grad_query, query_weight, preferred_element_type=jnp.float32
    )
    first_back = first_back + jnp.einsum(
        "tq,dq->td", grad_key_half, key_half, preferred_element_type=jnp.float32
    )
    first_back = first_back + jnp.einsum(
        "tq,dq->td", grad_value_half, value_half, preferred_element_type=jnp.float32
    )
    first_gain_term = jnp.sum(first_back * first_normed, axis=0)
    first_spread = norm_back(first_back, first_normed, first_scale, first_gain).reshape(
        row_count, shard_len, model_width
    )
    grad_stream_own = lax.dynamic_slice_in_dim(
        grad_stream.reshape(row_count, shard_len, model_width), heads_index * own_len, own_len, 1
    )
    residual_grad = (
        lax.psum_scatter(
            first_spread.astype(jnp.bfloat16), "heads", scatter_dimension=1, tiled=True
        ).astype(jnp.float32)
        + grad_stream_own
    )
    query_shift_term = lax.dynamic_update_slice_in_dim(
        jnp.zeros((H * HD,), jnp.float32),
        jnp.sum(grad_query.astype(jnp.float32), axis=0),
        heads_index * query_width,
        0,
    )
    key_shift_term = lax.dynamic_update_slice_in_dim(
        jnp.zeros((KVH * HD,), jnp.float32),
        jnp.sum(grad_key_half.astype(jnp.float32), axis=0),
        heads_index * half_size,
        0,
    )
    value_shift_term = lax.dynamic_update_slice_in_dim(
        jnp.zeros((KVH * HD,), jnp.float32),
        jnp.sum(grad_value_half.astype(jnp.float32), axis=0),
        heads_index * half_size,
        0,
    )
    small_sums = lax.psum(
        (first_gain_term, second_gain_term, query_shift_term, key_shift_term, value_shift_term),
        ("dp", "seq", "heads"),
    )
    gain_piece = model_width // lax.axis_size(("dp", "seq", "heads"))
    piece_index = lax.axis_index(("dp", "seq", "heads"))
    attn_gain_grad = lax.dynamic_slice_in_dim(
        small_sums[0], piece_index * gain_piece, gain_piece, 0
    )
    ffn_gain_grad = lax.dynamic_slice_in_dim(small_sums[1], piece_index * gain_piece, gain_piece, 0)
    query_bias_grad = lax.dynamic_slice_in_dim(
        small_sums[2], heads_index * query_width, query_width, 0
    )
    key_bias_grad = lax.dynamic_slice_in_dim(small_sums[3], heads_index * half_size, half_size, 0)
    value_bias_grad = lax.dynamic_slice_in_dim(small_sums[4], heads_index * half_size, half_size, 0)
    weight_sums = (
        lax.psum_scatter(
            query_grad.astype(jnp.bfloat16), ("dp", "seq"), scatter_dimension=0, tiled=True
        ).astype(jnp.float32),
        lax.psum_scatter(
            key_grad.astype(jnp.bfloat16), ("dp", "seq"), scatter_dimension=0, tiled=True
        ).astype(jnp.float32),
        lax.psum_scatter(
            value_grad.astype(jnp.bfloat16), ("dp", "seq"), scatter_dimension=0, tiled=True
        ).astype(jnp.float32),
        lax.psum_scatter(
            output_grad.astype(jnp.bfloat16), ("dp", "seq"), scatter_dimension=1, tiled=True
        ).astype(jnp.float32),
        lax.psum_scatter(
            gate_grad.astype(jnp.bfloat16), ("dp", "seq"), scatter_dimension=0, tiled=True
        ).astype(jnp.float32),
        lax.psum_scatter(
            up_grad.astype(jnp.bfloat16), ("dp", "seq"), scatter_dimension=0, tiled=True
        ).astype(jnp.float32),
        lax.psum_scatter(
            down_grad.astype(jnp.bfloat16), ("dp", "seq"), scatter_dimension=1, tiled=True
        ).astype(jnp.float32),
    )
    return (
        block_out,
        residual_grad,
        attn_gain_grad,
        weight_sums[0],
        query_bias_grad,
        weight_sums[1],
        key_bias_grad,
        weight_sums[2],
        value_bias_grad,
        weight_sums[3],
        ffn_gain_grad,
        weight_sums[4],
        weight_sums[5],
        weight_sums[6],
    )


def solution(mesh):
    in_specs = (
        P("dp", ("seq", "heads"), None),
        P("dp", "seq", None),
        P("dp"),
        P(),
        P(None, "heads"),
        P("heads"),
        P(),
        P(),
        P(),
        P(),
        P("heads", None),
        P(),
        P(("dp", "seq"), "heads"),
        P(("dp", "seq"), "heads"),
        P("heads", ("dp", "seq")),
    )
    out_specs = (
        P("dp", ("seq", "heads"), None),
        P("dp", ("seq", "heads"), None),
        P(("dp", "seq", "heads")),
        P(("dp", "seq"), "heads"),
        P("heads"),
        P(("dp", "seq"), "heads"),
        P("heads"),
        P(("dp", "seq"), "heads"),
        P("heads"),
        P("heads", ("dp", "seq")),
        P(("dp", "seq", "heads")),
        P(("dp", "seq"), "heads"),
        P(("dp", "seq"), "heads"),
        P("heads", ("dp", "seq")),
    )
    return jax.shard_map(local, mesh=mesh, in_specs=in_specs, out_specs=out_specs, check_vma=False)
```

profile of v0, /device:TPU:9, one launch (start us, length us, event | category | flops | bytes accessed | tf_op | source)
XLA Modules:
  0.0 1418.2 jit_solution(17231077435271165050)
XLA Ops:
  13.4 65.8 %all-gather.7.cloned.1.call-done = bf16[3,384,1536]{2,1,0:T(8,128)(2,1)} async-done(((bf16[3,96,1536]{2,1,0:T(8,128)(2,1)}), bf16[3,384,1536]{2,1,0:T(8,128)(2,1)}) %all-gather.7.cloned.1.call-update) | async-done | bytes 3538960 | tf_op jit(solution)/shard_map/all_gather | solution.py:81
  108.7 9.2 all-gather.9.cloned.1.call-done
  118.0 7.3 fusion.93
  125.3 7.3 copy-done.2
  137.2 10.9 all-gather.11.cloned.1.call-done
  148.2 9.3 fusion.49
  166.3 244.1 %all-reduce.4.cloned.1.call-done = f32[1152,1536]{1,0:T(8,128)} async-done(((f32[1152,1536]{1,0:T(8,128)}), f32[1152,1536]{1,0:T(8,128)}) %all-reduce.4.cloned.1.call-update) | async-done | bytes 7077904 | tf_op jit(solution)/shard_map/psum | solution.py:144
  420.8 14.9 %fusion.94 = f32[1152,2240]{0,1:T(8,128)} fusion(bf16[1152,1536]{1,0:T(8,128)(2,1)} %multiply_convert_fusion.4, bf16[1536,2240]{1,0:T(8,128)(2,1)} %all-gather.13.cloned.1.call-done), kind=kOutput, calls=%fused_computation.147 | convolution fusion | flops 7927234560 | bytes 20742144 | tf_op jit(solution)/shard_map/dot_general | solution.py:153
  435.7 15.0 %fusion.95 = f32[1152,2240]{0,1:T(8,128)} fusion(bf16[1152,1536]{1,0:T(8,128)(2,1)} %multiply_convert_fusion.4, bf16[1536,2240]{1,0:T(8,128)(2,1)} %all-gather.15.cloned.1.call-done), kind=kOutput, calls=%fused_computation.148 | convolution fusion | flops 7927234560 | bytes 20742144 | tf_op jit(solution)/shard_map/dot_general | solution.py:154
  450.7 24.5 %multiply_convert_fusion.1 = (bf16[1152,2240]{0,1:T(8,128)(2,1)}, bf16[1152,2240]{0,1:T(8,128)(2,1)}, bf16[1152,2240]{0,1:T(8,128)(2,1)}) fusion(f32[1152,2240]{0,1:T(8,128)} %fusion.94, f32[1152,2240]{0,1:T(8,128)} %fusion.95, bf16[1152,1536]{1,0:T(8,128)(2,1)} %bitcast.134, bf16[2240,1536]{0,1:T(8,128)(2,1)} %all-gather.17.cloned.1.call-done), kind=kOutput, calls=%fused_computation.22 | convolution fusion | flops 7965941760 | bytes 46546944 | tf_op jit(solution)/shard_map/td,fd->tf/dot_general | solution.py:169
  475.1 14.3 %fusion.96 = f32[1152,1536]{1,0:T(8,128)} fusion(bf16[1152,2240]{0,1:T(8,128)(2,1)} %get-tuple-element.30, bf16[1536,2240]{1,0:T(8,128)(2,1)} %all-gather.13.cloned.1.call-done), kind=kOutput, calls=%fused_computation.149 | convolution fusion | flops 7927234560 | bytes 19120128 | tf_op jit(solution)/shard_map/tf,df->td/dot_general | solution.py:177
  489.5 19.9 %multiply_reduce_fusion.1 = (f32[1536]{0:T(1024)}, f32[1152]{0:T(1024)S(1)}, f32[1152,1536]{1,0:T(8,128)}) fusion(f32[1152,1536]{1,0:T(8,128)} %copy-done.3, f32[1152]{0:T(1024)S(1)} %add_rsqrt_fusion, f32[1536]{0:T(1024)S(1)} %convert_element_type.172, f32[1152,1536]{1,0:T(8,128)} %fusion.96, bf16[1152,2240]{0,1:T(8,128)(2,1)} %get-tuple-element.29, ...), kind=kOutput, calls=%fused_computation.48 | convolution fusion | flops 7939618304 | bytes 33297408 | tf_op jit(solution)/shard_map/tf,df->td/dot_general | solution.py:179
  515.1 247.3 %all-reduce.6.cloned.1.call-done = f32[1152,1536]{1,0:T(8,128)} async-done(((f32[1152,1536]{1,0:T(8,128)}), f32[1152,1536]{1,0:T(8,128)}) %all-reduce.6.cloned.1.call-update) | async-done | bytes 7077904 | tf_op jit(solution)/shard_map/psum | solution.py:182
  773.1 8.8 fusion.52
  781.9 31.1 %fusion.39 = f32[3,1536,128]{2,1,0:T(8,128)} fusion(bf16[3,384,3,128]{1,3,2,0:T(8,128)(2,1)S(1)} %copy-done.10, f32[3,384,3,1536]{3,1,2,0:T(8,128)} %fusion.52, f32[3,384,3,1536]{3,1,2,0:T(8,128)} %copy-done.2, f32[3,384,3]{1,2,0:T(4,128)S(1)} %log_add_fusion), kind=kOutput, calls=%fused_computation.57 | convolution fusion | flops 1396118400 | bytes 45725184 | tf_op jit(solution)/shard_map/lnya,lnyz->laz/dot_general | solution.py:203
  813.1 11.1 fusion.36
  824.3 14.1 convolution_convert_fusion.3
  849.6 36.0 %fusion.10 = f32[3,384,3,128]{1,3,2,0:T(8,128)S(1)} fusion(f32[3,384,3,1536]{3,1,2,0:T(8,128)} %fusion.52, f32[3,384,3,1536]{3,1,2,0:T(8,128)} %copy-done.2, f32[3,384,3]{1,2,0:T(4,128)S(1)} %log_add_fusion, bf16[3,1536,128]{2,1,0:T(8,128)(2,1)} %all-gather.9.cloned.1.call-done), kind=kOutput, calls=%fused_computation.11 | convolution fusion | flops 1396118400 | bytes 45430272 | tf_op jit(solution)/shard_map/iaeg,ign->iaen/dot_general | solution.py:200
  894.7 14.3 %convolution_convert_fusion.2 = bf16[1536,2240]{1,0:T(8,128)(2,1)} fusion(bf16[1152,1536]{1,0:T(8,128)(2,1)} %multiply_convert_fusion.4, bf16[1152,2240]{0,1:T(8,128)(2,1)} %get-tuple-element.30), kind=kOutput, calls=%fused_computation.14 | convolution fusion | flops 7930675200 | bytes 15581184 | tf_op jit(solution)/shard_map/td,tf->df/dot_general | solution.py:175
  909.3 14.4 %convolution_convert_fusion.1 = bf16[1536,2240]{1,0:T(8,128)(2,1)} fusion(bf16[1152,1536]{1,0:T(8,128)(2,1)} %multiply_convert_fusion.4, bf16[1152,2240]{0,1:T(8,128)(2,1)} %get-tuple-element.29), kind=kOutput, calls=%fused_computation.13 | convolution fusion | flops 7930675200 | bytes 15581184 | tf_op jit(solution)/shard_map/td,tf->df/dot_general | solution.py:176
  923.8 14.4 %convolution_convert_fusion = bf16[2240,1536]{0,1:T(8,128)(2,1)} fusion(bf16[1152,2240]{0,1:T(8,128)(2,1)} %get-tuple-element.31, bf16[1152,1536]{1,0:T(8,128)(2,1)} %bitcast.135), kind=kOutput, calls=%fused_computation.12 | convolution fusion | flops 7930675200 | bytes 15581184 | tf_op jit(solution)/shard_map/tf,td->fd/dot_general | solution.py:174
  949.0 34.9 %collective-permute-done = f32[2,3,384,128]{3,2,1,0:T(8,128)} collective-permute-done((f32[2,3,384,128]{3,2,1,0:T(8,128)}, f32[2,3,384,128]{3,2,1,0:T(8,128)}, u32[]{:S(2)}, u32[]{:S(2)}) %collective-permute-start) | collective-permute-done | bytes 1179680 | tf_op jit(solution)/shard_map/ppermute | solution.py:19
  988.5 7.3 convolution_add_fusion.1
  995.8 7.3 fusion.32
  1005.0 7.5 fusion.31
  1017.4 39.2 %reduce-scatter.24.cloned.1.call-done = bf16[192,384]{1,0:T(8,128)(2,1)} async-done(((bf16[1536,384]{1,0:T(8,128)(2,1)}), bf16[192,384]{1,0:T(8,128)(2,1)}) %reduce-scatter.24.cloned.1.call-update) | async-done | bytes 147472 | tf_op jit(solution)/shard_map/reduce_scatter | solution.py:299
  1058.2 67.5 %reduce-scatter.28.cloned.1.call-done = bf16[192,2240]{1,0:T(8,128)(2,1)} async-done(((bf16[1536,2240]{1,0:T(8,128)(2,1)}), bf16[192,2240]{1,0:T(8,128)(2,1)}) %reduce-scatter.28.cloned.1.call-update) | async-done | bytes 860176 | tf_op jit(solution)/shard_map/reduce_scatter | solution.py:311
  1128.2 66.8 %reduce-scatter.30.cloned.1.call-done = bf16[192,2240]{1,0:T(8,128)(2,1)} async-done(((bf16[1536,2240]{1,0:T(8,128)(2,1)}), bf16[192,2240]{1,0:T(8,128)(2,1)}) %reduce-scatter.30.cloned.1.call-update) | async-done | bytes 860176 | tf_op jit(solution)/shard_map/reduce_scatter | solution.py:314
  1197.6 66.5 %reduce-scatter.32.cloned.1.call-done = bf16[2240,192]{0,1:T(8,128)(2,1)} async-done(((bf16[2240,1536]{0,1:T(8,128)(2,1)}), bf16[2240,192]{0,1:T(8,128)(2,1)}) %reduce-scatter.32.cloned.1.call-update) | async-done | bytes 860176 | tf_op jit(solution)/shard_map/reduce_scatter | solution.py:317
  1267.3 38.9 %all-reduce = (f32[1536]{0:T(1024)S(1)}, f32[1536]{0:T(1024)S(1)}, f32[256]{0:T(256)S(1)}, f32[256]{0:T(256)S(1)}, f32[1536]{0:T(1024)S(1)}) all-reduce(f32[1536]{0:T(1024)S(1)} %get-tuple-element.16, f32[1536]{0:T(1024)S(1)} %bitcast_dynamic-update-slice_fusion, ...), channel_id=1, replica_groups=mesh['dp'=2,'seq'=4,'heads'=4] {'dp','seq','heads'}, use_global_device_ids=true, to_apply=%region_14.15 | all-reduce | flops 5120 | bytes 40960 | tf_op jit(solution)/shard_map/psum | solution.py:283
  1310.7 27.6 %reduce-scatter.36.cloned.1.call-done = bf16[192,64]{1,0:T(8,128)(2,1)} async-done(((bf16[1536,64]{1,0:T(8,128)(2,1)}), bf16[192,64]{1,0:T(8,128)(2,1)}) %reduce-scatter.36.cloned.1.call-update) | async-done | bytes 24592
  1339.8 67.5 %reduce-scatter.22.cloned.1.call-done = bf16[3,96,1536]{2,1,0:T(8,128)(2,1)} async-done(((bf16[3,384,1536]{2,1,0:T(8,128)(2,1)}), bf16[3,96,1536]{2,1,0:T(8,128)(2,1)}) %reduce-scatter.22.cloned.1.call-update) | async-done | bytes 884752 | tf_op jit(solution)/shard_map/reduce_scatter | solution.py:260
  (203 shorter events, 136.3 us)
Async XLA Ops:
  8.0 151.2 %copy-start = (bf16[384,1536]{1,0:T(8,128)(2,1)S(1)}, bf16[384,1536]{1,0:T(8,128)(2,1)}, u32[]{:S(2)}) copy-start(bf16[384,1536]{1,0:T(8,128)(2,1)} %param.25) | copy-start | bytes 3538948
  8.0 78.6 %copy-start.23 = (bf16[1536,256]{1,0:T(8,128)(2,1)S(1)}, bf16[1536,256]{1,0:T(8,128)(2,1)}, u32[]{:S(2)}) copy-start(bf16[1536,256]{1,0:T(8,128)(2,1)} %param.21) | copy-start | bytes 2359300
  8.0 71.1 %all-gather.7.cloned.1.call-start = ((), (), s32[]{:S(2)}) async-start(), calls=%async_computation.11 | async-start | bytes 4423680 | tf_op jit(solution)/shard_map/all_gather | solution.py:81
  8.8 109.2 %all-gather.9.cloned.1.call-start = ((), (), s32[]{:S(2)}) async-start(), calls=%async_computation.12 | async-start | bytes 1474560 | tf_op jit(solution)/shard_map/all_gather | solution.py:111
  9.5 78.2 %copy-start.25 = (f32[1536]{0:T(1024)}, f32[1536]{0:T(1024)S(1)}, u32[]{:S(2)}) copy-start(f32[1536]{0:T(1024)S(1)} %convert_element_type.161) | copy-start | bytes 18436
  11.1 76.9 %copy-start.11 = (f32[384,128]{1,0:T(8,128)}, f32[384,128]{1,0:T(8,128)S(1)}, u32[]{:S(2)}) copy-start(f32[384,128]{1,0:T(8,128)S(1)} %get-tuple-element.43) | copy-start | bytes 589828
  11.2 76.9 %copy-start.13 = (f32[384,128]{1,0:T(8,128)}, f32[384,128]{1,0:T(8,128)S(1)}, u32[]{:S(2)}) copy-start(f32[384,128]{1,0:T(8,128)S(1)} %get-tuple-element.42) | copy-start | bytes 589828
  11.3 94.8 %copy-start.17 = (f32[384,128]{0,1:T(8,128)}, f32[384,128]{0,1:T(8,128)S(1)}, u32[]{:S(2)}) copy-start(f32[384,128]{0,1:T(8,128)S(1)} %copy.55) | copy-start | bytes 589828
  11.4 94.7 %copy-start.19 = (f32[384,128]{0,1:T(8,128)}, f32[384,128]{0,1:T(8,128)S(1)}, u32[]{:S(2)}) copy-start(f32[384,128]{0,1:T(8,128)S(1)} %copy.59) | copy-start | bytes 589828
  89.0 59.2 %all-gather.11.cloned.1.call-start = ((), (), s32[]{:S(2)}) async-start(), calls=%async_computation.13 | async-start | bytes 1474560 | tf_op jit(solution)/shard_map/all_gather | solution.py:112
  105.8 304.6 %all-reduce.4.cloned.1.call-start = ((), (), s32[]{:S(2)}) async-start(), calls=%async_computation.14 | async-start | bytes 14155776 | tf_op jit(solution)/shard_map/psum | solution.py:144
  164.1 256.7 %all-gather.13.cloned.1.call-start = ((), (), s32[]{:S(2)}) async-start(), calls=%async_computation.15 | async-start | bytes 7962624 | tf_op jit(solution)/shard_map/all_gather | solution.py:149
  164.7 271.0 %all-gather.15.cloned.1.call-start = ((), (), s32[]{:S(2)}) async-start(), calls=%async_computation.16 | async-start | bytes 7962624 | tf_op jit(solution)/shard_map/all_gather | solution.py:150
  165.3 285.4 %all-gather.17.cloned.1.call-start = ((), (), s32[]{:S(2)}) async-start(), calls=%async_computation.17 | async-start | bytes 7962624 | tf_op jit(solution)/shard_map/all_gather | solution.py:151
  165.9 596.6 %all-reduce.6.cloned.1.call-start = ((), (), s32[]{:S(2)}) async-start(), calls=%async_computation.19 | async-start | bytes 14155776 | tf_op jit(solution)/shard_map/psum | solution.py:182
  515.1 423.5 %reduce-scatter.18.cloned.1.call-start = ((), (), s32[]{:S(2)}) async-start(), calls=%async_computation.20 | async-start | bytes 2949120 | tf_op jit(solution)/shard_map/reduce_scatter | solution.py:218
  813.0 125.5 %reduce-scatter.20.cloned.1.call-start = ((), (), s32[]{:S(2)}) async-start(), calls=%async_computation.21 | async-start | bytes 2949120 | tf_op jit(solution)/shard_map/reduce_scatter | solution.py:219
  824.2 188.4 %reduce-scatter.16.cloned.1.call-start = ((), (), s32[]{:S(2)}) async-start(), calls=%async_computation.18 | async-start | bytes 4423680 | tf_op jit(solution)/shard_map/reduce_scatter | solution.py:161
  838.4 177.3 %reduce-scatter.26.cloned.1.call-start = ((), (), s32[]{:S(2)}) async-start(), calls=%async_computation.24 | async-start | bytes 1327104 | tf_op jit(solution)/shard_map/reduce_scatter | solution.py:308
  844.7 211.9 %reduce-scatter.24.cloned.1.call-start = ((), (), s32[]{:S(2)}) async-start(), calls=%async_computation.23 | async-start | bytes 1327104 | tf_op jit(solution)/shard_map/reduce_scatter | solution.py:299
  894.7 231.1 %reduce-scatter.28.cloned.1.call-start = ((), (), s32[]{:S(2)}) async-start(), calls=%async_computation.25 | async-start | bytes 7962624 | tf_op jit(solution)/shard_map/reduce_scatter | solution.py:311
  909.1 286.0 %reduce-scatter.30.cloned.1.call-start = ((), (), s32[]{:S(2)}) async-start(), calls=%async_computation.26 | async-start | bytes 7962624 | tf_op jit(solution)/shard_map/reduce_scatter | solution.py:314
  923.7 340.4 %reduce-scatter.32.cloned.1.call-start = ((), (), s32[]{:S(2)}) async-start(), calls=%async_computation.27 | async-start | bytes 7962624 | tf_op jit(solution)/shard_map/reduce_scatter | solution.py:317
  938.2 371.0 %reduce-scatter.34.cloned.1.call-start = ((), (), s32[]{:S(2)}) async-start(), calls=%async_computation.28 | async-start | bytes 442368
  938.6 45.4 %copy-start.15 = (f32[3,384,128]{2,1,0:T(8,128)S(1)}, f32[3,384,128]{2,1,0:T(8,128)}, u32[]{:S(2)}) copy-start(f32[3,384,128]{2,1,0:T(8,128)} %reduce-scatter.18.cloned.1.call-done) | copy-start | bytes 1769476
  938.6 45.4 %copy-start.16 = (f32[3,384,128]{2,1,0:T(8,128)S(1)}, f32[3,384,128]{2,1,0:T(8,128)}, u32[]{:S(2)}) copy-start(f32[3,384,128]{2,1,0:T(8,128)} %reduce-scatter.20.cloned.1.call-done) | copy-start | bytes 1769476
  941.0 43.0 %collective-permute-start = (f32[2,3,384,128]{3,2,1,0:T(8,128)}, f32[2,3,384,128]{3,2,1,0:T(8,128)}, u32[]{:S(2)}, u32[]{:S(2)}) collective-permute-start(f32[2,3,384,128]{3,2,1,0:T(8,128)} %pad_maximum_fusion), channel_id=1, source_target_pairs={{0,1},{1,0},{2,3},{3,2},{4,5},{5,4},{6,7},{7,6},{8,9},{9,8},{10,11... | collective-permute-start | bytes 3538952 | tf_op jit(solution)/shard_map/ppermute | solution.py:19
  949.0 37.7 %copy-start.5 = (bf16[1152,1536]{1,0:T(8,128)(2,1)S(1)}, bf16[1152,1536]{1,0:T(8,128)(2,1)}, u32[]{:S(2)}) copy-start(bf16[1152,1536]{1,0:T(8,128)(2,1)} %copy-done.4) | copy-start | bytes 10616836
  995.7 342.5 %reduce-scatter.36.cloned.1.call-start = ((), (), s32[]{:S(2)}) async-start(), calls=%async_computation.29 | async-start | bytes 442368
  1005.0 402.3 %reduce-scatter.22.cloned.1.call-start = ((), (), s32[]{:S(2)}) async-start(), calls=%async_computation.22 | async-start | bytes 4423680 | tf_op jit(solution)/shard_map/reduce_scatter | solution.py:260
  1012.5 254.7 %copy-start.32 = (f32[1536]{0:T(1024)S(1)}, f32[1536]{0:T(1024)}, u32[]{:S(2)}) copy-start(f32[1536]{0:T(1024)} %get-tuple-element.14) | copy-start | bytes 18436
  1012.7 397.7 %copy-start.1 = (bf16[384,1536]{1,0:T(8,128)(2,1)S(1)}, bf16[384,1536]{1,0:T(8,128)(2,1)}, u32[]{:S(2)}) copy-start(bf16[384,1536]{1,0:T(8,128)(2,1)} %param.25) | copy-start | bytes 3538948
  (25 other events, 307.3 us)
Sparse Core Ops, SparseCore 0:
  10.4 68.6 all-gather.6
  89.1 28.8 all-gather.8
  120.4 27.7 all-gather.10
  164.2 246.1 all-reduce.3
  515.2 247.2 all-reduce.5
  813.1 38.4 reduce-scatter.17
  854.7 37.4 reduce-scatter.19
  894.5 73.5 reduce-scatter.15
  971.9 43.8 reduce-scatter.25
  1019.8 36.7 reduce-scatter.23
  1060.1 65.5 reduce-scatter.27
  1129.5 65.5 reduce-scatter.29
  1198.6 65.4 reduce-scatter.31
  1267.9 33.2 reduce-scatter.33
  1304.4 33.7 reduce-scatter.35
  1340.5 66.6 reduce-scatter.21
Sparse Core Ops, SparseCore 1:
  166.5 49.1 all-gather.12
  217.4 48.6 all-gather.14
  267.8 48.6 all-gather.16
where the time goes:
time: 1430 us; the launch traced here: 1420 us
  waiting for transfers between devices  950 us (66%)
  matrix products  298 us (21%)
  other arithmetic  76.5 us (5%)
  blocking collectives  38.9 us (3%)
  local copies, waits for them, and re-layouts  32.7 us (2%)
  between operations  16.8 us (1%)
    psum x1, waiting for transfers between devices, local(): lax.psum(second_spread, 'heads')  247 us
    psum x1, waiting for transfers between devices, local(): second_stream = stream + lax.psum(attn_part, 'heads')  244 us
    reduce_scatter x1, waiting for transfers between devices, local(): lax.psum_scatter(gate_grad.astype(jnp.bfloat16), ('dp', 'seq'), scatter_d...  67.5 us
    reduce_scatter x1, waiting for transfers between devices, local(): lax.psum_scatter(first_spread.astype(jnp.bfloat16), 'heads', scatter_dime...  67.5 us
    reduce_scatter x1, waiting for transfers between devices, local(): lax.psum_scatter(up_grad.astype(jnp.bfloat16), ('dp', 'seq'), scatter_dim...  66.8 us
    reduce_scatter x1, waiting for transfers between devices, local(): lax.psum_scatter(down_grad.astype(jnp.bfloat16), ('dp', 'seq'), scatter_d...  66.5 us
    all_gather x1, waiting for transfers between devices, local(): gathered = lax.all_gather(residual, 'heads', axis=1, tiled=True)  65.8 us
    reduce_scatter x1, waiting for transfers between devices, local(): lax.psum_scatter(query_grad.astype(jnp.bfloat16), ('dp', 'seq'), scatter_...  39.2 us
  transfers between devices with their start and end apart: 20, of which 13 were waited for; matrix products, arithmetic and copies ran while one was open for 18% of the time, Pallas kernels for 0%

commit v1 on v0

v1 whole, which is shorter than its diff:
```python
import jax
import jax.numpy as jnp
from jax import lax
from jax.experimental import pallas as pl
from jax.experimental.pallas import tpu as pltpu
from jax.sharding import PartitionSpec as P

H = 12
KVH = 2
HD = 128

epsilon = 1e-06
rope_base = 1000000.0
hidden_logit = -1e30
log2_e = 1.4426950408889634

bf16 = jnp.bfloat16
f32 = jnp.float32
vmem_bytes = 48 * 2**20


def swap(value, axis, mask):
    pairs = [(source, source ^ mask) for source in range(lax.axis_size(axis))]
    return lax.ppermute(value, axis, pairs)


def rotate_down(value, axis):
    size = lax.axis_size(axis)
    pairs = [(source, (source - 1) % size) for source in range(size)]
    return lax.ppermute(value, axis, pairs)


def add_low(first, second):
    return (first.astype(f32) + second.astype(f32)).astype(bf16)


def join(parts, dim):
    return parts[0] if len(parts) == 1 else jnp.concatenate(parts, axis=dim)


def split(value, count, dim):
    return [value] if count == 1 else jnp.split(value, count, axis=dim)


def seq_masks():
    bits = lax.axis_size("seq").bit_length() - 1
    ahead = [1 << bit for bit in range(bits)]
    return ahead, ahead[bits // 2 :] + ahead[: bits // 2]


def gather_seq(block, masks, dim):
    held = {0: block}
    for mask in masks:
        keys = list(held)
        came = split(swap(join([held[k] for k in keys], dim), "seq", mask), len(keys), dim)
        held.update({k ^ mask: piece for k, piece in zip(keys, came)})
    return [held[r] for r in range(len(held))]


def scatter_seq(blocks, masks, dim):
    held = dict(enumerate(blocks))
    for mask in masks:
        away = [k for k in held if k & mask]
        came = split(swap(join([held[k] for k in away], dim), "seq", mask), len(away), dim)
        for k, piece in zip(away, came):
            held[k ^ mask] = add_low(held[k ^ mask], piece)
            del held[k]
    return held[0]


def gather_ring(block, axis):
    held = [block]
    for _ in range(lax.axis_size(axis) - 1):
        held.append(rotate_down(held[-1], axis))
    return held


def scatter_ring(blocks, axis):
    total = blocks[1]
    for block in blocks[2:] + blocks[:1]:
        total = add_low(rotate_down(total, axis), block)
    return total


def take(value, index, size, dim):
    return lax.dynamic_slice_in_dim(value, index * size, size, dim)


def turn(values, cosine, sine):
    return values * cosine + pltpu.roll(values, HD // 2, 1) * sine


def turn_back(values, cosine, sine):
    return values * cosine - pltpu.roll(values, HD // 2, 1) * sine


def first_kernel(x_ref, gain_ref, kw_ref, vw_ref, kb_ref, vb_ref, cos_ref, sin_ref, in_ref, kv_ref):
    x = x_ref[0].astype(f32)
    scale = lax.rsqrt(jnp.mean(x * x, axis=-1, keepdims=True) + epsilon)
    low = (x * scale * gain_ref[...].astype(f32)).astype(bf16)
    in_ref[0] = low
    width = kw_ref.shape[1]
    keys = jnp.dot(low, kw_ref[...], preferred_element_type=f32) + kb_ref[...].astype(f32)
    for at in range(0, width, HD):
        kv_ref[0, :, at : at + HD] = turn(
            keys[:, at : at + HD], cos_ref[...], sin_ref[...]
        ).astype(bf16)
    values = jnp.dot(low, vw_ref[...], preferred_element_type=f32) + vb_ref[...].astype(f32)
    kv_ref[0, :, width:] = values.astype(bf16)


def first_call(residual, gain, kw, vw, kb, vb, cosine, sine):
    rows, count, width = residual.shape
    kv = kw.shape[1]
    fixed = lambda shape: pl.BlockSpec(shape, lambda r: (0, 0))
    row = lambda size: pl.BlockSpec((1, count, size), lambda r: (r, 0, 0))
    return pl.pallas_call(
        first_kernel,
        grid=(rows,),
        in_specs=[
            row(width),
            fixed((1, width)),
            fixed((width, kv)),
            fixed((width, kv)),
            fixed((1, kv)),
            fixed((1, kv)),
            fixed((count, HD)),
            fixed((count, HD)),
        ],
        out_specs=[row(width), row(2 * kv)],
        out_shape=[
            jax.ShapeDtypeStruct((rows, count, width), bf16),
            jax.ShapeDtypeStruct((rows, count, 2 * kv), bf16),
        ],
        cost_estimate=pl.CostEstimate(
            flops=4 * rows * count * width * kv,
            bytes_accessed=2 * (2 * rows * count * width + 2 * width * kv),
            transcendentals=0,
        ),
        compiler_params=pltpu.CompilerParams(vmem_limit_bytes=vmem_bytes),
        name="first_norm",
    )(residual, gain[None], kw, vw, kb[None], vb[None], cosine, sine)


def attend_kernel(
    q_ref, cos_ref, sin_ref, k_ref, v_ref, kpos_ref, limit_ref, out_ref, turned_ref, log_ref
):
    count = q_ref.shape[1]
    heads = q_ref.shape[2] // HD
    turned = []
    for h in range(heads):
        u = turn(q_ref[0, :, h * HD : (h + 1) * HD], cos_ref[...], sin_ref[...])
        turned_ref[0, :, h * HD : (h + 1) * HD] = u.astype(bf16)
        turned.append(u)
    query = jnp.concatenate(turned, axis=0).astype(bf16)
    scores = lax.dot_general(
        k_ref[0], query, (((1,), (1,)), ((), ())), preferred_element_type=f32
    )
    seen = kpos_ref[...] <= limit_ref[0]
    scores = jnp.where(seen, scores * (HD**-0.5 * log2_e), hidden_logit)
    peak = jnp.max(scores, axis=0, keepdims=True)
    weight = jnp.exp2(scores - peak)
    total = jnp.sum(weight, axis=0, keepdims=True)
    log_ref[0, 0] = peak + jnp.log2(total)
    out = lax.dot_general(
        v_ref[0], weight.astype(bf16), (((0,), (0,)), ((), ())), preferred_element_type=f32
    )
    out = (out * (1.0 / total)).T
    for h in range(heads):
        out_ref[0, :, h * HD : (h + 1) * HD] = out[h * count : (h + 1) * count].astype(bf16)


def attend_call(query, cosine, sine, keys, values, kpos, limit):
    rows, count, width = query.shape
    length = keys.shape[1]
    groups = KVH
    wide = width // groups
    many = limit.shape[2]
    part = pl.BlockSpec((1, count, wide), lambda r, g: (r, 0, g))
    fixed = lambda shape: pl.BlockSpec(shape, lambda r, g: (0, 0))
    whole = pl.BlockSpec((1, length, HD), lambda r, g: (r, 0, g))
    work = rows * groups * length * many
    return pl.pallas_call(
        attend_kernel,
        grid=(rows, groups),
        in_specs=[
            part,
            fixed((count, HD)),
            fixed((count, HD)),
            whole,
            whole,
            fixed((length, 1)),
            pl.BlockSpec((1, 1, many), lambda r, g: (r, 0, 0)),
        ],
        out_specs=[part, part, pl.BlockSpec((1, 1, 1, many), lambda r, g: (r, g, 0, 0))],
        out_shape=[
            jax.ShapeDtypeStruct((rows, count, width), bf16),
            jax.ShapeDtypeStruct((rows, count, width), bf16),
            jax.ShapeDtypeStruct((rows, groups, 1, many), f32),
        ],
        cost_estimate=pl.CostEstimate(
            flops=4 * work * HD, bytes_accessed=4 * keys.size, transcendentals=work
        ),
        compiler_params=pltpu.CompilerParams(vmem_limit_bytes=vmem_bytes),
        name="attend",
    )(query, cosine, sine, keys, values, kpos, limit)


def attend_back_kernel(
    q_ref,
    og_ref,
    cos_ref,
    sin_ref,
    k_ref,
    v_ref,
    kpos_ref,
    limit_ref,
    log_ref,
    gq_ref,
    gk_ref,
    gv_ref,
):
    count = q_ref.shape[1]
    heads = q_ref.shape[2] // HD

    def rows_of(ref):
        parts = [ref[0, :, h * HD : (h + 1) * HD].astype(f32) for h in range(heads)]
        return jnp.concatenate(parts, axis=0).astype(bf16)

    query, upstream = rows_of(q_ref), rows_of(og_ref)
    last = (((1,), (1,)), ((), ()))
    scores = lax.dot_general(k_ref[0], query, last, preferred_element_type=f32)
    seen = kpos_ref[...] <= limit_ref[0]
    scale = HD**-0.5
    probs = jnp.exp2(jnp.where(seen, scores * (scale * log2_e) - log_ref[0, 0], hidden_logit))
    gv_ref[0] = jnp.dot(probs.astype(bf16), upstream, preferred_element_type=f32).astype(bf16)
    grad_probs = lax.dot_general(v_ref[0], upstream, last, preferred_element_type=f32)
    mixed = probs * grad_probs
    total = jnp.sum(mixed, axis=0, keepdims=True)
    grad_scores = ((mixed - probs * total) * scale).astype(bf16)
    gk_ref[0] = jnp.dot(grad_scores, query, preferred_element_type=f32).astype(bf16)
    grad_query = lax.dot_general(
        k_ref[0], grad_scores, (((0,), (0,)), ((), ())), preferred_element_type=f32
    ).T
    for h in range(heads):
        gq_ref[0, :, h * HD : (h + 1) * HD] = turn_back(
            grad_query[h * count : (h + 1) * count], cos_ref[...], sin_ref[...]
        ).astype(bf16)


def attend_back_call(query, upstream, cosine, sine, keys, values, kpos, limit, logs):
    rows, count, width = query.shape
    length = keys.shape[1]
    groups = KVH
    wide = width // groups
    many = limit.shape[2]
    part = pl.BlockSpec((1, count, wide), lambda r, g: (r, 0, g))
    fixed = lambda shape: pl.BlockSpec(shape, lambda r, g: (0, 0))
    whole = pl.BlockSpec((1, length, HD), lambda r, g: (r, 0, g))
    work = rows * groups * length * many
    return pl.pallas_call(
        attend_back_kernel,
        grid=(rows, groups),
        in_specs=[
            part,
            part,
            fixed((count, HD)),
            fixed((count, HD)),
            whole,
            whole,
            fixed((length, 1)),
            pl.BlockSpec((1, 1, many), lambda r, g: (r, 0, 0)),
            pl.BlockSpec((1, 1, 1, many), lambda r, g: (r, g, 0, 0)),
        ],
        out_specs=[part, whole, whole],
        out_shape=[
            jax.ShapeDtypeStruct((rows, count, width), bf16),
            jax.ShapeDtypeStruct((rows, length, groups * HD), bf16),
            jax.ShapeDtypeStruct((rows, length, groups * HD), bf16),
        ],
        cost_estimate=pl.CostEstimate(
            flops=10 * work * HD, bytes_accessed=8 * keys.size, transcendentals=work
        ),
        compiler_params=pltpu.CompilerParams(vmem_limit_bytes=vmem_bytes),
        name="attend_back",
    )(query, upstream, cosine, sine, keys, values, kpos, limit, logs)


def turn_back_kernel(kv_ref, cos_ref, sin_ref, out_ref):
    half = kv_ref.shape[2] // 2
    for at in range(0, half, HD):
        out_ref[0, :, at : at + HD] = turn_back(
            kv_ref[0, :, at : at + HD].astype(f32), cos_ref[...], sin_ref[...]
        ).astype(bf16)
    out_ref[0, :, half:] = kv_ref[0, :, half:]


def turn_back_call(kv, cosine, sine):
    rows, count, width = kv.shape
    row = pl.BlockSpec((1, count, width), lambda r: (r, 0, 0))
    table = pl.BlockSpec((count, HD), lambda r: (0, 0))
    return pl.pallas_call(
        turn_back_kernel,
        grid=(rows,),
        in_specs=[row, table, table],
        out_specs=row,
        out_shape=jax.ShapeDtypeStruct(kv.shape, bf16),
        cost_estimate=pl.CostEstimate(
            flops=4 * kv.size, bytes_accessed=4 * kv.size, transcendentals=0
        ),
        compiler_params=pltpu.CompilerParams(vmem_limit_bytes=vmem_bytes),
        name="turn_back",
    )(kv, cosine, sine)


def matmul(left, right):
    return jnp.dot(left, right, preferred_element_type=f32)


def matmul_nt(left, right):
    return lax.dot_general(left, right, (((1,), (1,)), ((), ())), preferred_element_type=f32)


def matmul_tn(left, right):
    return lax.dot_general(left, right, (((0,), (0,)), ((), ())), preferred_element_type=f32)


def angles(positions):
    inverse_freq = rope_base ** (-jnp.arange(0, HD // 2, dtype=f32) * 2.0 / HD)
    phase = positions[:, None] * inverse_freq[None, :]
    cosine, sine = jnp.cos(phase), jnp.sin(phase)
    return jnp.concatenate([cosine, cosine], -1), jnp.concatenate([-sine, sine], -1)


def norm_back(upstream, normed, inv_rms, gain_row):
    scaled = upstream * gain_row
    return inv_rms * (scaled - normed * jnp.mean(scaled * normed, axis=-1, keepdims=True))


def rms_scale(values):
    return lax.rsqrt(jnp.mean(values * values, axis=-1, keepdims=True) + epsilon)


def local(
    residual,
    out_grad,
    lengths,
    attn_gain,
    query_weight,
    query_bias,
    key_weight,
    key_bias,
    value_weight,
    value_bias,
    output_weight,
    ffn_gain,
    gate_weight,
    up_weight,
    down_weight,
):
    rows, own, width = residual.shape
    tokens = rows * own
    shard = own * lax.axis_size("heads")
    n_heads = lax.axis_size("heads")
    n_seq = lax.axis_size("seq")
    z = lax.axis_index("heads")
    s = lax.axis_index("seq")
    c = lax.axis_index("dp")
    piece = c * n_seq + s
    order_a, order_b = seq_masks()
    both = ("dp", "seq")
    depth = gate_weight.shape[0]
    half = n_seq * depth
    q_own = query_weight.shape[1]
    q_all = q_own * n_heads
    kv_width = key_weight.shape[1]
    group_heads = H // KVH

    start = s * shard + z * own
    positions = start + jnp.arange(own, dtype=jnp.int32)
    cosine, sine = angles(positions.astype(f32))

    first_input, kv_own = first_call(
        residual, attn_gain, key_weight, value_weight, key_bias, value_bias, cosine, sine
    )
    kv_ring = gather_ring(kv_own, "heads")
    key_block = jnp.concatenate([part[..., :kv_width] for part in kv_ring], axis=1)
    value_block = jnp.concatenate([part[..., kv_width:] for part in kv_ring], axis=1)
    keys = jnp.concatenate(gather_seq(key_block, order_a, 1), axis=1)
    values = jnp.concatenate(gather_seq(value_block, order_b, 1), axis=1)
    seq_at = jnp.arange(n_seq, dtype=jnp.int32) ^ s
    ring_at = (jnp.arange(n_heads, dtype=jnp.int32) + z) % n_heads
    key_pos = (
        seq_at[:, None, None] * shard
        + ring_at[None, :, None] * own
        + jnp.arange(own, dtype=jnp.int32)[None, None, :]
    ).reshape(-1, 1)
    limit = jnp.minimum(positions[None, :], lengths[:, None] - 1)
    limit = jnp.tile(limit, (1, group_heads))[:, None, :]

    query_piece = take(query_weight, piece, depth, 0)
    output_piece = take(output_weight, piece, depth, 1).T
    extra = 16
    bias_rows = jnp.pad(query_bias[None], ((0, extra - 1), (0, q_own)))
    sent = jnp.concatenate(
        [jnp.concatenate([query_piece, output_piece], axis=1), bias_rows], axis=0
    )
    qo_ring = gather_ring(sent, "heads")
    back = (n_heads - z) % n_heads

    def in_order(pieces):
        return lax.dynamic_slice_in_dim(
            jnp.concatenate(pieces + pieces[:-1], axis=1), back * q_own, q_all, 1
        )

    query_rows = in_order([part[:depth, :q_own] for part in qo_ring])
    output_rows = in_order([part[:depth, q_own:] for part in qo_ring])
    bias_all = in_order([part[depth : depth + 1, :q_own] for part in qo_ring]).astype(f32)

    def gather_rows(block, masks):
        held = jnp.zeros((half, block.shape[1]), block.dtype)
        for r, part in enumerate(gather_seq(block, masks, 0)):
            held = lax.dynamic_update_slice_in_dim(held, part, (s ^ r) * depth, 0)
        other = swap(held, "dp", 1)
        full = jnp.zeros((2 * half, block.shape[1]), block.dtype)
        full = lax.dynamic_update_slice_in_dim(full, held, c * half, 0)
        return lax.dynamic_update_slice_in_dim(full, other, (1 - c) * half, 0)

    query_full = gather_rows(query_rows, order_a)
    output_full = gather_rows(output_rows, order_b)

    down_full = lax.all_gather(down_weight.T, both, axis=0, tiled=True)
    gate_full = lax.all_gather(gate_weight, both, axis=0, tiled=True)
    up_full = lax.all_gather(up_weight, both, axis=0, tiled=True)

    input_flat = first_input.reshape(tokens, width)
    query_lin = (matmul(input_flat, query_full) + bias_all).reshape(rows, own, q_all)
    attended, query_rot, logs = attend_call(
        query_lin, cosine, sine, keys, values, key_pos, limit
    )
    attended = attended.reshape(tokens, q_all)
    stream = residual.astype(f32).reshape(tokens, width)
    second_stream = stream + matmul_nt(attended, output_full)
    second_scale = rms_scale(second_stream)
    second_normed = second_stream * second_scale
    second_gain = ffn_gain.astype(f32)
    second_own = (second_normed * second_gain).astype(bf16).reshape(rows, own, width)

    count = rows * shard
    second_input = lax.all_gather(second_own, "heads", axis=1, tiled=True).reshape(count, width)
    grad_flat = out_grad.reshape(count, width)
    grad_hidden = matmul(grad_flat, down_full)
    gate_act = matmul(second_input, gate_full)
    up_act = matmul(second_input, up_full)
    sigmoid_gate = jax.nn.sigmoid(gate_act)
    silu_gate = gate_act * sigmoid_gate
    hidden = (silu_gate * up_act).astype(bf16)
    grad_gate = (
        grad_hidden * up_act * sigmoid_gate * (1.0 + gate_act * (1.0 - sigmoid_gate))
    ).astype(bf16)
    grad_up = (grad_hidden * silu_gate).astype(bf16)
    second_back = matmul_nt(grad_gate, gate_full) + matmul_nt(grad_up, up_full)
    second_back = lax.psum_scatter(
        second_back.astype(bf16).reshape(rows, shard, width),
        "heads",
        scatter_dimension=1,
        tiled=True,
    )
    ffn_part = matmul_nt(hidden, down_full).astype(bf16).reshape(rows, shard, width)
    ffn_own = lax.psum_scatter(ffn_part, "heads", scatter_dimension=1, tiled=True)
    block_out = second_stream.reshape(rows, own, width) + ffn_own.astype(f32)
    down_grad = matmul_tn(grad_flat, hidden).astype(bf16)
    gate_grad = matmul_tn(second_input, grad_gate).astype(bf16)
    up_grad = matmul_tn(second_input, grad_up).astype(bf16)
    down_grad, gate_grad, up_grad = (
        lax.psum_scatter(item, both, scatter_dimension=0, tiled=True).astype(f32)
        for item in (down_grad, gate_grad, up_grad)
    )

    second_back = second_back.reshape(tokens, width).astype(f32)
    second_gain_term = jnp.sum(second_back * second_normed, axis=0)
    grad_own = take(out_grad, z, own, 1).reshape(tokens, width).astype(f32)
    grad_stream = grad_own + norm_back(second_back, second_normed, second_scale, second_gain)
    grad_attn = grad_stream.astype(bf16)

    grad_attended = matmul(grad_attn, output_full).astype(bf16)
    grad_query, key_terms, value_terms = attend_back_call(
        query_rot,
        grad_attended.reshape(rows, own, q_all),
        cosine,
        sine,
        keys,
        values,
        key_pos,
        limit,
        logs,
    )
    key_terms = scatter_seq(split(key_terms, n_seq, 1), order_b, 1)
    value_terms = scatter_seq(split(value_terms, n_seq, 1), order_a, 1)
    kv_terms = [
        jnp.concatenate(pair, axis=-1)
        for pair in zip(split(key_terms, n_heads, 1), split(value_terms, n_heads, 1))
    ]
    grad_kv = turn_back_call(scatter_ring(kv_terms, "heads"), cosine, sine)
    grad_kv = grad_kv.reshape(tokens, 2 * kv_width)
    grad_query = grad_query.reshape(tokens, q_all)

    query_grad = matmul_tn(input_flat, grad_query).astype(bf16)
    output_grad = matmul_tn(grad_attn, attended).astype(bf16)

    def scatter_rows(full, masks):
        mine = add_low(take(full, c, half, 0), swap(take(full, 1 - c, half, 0), "dp", 1))
        blocks = [take(mine, s ^ r, depth, 0) for r in range(n_seq)]
        return scatter_seq(blocks, masks, 0)

    query_part = scatter_rows(query_grad, order_b)
    output_part = scatter_rows(output_grad, order_a)
    qo_parts = [
        jnp.concatenate(
            [
                take(part, (z + m) % n_heads, q_own, 1)
                for part in (query_part, output_part)
            ],
            axis=1,
        )
        for m in range(n_heads)
    ]
    qo_grad = scatter_ring(qo_parts, "heads").astype(f32)
    query_weight_grad = qo_grad[:, :q_own]
    output_weight_grad = qo_grad[:, q_own:].T

    kv_grad = matmul_tn(input_flat, grad_kv).astype(bf16)
    kv_part = scatter_rows(kv_grad, order_a)
    kv_cut = kv_width // n_heads
    kv_parts = [
        jnp.concatenate(
            [
                take(part, (z + m) % n_heads, kv_cut, 1)
                for part in (kv_part[:, :kv_width], kv_part[:, kv_width:])
            ],
            axis=1,
        )
        for m in range(n_heads)
    ]
    kv_sum = scatter_ring(kv_parts, "heads").astype(f32)

    first_scale = rms_scale(stream)
    first_normed = stream * first_scale
    first_gain = attn_gain.astype(f32)
    first_back = (
        matmul_nt(grad_query, query_full)
        + matmul_nt(grad_kv[:, :kv_width], key_weight)
        + matmul_nt(grad_kv[:, kv_width:], value_weight)
    )
    first_gain_term = jnp.sum(first_back * first_normed, axis=0)
    residual_grad = grad_stream + norm_back(first_back, first_normed, first_scale, first_gain)

    terms = [
        first_gain_term,
        second_gain_term,
        jnp.sum(grad_query.astype(f32), axis=0),
        jnp.sum(grad_kv.astype(f32), axis=0),
    ]
    sums = jnp.concatenate(terms).reshape(-1, HD)
    for axis in ("dp", "seq", "heads"):
        bit = 1
        while bit < lax.axis_size(axis):
            sums = sums + swap(sums, axis, bit)
            bit *= 2
    sums = sums.reshape(-1)
    gain_piece = width // (lax.axis_size("dp") * n_seq * n_heads)
    gain_at = (piece * n_heads + z) * gain_piece
    attn_gain_grad = lax.dynamic_slice_in_dim(sums, gain_at, gain_piece, 0)
    ffn_gain_grad = lax.dynamic_slice_in_dim(sums, width + gain_at, gain_piece, 0)
    query_bias_grad = lax.dynamic_slice_in_dim(sums, 2 * width + z * q_own, q_own, 0)
    kv_at = 2 * width + q_all + z * kv_cut
    key_bias_grad = lax.dynamic_slice_in_dim(sums, kv_at, kv_cut, 0)
    value_bias_grad = lax.dynamic_slice_in_dim(sums, kv_at + kv_width, kv_cut, 0)

    return (
        block_out.astype(bf16),
        residual_grad.reshape(rows, own, width),
        attn_gain_grad,
        query_weight_grad,
        query_bias_grad,
        kv_sum[:, :kv_cut],
        key_bias_grad,
        kv_sum[:, kv_cut:],
        value_bias_grad,
        output_weight_grad,
        ffn_gain_grad,
        gate_grad,
        up_grad,
        down_grad.T,
    )


def solution(mesh):
    in_specs = (
        P("dp", ("seq", "heads"), None),
        P("dp", "seq", None),
        P("dp"),
        P(),
        P(None, "heads"),
        P("heads"),
        P(),
        P(),
        P(),
        P(),
        P("heads", None),
        P(),
        P(("dp", "seq"), "heads"),
        P(("dp", "seq"), "heads"),
        P("heads", ("dp", "seq")),
    )
    out_specs = (
        P("dp", ("seq", "heads"), None),
        P("dp", ("seq", "heads"), None),
        P(("dp", "seq", "heads")),
        P(("dp", "seq"), "heads"),
        P("heads"),
        P(("dp", "seq"), "heads"),
        P("heads"),
        P(("dp", "seq"), "heads"),
        P("heads"),
        P("heads", ("dp", "seq")),
        P(("dp", "seq", "heads")),
        P(("dp", "seq"), "heads"),
        P(("dp", "seq"), "heads"),
        P("heads", ("dp", "seq")),
    )
    return jax.shard_map(local, mesh=mesh, in_specs=in_specs, out_specs=out_specs, check_vma=False)
```

time: 1430 us -> 847 us (0.59)
  waiting for transfers between devices: 950 us -> 423 us
  matrix products: 298 us -> 149 us
  starting transfers between devices: 5.21 us -> 79.8 us
  local copies, waits for them, and re-layouts: 32.7 us -> 77.1 us
  blocking collectives: 38.9 us -> 0 us
  Pallas kernels: 0 us -> 38.1 us
  other arithmetic: 76.5 us -> 49.3 us
    psum x2 -> x0, waiting for transfers between devices: 491 us -> none  [the longest x1 247 us: local(): lax.psum(second_spread, 'heads')]
    reduce_scatter x9 -> x4, waiting for transfers between devices: 308 us -> 93.9 us  [the longest x2 88 us: local(): lax.psum_scatter(item, both, scatter_dimension=0, tiled=True).astype(f32)]
    dot_general x27 -> x18, matrix products: 298 us -> 149 us  [the longest x5 59.2 us: matmul(): return jnp.dot(left, right, preferred_element_type=f32)]
    all_gather x6 -> x4, waiting for transfers between devices: 86 us -> 192 us  [the longest x1 68.5 us: local(): lax.all_gather(second_own, 'heads', axis=1, tiled=True)]
    ppermute x1 -> x43, waiting for transfers between devices: 34.9 us -> 135 us  [the longest x28 124 us: swap(): return lax.ppermute(value, axis, pairs)]
    ppermute x1 -> x43, starting transfers between devices: 3.17 us -> 79.2 us  [the longest x28 54.9 us: swap(): return lax.ppermute(value, axis, pairs)]
    psum x1 -> x0, blocking collectives: 38.9 us -> none  [local(): lax.psum((first_gain_term, second_gain_term, query_shift_term, key_shift_...]
    pallas_call x0 -> x4, Pallas kernels: none -> 38.1 us  [the longest x1 21.6 us: attend_back_call(): pl.pallas_call(attend_back_kernel, grid=(rows, groups), in_specs=[part, p...]
  transfers between devices with their start and end apart: 20 -> 52, of which waited for: 13 -> 27; matrix products, arithmetic and copies ran while one was open for 18% -> 25% of each run, Pallas kernels for 0% -> 3%
where the time goes in v1:
time: 847 us; the launch traced here: 833 us
  waiting for transfers between devices  423 us (50%)
  matrix products  149 us (18%)
  starting transfers between devices  79.8 us (9%)
  local copies, waits for them, and re-layouts  77.1 us (9%)
  other arithmetic  49.3 us (6%)
  Pallas kernels  38.1 us (4%)
  between operations  15.6 us (2%)
    ppermute x28, waiting for transfers between devices, swap(): return lax.ppermute(value, axis, pairs)  124 us
    reduce_scatter x2, waiting for transfers between devices, local(): lax.psum_scatter(item, both, scatter_dimension=0, tiled=True).astype(f32)  88 us
    all_gather x1, waiting for transfers between devices, local(): lax.all_gather(second_own, 'heads', axis=1, tiled=True)  68.5 us
    dot_general x5, matrix products, matmul(): return jnp.dot(left, right, preferred_element_type=f32)  59.2 us
    ppermute x28, starting transfers between devices, swap(): return lax.ppermute(value, axis, pairs)  54.9 us
    all_gather x1, waiting for transfers between devices, local(): gate_full = lax.all_gather(gate_weight, both, axis=0, tiled=True)  52.3 us
    dot_general x6, matrix products, matmul_tn(): lax.dot_general(left, right, (((0,), (0,)), ((), ())), preferred_element_...  46.4 us
    unnamed x192, local copies, waits for them, and re-layouts  45.1 us
  transfers between devices with their start and end apart: 52, of which 27 were waited for; matrix products, arithmetic and copies ran while one was open for 25% of the time, Pallas kernels for 3%

profile of v1, /device:TPU:9, one launch (start us, length us, event | category | flops | bytes accessed | tf_op | source)
XLA Modules:
  0.0 832.6 jit_solution(5911523118307279069)
XLA Ops:
  22.6 3.5 collective-permute-start
  65.2 7.6 collective-permute-done.3
  76.8 8.7 %collective-permute-done.9 = bf16[3,384,256]{2,1,0:T(8,128)(2,1)S(1)} collective-permute-done((bf16[3,384,256]{2,1,0:T(8,128)(2,1)S(1)}, bf16[3,384,256]{2,1,0:T(8,128)(2,1)S(1)}, u32[]{:S(2)}, u32[]{:S(2)}) %collective-permute-start.9) | collective-permute-done | bytes 589856 | tf_op jit(solution)/shard_map/ppermute | solution.py:24
  86.8 23.1 %collective-permute-done.13 = bf16[192,1536]{1,0:T(8,128)(2,1)S(1)} collective-permute-done((bf16[192,1536]{1,0:T(8,128)(2,1)S(1)}, bf16[192,1536]{1,0:T(8,128)(2,1)S(1)}, u32[]{:S(2)}, u32[]{:S(2)}) %collective-permute-start.13) | collective-permute-done | bytes 589856 | tf_op jit(solution)/shard_map/ppermute | solution.py:24
  110.3 15.5 %collective-permute-start.5 = (bf16[768,1536]{1,0:T(8,128)(2,1)S(1)}, bf16[768,1536]{1,0:T(8,128)(2,1)S(1)}, u32[]{:S(2)}, u32[]{:S(2)}) collective-permute-start(bf16[768,1536]{1,0:T(8,128)(2,1)S(1)} %slice_dynamic-update-slice_fusion.4), channel_id=1, source_target_pairs={{0,16},{16,0},{1,17},{17,1},{2,18},{18,2},{3,19},{19,3},{4,20},{20... | collective-permute-start | bytes 7077896 | tf_op jit(solution)/shard_map/ppermute | solution.py:24
  128.6 12.5 %collective-permute-start.15 = (bf16[768,1536]{1,0:T(8,128)(2,1)S(1)}, bf16[768,1536]{1,0:T(8,128)(2,1)S(1)}, u32[]{:S(2)}, u32[]{:S(2)}) collective-permute-start(bf16[768,1536]{1,0:T(8,128)(2,1)S(1)} %slice_dynamic-update-slice_fusion), channel_id=1, source_target_pairs={{0,16},{16,0},{1,17},{17,1},{2,18},{18,2},{3,19},{19,3},{4,20},{20... | collective-permute-start | bytes 7077896 | tf_op jit(solution)/shard_map/ppermute | solution.py:24
  149.4 13.8 %attend.1 = (bf16[3,96,1536]{2,1,0:T(8,128)(2,1)S(1)}, bf16[3,96,1536]{2,1,0:T(8,128)(2,1)S(1)}, f32[3,2,1,576]{3,2,1,0:T(1,128)S(1)}) custom-call(f32[3,96,1536]{2,1,0:T(8,128)S(1)} %bitcast.91, f32[96,128]{1,0:T(8,128)S(1)} %copy-done.14, f32[96,128]{1,0:T(8,128)S(1)} %copy-done.18, bf16[3,1536,256]{2,1,0:T(8,128)(2,1)} %copy-done.71, ...), custom_call_target="tpu_custom_call" | custom-call | flops 2717908992 | bytes 4718592 | tf_op jit(solution)/shard_map/attend/pallas_call | solution.py:183
  169.6 68.5 %all-gather.5.cloned.1.call-done = bf16[3,384,1536]{2,1,0:T(8,128)(2,1)} async-done(((bf16[3,96,1536]{2,1,0:T(8,128)(2,1)}), bf16[3,384,1536]{2,1,0:T(8,128)(2,1)}) %all-gather.5.cloned.1.call-update) | async-done | bytes 3538960 | tf_op jit(solution)/shard_map/all_gather | solution.py:450
  238.1 52.3 %all-gather.7.cloned.1.call-done = bf16[1536,2240]{1,0:T(8,128)(2,1)} async-done(((bf16[192,2240]{1,0:T(8,128)(2,1)}), bf16[1536,2240]{1,0:T(8,128)(2,1)}) %all-gather.7.cloned.1.call-update) | async-done | bytes 6881296 | tf_op jit(solution)/shard_map/all_gather | solution.py:433
  290.4 14.9 %fusion.38 = f32[1152,2240]{0,1:T(8,128)} fusion(bf16[1152,1536]{1,0:T(8,128)(2,1)} %bitcast.107, bf16[1536,2240]{1,0:T(8,128)(2,1)} %all-gather.7.cloned.1.call-done), kind=kOutput, calls=%fused_computation.214 | convolution fusion | flops 7927234560 | bytes 20742144 | tf_op jit(solution)/shard_map/dot_general | solution.py:317
  305.3 35.9 %all-gather.9.cloned.1.call-done = bf16[1536,2240]{1,0:T(8,128)(2,1)} async-done(((bf16[192,2240]{1,0:T(8,128)(2,1)}), bf16[1536,2240]{1,0:T(8,128)(2,1)}) %all-gather.9.cloned.1.call-update) | async-done | bytes 6881296 | tf_op jit(solution)/shard_map/all_gather | solution.py:434
  341.2 15.0 %fusion.39 = f32[1152,2240]{0,1:T(8,128)} fusion(bf16[1152,1536]{1,0:T(8,128)(2,1)} %bitcast.108, bf16[1536,2240]{1,0:T(8,128)(2,1)} %all-gather.9.cloned.1.call-done), kind=kOutput, calls=%fused_computation.215 | convolution fusion | flops 7927234560 | bytes 20742144 | tf_op jit(solution)/shard_map/dot_general | solution.py:317
  356.2 35.6 %all-gather.11.cloned.1.call-done = bf16[1536,2240]{1,0:T(8,128)(2,1)} async-done(((bf16[192,2240]{1,0:T(8,128)(2,1)}), bf16[1536,2240]{1,0:T(8,128)(2,1)}) %all-gather.11.cloned.1.call-update) | async-done | bytes 6881296 | tf_op jit(solution)/shard_map/all_gather | solution.py:432
  391.8 23.2 %multiply_convert_fusion = (bf16[1152,2240]{0,1:T(8,128)(2,1)}, bf16[1152,2240]{0,1:T(8,128)(2,1)}, bf16[1152,2240]{0,1:T(8,128)(2,1)}) fusion(f32[1152,2240]{0,1:T(8,128)} %fusion.38, f32[1152,2240]{0,1:T(8,128)} %fusion.39, bf16[1152,1536]{1,0:T(8,128)(2,1)S(1)} %bitcast.84, bf16[1536,2240]{1,0:T(8,128)(2,1)} %all-gather.11.cloned.1.call-done), kind=kOutput, calls=%fused_computation.3 | convolution fusion | flops 7965941760 | bytes 46546944 | tf_op jit(solution)/shard_map/dot_general | solution.py:317
  415.1 12.6 %fusion.40 = f32[1152,1536]{1,0:T(8,128)S(1)} fusion(bf16[1152,2240]{0,1:T(8,128)(2,1)} %get-tuple-element.83, bf16[1536,2240]{1,0:T(8,128)(2,1)} %all-gather.7.cloned.1.call-done), kind=kOutput, calls=%fused_computation.216 | convolution fusion | flops 7927234560 | bytes 19120128 | tf_op jit(solution)/shard_map/dot_general | solution.py:321
  427.7 13.2 %fusion.2 = bf16[1152,1536]{1,0:T(8,128)(2,1)} fusion(f32[1152,1536]{1,0:T(8,128)S(1)} %fusion.40, bf16[1152,2240]{0,1:T(8,128)(2,1)} %get-tuple-element.82, bf16[1536,2240]{1,0:T(8,128)(2,1)S(1)} %copy-done.76), kind=kOutput, calls=%fused_computation.11 | convolution fusion | flops 7930773504 | bytes 22659072 | tf_op jit(solution)/shard_map/dot_general | solution.py:321
  440.9 13.6 %convolution_convert_fusion.4 = bf16[1152,1536]{1,0:T(8,128)(2,1)} fusion(bf16[1152,2240]{0,1:T(8,128)(2,1)} %get-tuple-element.84, bf16[1536,2240]{1,0:T(8,128)(2,1)} %all-gather.11.cloned.1.call-done), kind=kOutput, calls=%fused_computation.13 | convolution fusion | flops 7929004032 | bytes 15581184 | tf_op jit(solution)/shard_map/dot_general | solution.py:321
  454.6 13.4 %fusion.1 = bf16[1536,2240]{0,1:T(8,128)(2,1)} fusion(bf16[1152,2240]{0,1:T(8,128)(2,1)} %get-tuple-element.84, bf16[1152,1536]{1,0:T(8,128)(2,1)S(1)} %bitcast.85), kind=kOutput, calls=%fused_computation.8 | convolution fusion | flops 7930675200 | bytes 15581184 | tf_op jit(solution)/shard_map/dot_general | solution.py:325
  468.1 10.0 %copy.45 = bf16[1536,2240]{1,0:T(8,128)(2,1)} copy(bf16[1536,2240]{0,1:T(8,128)(2,1)} %fusion.1) | data formatting | bytes 13762560
  478.2 14.6 %convolution_convert_fusion.1 = bf16[1536,2240]{1,0:T(8,128)(2,1)} fusion(bf16[1152,1536]{1,0:T(8,128)(2,1)} %bitcast.109, bf16[1152,2240]{0,1:T(8,128)(2,1)} %get-tuple-element.82), kind=kOutput, calls=%fused_computation.1 | convolution fusion | flops 7930675200 | bytes 15581184 | tf_op jit(solution)/shard_map/dot_general | solution.py:325
  500.9 5.9 reduce-scatter.10.cloned.1.call-done
  510.8 4.5 convolution_convert_fusion.5
  515.4 21.6 %attend_back.1 = (bf16[3,96,1536]{2,1,0:T(8,128)(2,1)S(1)}, bf16[3,1536,256]{2,1,0:T(8,128)(2,1)S(1)}, bf16[3,1536,256]{2,1,0:T(8,128)(2,1)}) custom-call(bf16[3,96,1536]{2,1,0:T(8,128)(2,1)S(1)} %copy-done.28, bf16[3,96,1536]{2,1,0:T(8,128)(2,1)S(1)} %bitcast.94, f32[96,128]{1,0:T(8,128)S(1)} %copy-done.15, f32[96,128]{1,0:T(8,128)S(1)} %copy-done.19, ...), custom_call_target="tpu_custom_call" | custom-call | flops 6794772480 | bytes 9437184 | tf_op jit(solution)/shard_map/attend_back/pallas_call | solution.py:261
  546.3 17.9 %collective-permute-done.16 = bf16[3,768,256]{2,1,0:T(8,128)(2,1)S(1)} collective-permute-done((bf16[3,768,256]{2,1,0:T(8,128)(2,1)S(1)}, bf16[3,768,256]{2,1,0:T(8,128)(2,1)S(1)}, u32[]{:S(2)}, u32[]{:S(2)}) %collective-permute-start.16) | collective-permute-done | bytes 1179680 | tf_op jit(solution)/shard_map/ppermute | solution.py:24
  572.0 6.1 collective-permute-done.17
  579.2 4.8 collective-permute-done.19
  586.0 11.6 %convolution_convert_fusion.2 = bf16[1536,2240]{1,0:T(8,128)(2,1)} fusion(bf16[1152,1536]{1,0:T(8,128)(2,1)S(1)} %bitcast.110, bf16[1152,2240]{0,1:T(8,128)(2,1)S(1)} %bitcast.112), kind=kOutput, calls=%fused_computation.2 | convolution fusion | flops 7930675200 | bytes 15581184 | tf_op jit(solution)/shard_map/dot_general | solution.py:325
  629.9 34.9 %collective-permute-done.24 = f32[40,128]{1,0:T(8,128)S(1)} collective-permute-done((f32[40,128]{1,0:T(8,128)S(1)}, f32[40,128]{1,0:T(8,128)S(1)}, u32[]{:S(2)}, u32[]{:S(2)}) %collective-permute-start.24) | collective-permute-done | bytes 20512 | tf_op jit(solution)/shard_map/ppermute | solution.py:24
  679.3 3.8 collective-permute-done.38
  691.9 6.5 collective-permute-done.30
  718.9 21.4 %reduce-scatter.14.cloned.1.call-done = bf16[192,2240]{1,0:T(8,128)(2,1)} async-done(((bf16[1536,2240]{1,0:T(8,128)(2,1)}), bf16[192,2240]{1,0:T(8,128)(2,1)}) %reduce-scatter.14.cloned.1.call-update) | async-done | bytes 860176 | tf_op jit(solution)/shard_map/reduce_scatter | solution.py:476
  742.7 66.6 %reduce-scatter.12.cloned.1.call-done = bf16[192,2240]{1,0:T(8,128)(2,1)} async-done(((bf16[1536,2240]{1,0:T(8,128)(2,1)}), bf16[192,2240]{1,0:T(8,128)(2,1)}) %reduce-scatter.12.cloned.1.call-update) | async-done | bytes 860176 | tf_op jit(solution)/shard_map/reduce_scatter | solution.py:476
  (423 shorter events, 203.7 us)
Async XLA Ops:
  7.2 230.9 %all-gather.5.cloned.1.call-start = ((), (), s32[]{:S(2)}) async-start(), calls=%async_computation.5 | async-start | bytes 4423680 | tf_op jit(solution)/shard_map/all_gather | solution.py:450
  16.5 21.6 %collective-permute-start.6 = (bf16[3,96,512]{2,1,0:T(8,128)(2,1)}, bf16[3,96,512]{2,1,0:T(8,128)(2,1)}, u32[]{:S(2)}, u32[]{:S(2)}) collective-permute-start(bf16[3,96,512]{2,1,0:T(8,128)(2,1)} %get-tuple-element.23), channel_id=1, source_target_pairs={{0,3},{1,0},{2,1},{3,2},{4,7},{5,4},{6,5},{7,6},{8,11},{9,8},{10,9... | collective-permute-start | bytes 884744 | tf_op jit(solution)/shard_map/ppermute | solution.py:30
  46.6 16.7 %collective-permute-start.8 = (bf16[3,96,512]{2,1,0:T(8,128)(2,1)S(1)}, bf16[3,96,512]{2,1,0:T(8,128)(2,1)S(1)}, u32[]{:S(2)}, u32[]{:S(2)}) collective-permute-start(bf16[3,96,512]{2,1,0:T(8,128)(2,1)S(1)} %collective-permute-done.7), channel_id=1, source_target_pairs={{0,3},{1,0},{2,1},{3,2},{4,7},{5,4},{6,5},{7,6},{8,11},{9,8},{10,9... | collective-permute-start | bytes 884744 | tf_op jit(solution)/shard_map/ppermute | solution.py:30
  64.6 20.9 %collective-permute-start.9 = (bf16[3,384,256]{2,1,0:T(8,128)(2,1)S(1)}, bf16[3,384,256]{2,1,0:T(8,128)(2,1)S(1)}, u32[]{:S(2)}, u32[]{:S(2)}) collective-permute-start(bf16[3,384,256]{2,1,0:T(8,128)(2,1)S(1)} %pad_maximum_fusion.5), channel_id=1, source_target_pairs={{0,4},{4,0},{8,12},{12,8},{1,5},{5,1},{9,13},{13,9},{2,6},{6,2},{1... | collective-permute-start | bytes 1769480 | tf_op jit(solution)/shard_map/ppermute | solution.py:24
  72.9 37.3 %collective-permute-start.4 = (bf16[384,1536]{1,0:T(8,128)(2,1)S(1)}, bf16[384,1536]{1,0:T(8,128)(2,1)S(1)}, u32[]{:S(2)}, u32[]{:S(2)}) collective-permute-start(bf16[384,1536]{1,0:T(8,128)(2,1)S(1)} %pad_maximum_fusion), channel_id=1, source_target_pairs={{0,8},{4,12},{8,0},{12,4},{1,9},{5,13},{9,1},{13,5},{2,10},{6,14},... | collective-permute-start | bytes 3538952 | tf_op jit(solution)/shard_map/ppermute | solution.py:24
  74.5 35.5 %collective-permute-start.13 = (bf16[192,1536]{1,0:T(8,128)(2,1)S(1)}, bf16[192,1536]{1,0:T(8,128)(2,1)S(1)}, u32[]{:S(2)}, u32[]{:S(2)}) collective-permute-start(bf16[192,1536]{1,0:T(8,128)(2,1)S(1)} %get-tuple-element.77), channel_id=1, source_target_pairs={{0,8},{4,12},{8,0},{12,4},{1,9},{5,13},{9,1},{13,5},{2,10},{6,14},... | collective-permute-start | bytes 1769480 | tf_op jit(solution)/shard_map/ppermute | solution.py:24
  75.5 67.8 %collective-permute-start.12 = (bf16[3,768,256]{2,1,0:T(8,128)(2,1)S(1)}, bf16[3,768,256]{2,1,0:T(8,128)(2,1)S(1)}, u32[]{:S(2)}, u32[]{:S(2)}) collective-permute-start(bf16[3,768,256]{2,1,0:T(8,128)(2,1)S(1)} %constant_dynamic-update-slice_fusion.20), channel_id=1, source_target_pairs={{0,4},{4,0},{8,12},{12,8},{1,5},{5,1},{9,13},{13,9},{2,6},{6,2},{1... | collective-permute-start | bytes 3538952 | tf_op jit(solution)/shard_map/ppermute | solution.py:24
  85.5 57.8 %collective-permute-start.10 = (bf16[3,768,256]{2,1,0:T(8,128)(2,1)S(1)}, bf16[3,768,256]{2,1,0:T(8,128)(2,1)S(1)}, u32[]{:S(2)}, u32[]{:S(2)}) collective-permute-start(bf16[3,768,256]{2,1,0:T(8,128)(2,1)S(1)} %get-tuple-element.111), channel_id=1, source_target_pairs={{0,8},{4,12},{8,0},{12,4},{1,9},{5,13},{9,1},{13,5},{2,10},{6,14},... | collective-permute-start | bytes 3538952 | tf_op jit(solution)/shard_map/ppermute | solution.py:24
  110.0 18.4 %collective-permute-start.14 = (bf16[384,1536]{1,0:T(8,128)(2,1)S(1)}, bf16[384,1536]{1,0:T(8,128)(2,1)S(1)}, u32[]{:S(2)}, u32[]{:S(2)}) collective-permute-start(bf16[384,1536]{1,0:T(8,128)(2,1)S(1)} %pad_maximum_fusion.1), channel_id=1, source_target_pairs={{0,4},{4,0},{8,12},{12,8},{1,5},{5,1},{9,13},{13,9},{2,6},{6,2},{1... | collective-permute-start | bytes 3538952 | tf_op jit(solution)/shard_map/ppermute | solution.py:24
  110.3 36.2 %collective-permute-start.5 = (bf16[768,1536]{1,0:T(8,128)(2,1)S(1)}, bf16[768,1536]{1,0:T(8,128)(2,1)S(1)}, u32[]{:S(2)}, u32[]{:S(2)}) collective-permute-start(bf16[768,1536]{1,0:T(8,128)(2,1)S(1)} %slice_dynamic-update-slice_fusion.4), channel_id=1, source_target_pairs={{0,16},{16,0},{1,17},{17,1},{2,18},{18,2},{3,19},{19,3},{4,20},{20... | collective-permute-start | bytes 7077896 | tf_op jit(solution)/shard_map/ppermute | solution.py:24
  128.6 17.9 %collective-permute-start.15 = (bf16[768,1536]{1,0:T(8,128)(2,1)S(1)}, bf16[768,1536]{1,0:T(8,128)(2,1)S(1)}, u32[]{:S(2)}, u32[]{:S(2)}) collective-permute-start(bf16[768,1536]{1,0:T(8,128)(2,1)S(1)} %slice_dynamic-update-slice_fusion), channel_id=1, source_target_pairs={{0,16},{16,0},{1,17},{17,1},{2,18},{18,2},{3,19},{19,3},{4,20},{20... | collective-permute-start | bytes 7077896 | tf_op jit(solution)/shard_map/ppermute | solution.py:24
  167.4 123.1 %all-gather.7.cloned.1.call-start = ((), (), s32[]{:S(2)}) async-start(), calls=%async_computation.6 | async-start | bytes 7962624 | tf_op jit(solution)/shard_map/all_gather | solution.py:433
  168.1 173.1 %all-gather.9.cloned.1.call-start = ((), (), s32[]{:S(2)}) async-start(), calls=%async_computation.7 | async-start | bytes 7962624 | tf_op jit(solution)/shard_map/all_gather | solution.py:434
  168.9 223.0 %all-gather.11.cloned.1.call-start = ((), (), s32[]{:S(2)}) async-start(), calls=%async_computation.8 | async-start | bytes 7962624 | tf_op jit(solution)/shard_map/all_gather | solution.py:432
  169.4 337.4 %reduce-scatter.10.cloned.1.call-start = ((), (), s32[]{:S(2)}) async-start(), calls=%async_computation.10 | async-start | bytes 4423680 | tf_op jit(solution)/shard_map/reduce_scatter | solution.py:463
  440.9 161.1 %reduce-scatter.8.cloned.1.call-start = ((), (), s32[]{:S(2)}) async-start(), calls=%async_computation.9 | async-start | bytes 4423680 | tf_op jit(solution)/shard_map/reduce_scatter | solution.py:470
  454.6 251.0 %reduce-scatter.16.cloned.1.call-start = ((), (), s32[]{:S(2)}) async-start(), calls=%async_computation.13 | async-start | bytes 7962624
  478.1 262.1 %reduce-scatter.14.cloned.1.call-start = ((), (), s32[]{:S(2)}) async-start(), calls=%async_computation.12 | async-start | bytes 7962624 | tf_op jit(solution)/shard_map/reduce_scatter | solution.py:476
  492.8 316.5 %reduce-scatter.12.cloned.1.call-start = ((), (), s32[]{:S(2)}) async-start(), calls=%async_computation.11 | async-start | bytes 7962624 | tf_op jit(solution)/shard_map/reduce_scatter | solution.py:476
  537.1 27.1 %collective-permute-start.16 = (bf16[3,768,256]{2,1,0:T(8,128)(2,1)S(1)}, bf16[3,768,256]{2,1,0:T(8,128)(2,1)S(1)}, u32[]{:S(2)}, u32[]{:S(2)}) collective-permute-start(bf16[3,768,256]{2,1,0:T(8,128)(2,1)S(1)} %concatenate.118), channel_id=1, source_target_pairs={{0,8},{4,12},{8,0},{12,4},{1,9},{5,13},{9,1},{13,5},{2,10},{6,14},... | collective-permute-start | bytes 3538952 | tf_op jit(solution)/shard_map/ppermute | solution.py:24
  539.2 29.6 %collective-permute-start.18 = (bf16[3,768,256]{2,1,0:T(8,128)(2,1)S(1)}, bf16[3,768,256]{2,1,0:T(8,128)(2,1)S(1)}, u32[]{:S(2)}, u32[]{:S(2)}) collective-permute-start(bf16[3,768,256]{2,1,0:T(8,128)(2,1)S(1)} %pad_maximum_fusion.2), channel_id=1, source_target_pairs={{0,4},{4,0},{8,12},{12,8},{1,5},{5,1},{9,13},{13,9},{2,6},{6,2},{1... | collective-permute-start | bytes 3538952 | tf_op jit(solution)/shard_map/ppermute | solution.py:24
  567.1 44.1 %collective-permute-start.28 = (bf16[768,1536]{1,0:T(8,128)(2,1)}, bf16[768,1536]{1,0:T(8,128)(2,1)}, u32[]{:S(2)}, u32[]{:S(2)}) collective-permute-start(bf16[768,1536]{1,0:T(8,128)(2,1)} %constant_dynamic-slice_fusion.24), channel_id=1, source_target_pairs={{0,16},{16,0},{1,17},{17,1},{2,18},{18,2},{3,19},{19,3},{4,20},{20... | collective-permute-start | bytes 7077896 | tf_op jit(solution)/shard_map/ppermute | solution.py:24
  568.9 15.0 %collective-permute-start.19 = (bf16[3,384,256]{2,1,0:T(8,128)(2,1)S(1)}, bf16[3,384,256]{2,1,0:T(8,128)(2,1)S(1)}, u32[]{:S(2)}, u32[]{:S(2)}) collective-permute-start(bf16[3,384,256]{2,1,0:T(8,128)(2,1)S(1)} %add_convert_fusion.11), channel_id=1, source_target_pairs={{0,8},{4,12},{8,0},{12,4},{1,9},{5,13},{9,1},{13,5},{2,10},{6,14},... | collective-permute-start | bytes 1769480 | tf_op jit(solution)/shard_map/ppermute | solution.py:24
  571.8 45.2 %collective-permute-start.31 = (bf16[768,1536]{1,0:T(8,128)(2,1)}, bf16[768,1536]{1,0:T(8,128)(2,1)}, u32[]{:S(2)}, u32[]{:S(2)}) collective-permute-start(bf16[768,1536]{1,0:T(8,128)(2,1)} %constant_dynamic-slice_fusion.20), channel_id=1, source_target_pairs={{0,16},{16,0},{1,17},{17,1},{2,18},{18,2},{3,19},{19,3},{4,20},{20... | collective-permute-start | bytes 7077896 | tf_op jit(solution)/shard_map/ppermute | solution.py:24
  615.8 60.9 %collective-permute-start.29 = (bf16[384,1536]{1,0:T(8,128)(2,1)}, bf16[384,1536]{1,0:T(8,128)(2,1)}, u32[]{:S(2)}, u32[]{:S(2)}) collective-permute-start(bf16[384,1536]{1,0:T(8,128)(2,1)} %pad_maximum_fusion.3), channel_id=1, source_target_pairs={{0,8},{4,12},{8,0},{12,4},{1,9},{5,13},{9,1},{13,5},{2,10},{6,14},... | collective-permute-start | bytes 3538952 | tf_op jit(solution)/shard_map/ppermute | solution.py:24
  627.3 56.2 %collective-permute-start.32 = (bf16[384,1536]{1,0:T(8,128)(2,1)S(1)}, bf16[384,1536]{1,0:T(8,128)(2,1)S(1)}, u32[]{:S(2)}, u32[]{:S(2)}) collective-permute-start(bf16[384,1536]{1,0:T(8,128)(2,1)S(1)} %pad_maximum_fusion.4), channel_id=1, source_target_pairs={{0,4},{4,0},{8,12},{12,8},{1,5},{5,1},{9,13},{13,9},{2,6},{6,2},{1... | collective-permute-start | bytes 3538952 | tf_op jit(solution)/shard_map/ppermute | solution.py:24
  628.1 36.8 %collective-permute-start.24 = (f32[40,128]{1,0:T(8,128)S(1)}, f32[40,128]{1,0:T(8,128)S(1)}, u32[]{:S(2)}, u32[]{:S(2)}) collective-permute-start(f32[40,128]{1,0:T(8,128)S(1)} %fusion.73), channel_id=1, source_target_pairs={{0,4},{4,0},{8,12},{12,8},{1,5},{5,1},{9,13},{13,9},{2,6},{6,2},{1... | collective-permute-start | bytes 61448 | tf_op jit(solution)/shard_map/ppermute | solution.py:24
  678.0 20.4 %collective-permute-start.30 = (bf16[192,1536]{1,0:T(8,128)(2,1)S(1)}, bf16[192,1536]{1,0:T(8,128)(2,1)S(1)}, u32[]{:S(2)}, u32[]{:S(2)}) collective-permute-start(bf16[192,1536]{1,0:T(8,128)(2,1)S(1)} %add_convert_fusion.8), channel_id=1, source_target_pairs={{0,4},{4,0},{8,12},{12,8},{1,5},{5,1},{9,13},{13,9},{2,6},{6,2},{1... | collective-permute-start | bytes 1769480 | tf_op jit(solution)/shard_map/ppermute | solution.py:24
  683.7 16.8 %collective-permute-start.33 = (bf16[192,1536]{1,0:T(8,128)(2,1)S(1)}, bf16[192,1536]{1,0:T(8,128)(2,1)S(1)}, u32[]{:S(2)}, u32[]{:S(2)}) collective-permute-start(bf16[192,1536]{1,0:T(8,128)(2,1)S(1)} %add_convert_fusion.5), channel_id=1, source_target_pairs={{0,8},{4,12},{8,0},{12,4},{1,9},{5,13},{9,1},{13,5},{2,10},{6,14},... | collective-permute-start | bytes 1769480 | tf_op jit(solution)/shard_map/ppermute | solution.py:24
  690.4 17.5 %collective-permute-start.40 = (bf16[192,128]{1,0:T(8,128)(2,1)}, bf16[192,128]{1,0:T(8,128)(2,1)}, u32[]{:S(2)}, u32[]{:S(2)}) collective-permute-start(bf16[192,128]{1,0:T(8,128)(2,1)} %pad_maximum_fusion.12), channel_id=1, source_target_pairs={{0,3},{1,0},{2,1},{3,2},{4,7},{5,4},{6,5},{7,6},{8,11},{9,8},{10,9... | collective-permute-start | bytes 147464 | tf_op jit(solution)/shard_map/ppermute | solution.py:30
  709.5 102.4 %collective-permute-start.41 = (bf16[192,128]{1,0:T(8,128)(2,1)}, bf16[192,128]{1,0:T(8,128)(2,1)}, u32[]{:S(2)}, u32[]{:S(2)}) collective-permute-start(bf16[192,128]{1,0:T(8,128)(2,1)} %add_convert_fusion.27), channel_id=1, source_target_pairs={{0,3},{1,0},{2,1},{3,2},{4,7},{5,4},{6,5},{7,6},{8,11},{9,8},{10,9... | collective-permute-start | bytes 147464 | tf_op jit(solution)/shard_map/ppermute | solution.py:30
  711.4 101.7 %collective-permute-start.35 = (bf16[192,768]{1,0:T(8,128)(2,1)}, bf16[192,768]{1,0:T(8,128)(2,1)}, u32[]{:S(2)}, u32[]{:S(2)}) collective-permute-start(bf16[192,768]{1,0:T(8,128)(2,1)} %add_convert_fusion.18), channel_id=1, source_target_pairs={{0,3},{1,0},{2,1},{3,2},{4,7},{5,4},{6,5},{7,6},{8,11},{9,8},{10,9... | collective-permute-start | bytes 884744 | tf_op jit(solution)/shard_map/ppermute | solution.py:30
  (104 other events, 1180.9 us)
Sparse Core Ops, SparseCore 0:
  167.5 70.6 all-gather.4
  240.0 50.3 all-gather.6
  292.3 48.8 all-gather.8
  342.9 48.8 all-gather.10
  441.0 65.7 reduce-scatter.9
  509.0 66.6 reduce-scatter.7
  579.2 83.5 reduce-scatter.15
  666.7 73.5 reduce-scatter.13
  743.8 65.5 reduce-scatter.11

commit v2 on v1

v2 whole, which is shorter than its diff:
```python
import jax
import jax.numpy as jnp
from jax import lax
from jax.experimental import pallas as pl
from jax.experimental.layout import Layout, with_layout_constraint
from jax.experimental.pallas import tpu as pltpu
from jax.sharding import PartitionSpec as P

H = 12
KVH = 2
HD = 128

epsilon = 1e-06
rope_base = 1000000.0
hidden_logit = -1e30
log2_e = 1.4426950408889634

bf16 = jnp.bfloat16
f32 = jnp.float32
vmem_bytes = 48 * 2**20


def after(value, earlier):
    return lax.optimization_barrier((value, earlier))[0]


def swap(value, axis, mask):
    pairs = [(source, source ^ mask) for source in range(lax.axis_size(axis))]
    return lax.ppermute(value, axis, pairs)


def rotate_down(value, axis):
    size = lax.axis_size(axis)
    pairs = [(source, (source - 1) % size) for source in range(size)]
    return lax.ppermute(value, axis, pairs)


class Lanes:
    def __init__(self):
        self.sent = {}
        self.came = {}

    def send(self, key, value, move):
        sent, came = self.sent.setdefault(key, []), self.came.setdefault(key, [])
        if sent:
            value = after(value, (sent[-1], came[-2:][0]) if len(came) > 1 else sent[-1])
        sent.append(value)
        came.append(move(value))
        return came[-1]

    def seq(self, value, stage):
        size = lax.axis_size("seq")
        pairs = [
            (core * size + place, core * size + (place ^ masks[stage]))
            for core, masks in enumerate(seq_masks())
            for place in range(size)
        ]
        return self.send("seq", value, lambda v: lax.ppermute(v, ("dp", "seq"), pairs))

    def core(self, value):
        return self.send("dp", value, lambda v: swap(v, "dp", 1))

    def direct(self, values, away, gate=None):
        size = lax.axis_size("heads")
        if gate is not None:
            values = after(values, gate)
        return [
            lax.ppermute(
                value, "heads", [(i, (i + m if away else i - m) % size) for i in range(size)]
            )
            for m, value in enumerate(values, 1)
        ]

    def gather(self, block, gate=None):
        return [block] + self.direct([block] * (lax.axis_size("heads") - 1), False, gate)

    def ring(self, value):
        return self.send("heads", value, lambda v: rotate_down(v, "heads"))


class Order:
    def __init__(self):
        self.last = None

    def then(self, value):
        return value if self.last is None else after(value, self.last)

    def mark(self, value):
        self.last = value
        return value


def total_of(parts):
    result = parts[0].astype(f32)
    for part in parts[1:]:
        result = result + part.astype(f32)
    return result


def low_total(parts):
    return parts[0] if len(parts) == 1 else total_of(parts).astype(bf16)


def as_sent(sums):
    return lax.reduce_precision(sums, exponent_bits=8, mantissa_bits=7)


def join(parts, dim):
    return parts[0] if len(parts) == 1 else jnp.concatenate(parts, axis=dim)


def split(value, count, dim):
    return [value] if count == 1 else jnp.split(value, count, axis=dim)


def seq_masks():
    bits = lax.axis_size("seq").bit_length() - 1
    masks = [1 << bit for bit in range(bits)]
    return masks, masks[bits // 2 :] + masks[: bits // 2]


def seq_places():
    at = []
    for masks in seq_masks():
        mixed = [0]
        for mask in masks:
            mixed += [m ^ mask for m in mixed]
        at.append(mixed)
    s, c = lax.axis_index("seq"), lax.axis_index("dp")
    return [s ^ jnp.where(c == 0, first, second) for first, second in zip(*at)]


class SeqGather:
    def __init__(self, lanes, block, dim):
        self.lanes, self.held, self.dim, self.stage = lanes, [block], dim, 0

    def step(self):
        came = self.lanes.seq(join(self.held, self.dim), self.stage)
        self.held = self.held + [came]
        self.stage += 1
        return self

    def blocks(self, gate):
        parts, count = [], 1
        for index, part in enumerate(after(self.held, gate)):
            parts += split(part, count, self.dim)
            count *= 2 if index else 1
        return parts


class SeqScatter:
    def __init__(self, lanes, items, dim):
        self.lanes, self.items, self.dim = lanes, items, dim

    def step(self, message=None):
        half = len(self.items[0]) // 2
        if message is None:
            message = join(
                [low_total(terms) for held in self.items for terms in held[half:]], self.dim
            )
        came = self.lanes.seq(message, half.bit_length() - 1)
        parts = split(came, half * len(self.items), self.dim)
        self.items = [
            [terms + [parts[i * half + p]] for p, terms in enumerate(held[:half])]
            for i, held in enumerate(self.items)
        ]
        return self

    def terms(self):
        while len(self.items[0]) > 1:
            self.step()
        return [held[0] for held in self.items]


def gather_ring(lanes, block):
    held = [block]
    for _ in range(lax.axis_size("heads") - 1):
        held.append(lanes.ring(held[-1]))
    return held


def scatter_ring(lanes, blocks):
    terms = blocks[1]
    for block in blocks[2:] + blocks[:1]:
        terms = [lanes.ring(low_total(terms))] + block
    return terms


def by_rows(value):
    return with_layout_constraint(value, Layout(major_to_minor=tuple(range(value.ndim))))


def take(value, index, size, dim):
    return lax.dynamic_slice_in_dim(value, index * size, size, dim)


def turn(values, cosine, sine):
    return values * cosine + pltpu.roll(values, HD // 2, 1) * sine


def turn_back(values, cosine, sine):
    return values * cosine - pltpu.roll(values, HD // 2, 1) * sine


def first_kernel(x_ref, gain_ref, kw_ref, vw_ref, kb_ref, vb_ref, cos_ref, sin_ref, in_ref, kv_ref):
    x = x_ref[0].astype(f32)
    scale = lax.rsqrt(jnp.mean(x * x, axis=-1, keepdims=True) + epsilon)
    low = (x * scale * gain_ref[...].astype(f32)).astype(bf16)
    in_ref[0] = low
    width = kw_ref.shape[1]
    keys = jnp.dot(low, kw_ref[...], preferred_element_type=f32) + kb_ref[...].astype(f32)
    for at in range(0, width, HD):
        kv_ref[0, :, at : at + HD] = turn(
            keys[:, at : at + HD], cos_ref[...], sin_ref[...]
        ).astype(bf16)
    values = jnp.dot(low, vw_ref[...], preferred_element_type=f32) + vb_ref[...].astype(f32)
    kv_ref[0, :, width:] = values.astype(bf16)


def first_call(residual, gain, kw, vw, kb, vb, cosine, sine):
    rows, count, width = residual.shape
    kv = kw.shape[1]
    fixed = lambda shape: pl.BlockSpec(shape, lambda r: (0, 0))
    row = lambda size: pl.BlockSpec((1, count, size), lambda r: (r, 0, 0))
    return pl.pallas_call(
        first_kernel,
        grid=(rows,),
        in_specs=[
            row(width),
            fixed((1, width)),
            fixed((width, kv)),
            fixed((width, kv)),
            fixed((1, kv)),
            fixed((1, kv)),
            fixed((count, HD)),
            fixed((count, HD)),
        ],
        out_specs=[row(width), row(2 * kv)],
        out_shape=[
            jax.ShapeDtypeStruct((rows, count, width), bf16),
            jax.ShapeDtypeStruct((rows, count, 2 * kv), bf16),
        ],
        cost_estimate=pl.CostEstimate(
            flops=4 * rows * count * width * kv,
            bytes_accessed=2 * (2 * rows * count * width + 2 * width * kv),
            transcendentals=0,
        ),
        compiler_params=pltpu.CompilerParams(vmem_limit_bytes=vmem_bytes),
        name="first_norm",
    )(residual, gain[None], kw, vw, kb[None], vb[None], cosine, sine)


def head_columns(shift_ref, width):
    heads = width // HD
    first = pl.program_id(1) * (heads // KVH) + shift_ref[0]
    places = [lax.rem(first + h, heads) for h in range(heads // KVH)]
    return [pl.ds(pl.multiple_of(place * HD, HD), HD) for place in places]


def attend_kernel(
    shift_ref,
    q_ref,
    cos_ref,
    sin_ref,
    k_ref,
    v_ref,
    kpos_ref,
    limit_ref,
    out_ref,
    turned_ref,
    log_ref,
):
    count = q_ref.shape[1]
    columns = head_columns(shift_ref, q_ref.shape[2])
    turned = []
    for at in columns:
        u = turn(q_ref[0, :, at], cos_ref[...], sin_ref[...])
        turned_ref[0, :, at] = u.astype(bf16)
        turned.append(u)
    query = jnp.concatenate(turned, axis=0).astype(bf16)
    scores = lax.dot_general(
        k_ref[0], query, (((1,), (1,)), ((), ())), preferred_element_type=f32
    )
    seen = kpos_ref[...] <= limit_ref[0]
    scores = jnp.where(seen, scores * (HD**-0.5 * log2_e), hidden_logit)
    peak = jnp.max(scores, axis=0, keepdims=True)
    weight = jnp.exp2(scores - peak)
    total = jnp.sum(weight, axis=0, keepdims=True)
    log_ref[0, 0] = peak + jnp.log2(total)
    out = lax.dot_general(
        v_ref[0], weight.astype(bf16), (((0,), (0,)), ((), ())), preferred_element_type=f32
    )
    out = (out * (1.0 / total)).T
    for h, at in enumerate(columns):
        out_ref[0, :, at] = out[h * count : (h + 1) * count].astype(bf16)


def attend_call(shift, query, cosine, sine, kv, kpos, limit):
    rows, count, width = query.shape
    length = kv.shape[1]
    groups = KVH
    many = limit.shape[2]
    part = pl.BlockSpec((1, count, width), lambda r, g, shift: (r, 0, 0))
    fixed = lambda shape: pl.BlockSpec(shape, lambda r, g, shift: (0, 0))
    keys = pl.BlockSpec((1, length, HD), lambda r, g, shift: (r, 0, g))
    values = pl.BlockSpec((1, length, HD), lambda r, g, shift: (r, 0, KVH + g))
    work = rows * groups * length * many
    return pl.pallas_call(
        attend_kernel,
        grid_spec=pltpu.PrefetchScalarGridSpec(
            num_scalar_prefetch=1,
            grid=(rows, groups),
            in_specs=[
                part,
                fixed((count, HD)),
                fixed((count, HD)),
                keys,
                values,
                fixed((length, 1)),
                pl.BlockSpec((1, 1, many), lambda r, g, shift: (r, 0, 0)),
            ],
            out_specs=[part, part, pl.BlockSpec((1, 1, 1, many), lambda r, g, shift: (r, g, 0, 0))],
        ),
        out_shape=[
            jax.ShapeDtypeStruct((rows, count, width), bf16),
            jax.ShapeDtypeStruct((rows, count, width), bf16),
            jax.ShapeDtypeStruct((rows, groups, 1, many), f32),
        ],
        cost_estimate=pl.CostEstimate(
            flops=4 * work * HD, bytes_accessed=2 * kv.size, transcendentals=work
        ),
        compiler_params=pltpu.CompilerParams(vmem_limit_bytes=vmem_bytes),
        name="attend",
    )(shift, query, cosine, sine, kv, kv, kpos, limit)


def attend_back_kernel(
    shift_ref,
    q_ref,
    og_ref,
    cos_ref,
    sin_ref,
    k_ref,
    v_ref,
    kpos_ref,
    limit_ref,
    log_ref,
    gq_ref,
    low_ref,
    high_ref,
):
    count = q_ref.shape[1]
    columns = head_columns(shift_ref, q_ref.shape[2])

    def rows_of(ref):
        parts = [ref[0, :, at].astype(f32) for at in columns]
        return jnp.concatenate(parts, axis=0).astype(bf16)

    query, upstream = rows_of(q_ref), rows_of(og_ref)
    last = (((1,), (1,)), ((), ()))
    scores = lax.dot_general(k_ref[0], query, last, preferred_element_type=f32)
    seen = kpos_ref[...] <= limit_ref[0]
    scale = HD**-0.5
    probs = jnp.exp2(jnp.where(seen, scores * (scale * log2_e) - log_ref[0, 0], hidden_logit))
    at_keys, at_values = (
        pl.ds(pl.multiple_of((first + pl.program_id(1)) * HD, HD), HD) for first in (0, KVH)
    )
    middle = low_ref.shape[1]
    grad_values = jnp.dot(probs.astype(bf16), upstream, preferred_element_type=f32)
    low_ref[0, :, at_values] = grad_values[:middle].astype(bf16)
    high_ref[0, :, at_values] = grad_values[middle:].astype(bf16)
    grad_probs = lax.dot_general(v_ref[0], upstream, last, preferred_element_type=f32)
    mixed = probs * grad_probs
    total = jnp.sum(mixed, axis=0, keepdims=True)
    grad_scores = ((mixed - probs * total) * scale).astype(bf16)
    grad_keys = jnp.dot(grad_scores, query, preferred_element_type=f32)
    low_ref[0, :, at_keys] = grad_keys[:middle].astype(bf16)
    high_ref[0, :, at_keys] = grad_keys[middle:].astype(bf16)
    grad_query = lax.dot_general(
        k_ref[0], grad_scores, (((0,), (0,)), ((), ())), preferred_element_type=f32
    ).T
    for h, at in enumerate(columns):
        gq_ref[0, :, at] = turn_back(
            grad_query[h * count : (h + 1) * count], cos_ref[...], sin_ref[...]
        ).astype(bf16)


def attend_back_call(shift, query, upstream, cosine, sine, kv, kpos, limit, logs):
    rows, count, width = query.shape
    length = kv.shape[1]
    groups = KVH
    many = limit.shape[2]
    part = pl.BlockSpec((1, count, width), lambda r, g, shift: (r, 0, 0))
    fixed = lambda shape: pl.BlockSpec(shape, lambda r, g, shift: (0, 0))
    keys = pl.BlockSpec((1, length, HD), lambda r, g, shift: (r, 0, g))
    values = pl.BlockSpec((1, length, HD), lambda r, g, shift: (r, 0, KVH + g))
    work = rows * groups * length * many
    return pl.pallas_call(
        attend_back_kernel,
        grid_spec=pltpu.PrefetchScalarGridSpec(
            num_scalar_prefetch=1,
            grid=(rows, groups),
            in_specs=[
                part,
                part,
                fixed((count, HD)),
                fixed((count, HD)),
                keys,
                values,
                fixed((length, 1)),
                pl.BlockSpec((1, 1, many), lambda r, g, shift: (r, 0, 0)),
                pl.BlockSpec((1, 1, 1, many), lambda r, g, shift: (r, g, 0, 0)),
            ],
            out_specs=[
                part,
                pl.BlockSpec((1, length // 2, 2 * KVH * HD), lambda r, g, shift: (r, 0, 0)),
                pl.BlockSpec((1, length // 2, 2 * KVH * HD), lambda r, g, shift: (r, 0, 0)),
            ],
        ),
        out_shape=[
            jax.ShapeDtypeStruct((rows, count, width), bf16),
            jax.ShapeDtypeStruct((rows, length // 2, 2 * KVH * HD), bf16),
            jax.ShapeDtypeStruct((rows, length // 2, 2 * KVH * HD), bf16),
        ],
        cost_estimate=pl.CostEstimate(
            flops=10 * work * HD, bytes_accessed=4 * kv.size, transcendentals=work
        ),
        compiler_params=pltpu.CompilerParams(vmem_limit_bytes=vmem_bytes),
        name="attend_back",
    )(shift, query, upstream, cosine, sine, kv, kv, kpos, limit, logs)


def turn_back_kernel(kv_ref, cos_ref, sin_ref, out_ref):
    half = kv_ref.shape[2] // 2
    for at in range(0, half, HD):
        out_ref[0, :, at : at + HD] = turn_back(
            kv_ref[0, :, at : at + HD].astype(f32), cos_ref[...], sin_ref[...]
        ).astype(bf16)
    out_ref[0, :, half:] = kv_ref[0, :, half:]


def turn_back_call(kv, cosine, sine):
    rows, count, width = kv.shape
    row = pl.BlockSpec((1, count, width), lambda r: (r, 0, 0))
    table = pl.BlockSpec((count, HD), lambda r: (0, 0))
    return pl.pallas_call(
        turn_back_kernel,
        grid=(rows,),
        in_specs=[row, table, table],
        out_specs=row,
        out_shape=jax.ShapeDtypeStruct(kv.shape, bf16),
        cost_estimate=pl.CostEstimate(
            flops=4 * kv.size, bytes_accessed=4 * kv.size, transcendentals=0
        ),
        compiler_params=pltpu.CompilerParams(vmem_limit_bytes=vmem_bytes),
        name="turn_back",
    )(kv, cosine, sine)


def matmul(left, right):
    return jnp.dot(left, right, preferred_element_type=f32)


def matmul_nt(left, right):
    return lax.dot_general(left, right, (((1,), (1,)), ((), ())), preferred_element_type=f32)


def matmul_tn(left, right):
    return lax.dot_general(left, right, (((0,), (0,)), ((), ())), preferred_element_type=f32)


def angles(positions):
    inverse_freq = rope_base ** (-jnp.arange(0, HD // 2, dtype=f32) * 2.0 / HD)
    phase = positions[:, None] * inverse_freq[None, :]
    cosine, sine = jnp.cos(phase), jnp.sin(phase)
    return jnp.concatenate([cosine, cosine], -1), jnp.concatenate([-sine, sine], -1)


def norm_back(upstream, normed, inv_rms, gain_row):
    scaled = upstream * gain_row
    return inv_rms * (scaled - normed * jnp.mean(scaled * normed, axis=-1, keepdims=True))


def rms_scale(values):
    return lax.rsqrt(jnp.mean(values * values, axis=-1, keepdims=True) + epsilon)


def local(
    residual,
    out_grad,
    lengths,
    attn_gain,
    query_weight,
    query_bias,
    key_weight,
    key_bias,
    value_weight,
    value_bias,
    output_weight,
    ffn_gain,
    gate_weight,
    up_weight,
    down_weight,
):
    rows, own, width = residual.shape
    tokens = rows * own
    shard = own * lax.axis_size("heads")
    n_heads = lax.axis_size("heads")
    n_seq = lax.axis_size("seq")
    z = lax.axis_index("heads")
    s = lax.axis_index("seq")
    c = lax.axis_index("dp")
    piece = c * n_seq + s
    order_a, order_b = seq_masks()
    depth = gate_weight.shape[0]
    half = n_seq * depth
    q_own = query_weight.shape[1]
    q_all = q_own * n_heads
    kv_width = key_weight.shape[1]
    group_heads = H // KVH

    start = s * shard + z * own
    positions = start + jnp.arange(own, dtype=jnp.int32)
    cosine, sine = angles(positions.astype(f32))

    lanes = Lanes()
    places = seq_places()
    stages = range(len(places).bit_length() - 1)

    def both_cores(mine):
        other = lanes.core(mine)
        full = jnp.zeros((2 * half, mine.shape[1]), bf16)
        full = lax.dynamic_update_slice_in_dim(full, mine, c * half, 0)
        return by_rows(lax.dynamic_update_slice_in_dim(full, other, (1 - c) * half, 0))

    def halves_grad(left, right):
        terms = [
            order.mark(by_rows(matmul_tn(take(left, at, half, 1), order.then(right)).astype(bf16)))
            for at in (1 - c, c)
        ]
        return [terms[1], lanes.core(terms[0])]

    def row_blocks(parts):
        return [[take(part, place, depth, 0) for part in parts] for place in places]

    units = gate_weight.shape[1]
    spare = -units % 256
    both = ("dp", "seq")
    down_full, gate_full, up_full = (
        lax.all_gather(jnp.pad(part, ((0, 0), (0, spare))), both, axis=0, tiled=True)
        for part in (down_weight.T, gate_weight, up_weight)
    )

    first_input, kv_own = first_call(
        residual, attn_gain, key_weight, value_weight, key_bias, value_bias, cosine, sine
    )
    kv_ring = lanes.gather(kv_own)
    kv_gather = SeqGather(lanes, jnp.concatenate(kv_ring, axis=1), 1)
    for _ in stages:
        kv_gather.step()
    kv_sent = lanes.sent["seq"][-1]
    kv_all = jnp.concatenate(kv_gather.held, axis=1)
    ring_at = (jnp.arange(n_heads, dtype=jnp.int32) + z) % n_heads
    key_pos = (
        jnp.stack(places)[:, None, None] * shard
        + ring_at[None, :, None] * own
        + jnp.arange(own, dtype=jnp.int32)[None, None, :]
    ).reshape(-1, 1)
    limit = jnp.minimum(positions[None, :], lengths[:, None] - 1)
    limit = jnp.tile(limit, (1, group_heads))[:, None, :]

    extra = 16
    query_half = take(query_weight, c, half, 0)
    bias_rows = jnp.pad(query_bias[None], ((0, extra - 1), (0, 0)))
    query_ring = lanes.gather(jnp.concatenate([query_half, bias_rows], axis=0), kv_ring)
    bias_all = jnp.concatenate([part[half : half + 1] for part in query_ring], axis=1).astype(f32)
    query_rest = both_cores(
        jnp.concatenate([part[:half] for part in after(query_ring[1:], kv_sent)], axis=1)
    )
    output_ring = lanes.gather(take(output_weight, c, half, 1).T, query_ring)
    shift = ((H - z * (q_own // HD)) % H).reshape(1)

    input_flat = first_input.reshape(tokens, width)
    query_lin = jnp.concatenate(
        [matmul(input_flat, query_weight), matmul(input_flat, query_rest)], axis=1
    )
    query_lin = (query_lin + bias_all).reshape(rows, own, q_all)
    attended, query_rot, logs = attend_call(
        shift, query_lin, cosine, sine, kv_all, key_pos, limit
    )
    attended = attended.reshape(tokens, q_all)
    output_rest = both_cores(jnp.concatenate(after(output_ring[1:], attended), axis=1))
    stream = residual.astype(f32).reshape(tokens, width)
    second_stream = (
        stream
        + matmul(attended[:, :q_own], output_weight)
        + matmul_nt(attended[:, q_own:], output_rest)
    )
    second_scale = rms_scale(second_stream)
    second_normed = second_stream * second_scale
    second_gain = ffn_gain.astype(f32)
    second_own = (second_normed * second_gain).astype(bf16)

    order = Order()
    order.mark(second_own)
    tokens_ring = gather_ring(lanes, second_own)
    grad_flat = out_grad.reshape(rows, n_heads, own, width).transpose(1, 0, 2, 3)
    grad_flat = grad_flat.reshape(n_heads * tokens, width)
    grad_hidden_all = order.mark(matmul(order.then(grad_flat), down_full))

    def all_tokens(parts):
        full = jnp.zeros((n_heads * tokens, parts[0].shape[1]), bf16)
        for m, part in enumerate(parts):
            full = lax.dynamic_update_slice_in_dim(full, part, (z + m) % n_heads * tokens, 0)
        return by_rows(full)

    hidden_parts, gate_parts, up_parts, back_parts = [], [], [], []
    for m, part in enumerate(tokens_ring):
        part = order.then(part)
        grad_hidden = take(grad_hidden_all, (z + m) % n_heads, tokens, 0)
        gate_act = matmul(part, gate_full)
        up_act = matmul(part, up_full)
        sigmoid_gate = jax.nn.sigmoid(gate_act)
        silu_gate = gate_act * sigmoid_gate
        hidden_parts.append(by_rows((silu_gate * up_act).astype(bf16)))
        gate_parts.append(
            by_rows(
                (
                    grad_hidden * up_act * sigmoid_gate * (1.0 + gate_act * (1.0 - sigmoid_gate))
                ).astype(bf16)
            )
        )
        up_parts.append(by_rows((grad_hidden * silu_gate).astype(bf16)))
        back = matmul_nt(gate_parts[m], gate_full) + matmul_nt(up_parts[m], up_full)
        back_parts.append(order.mark(back.astype(bf16)))
    back_all = order.mark(all_tokens(back_parts))
    second_back = lax.psum_scatter(back_all, "heads", scatter_dimension=0, tiled=True)

    hidden = order.mark(all_tokens(order.then(hidden_parts)))
    down_terms = halves_grad(grad_flat, hidden)
    ffn_part = order.mark(matmul_nt(order.then(hidden), down_full).astype(bf16))
    ffn_own = lax.psum_scatter(
        after(ffn_part, back_all), "heads", scatter_dimension=0, tiled=True
    )
    block_out = (second_stream + ffn_own.astype(f32)).reshape(rows, own, width)
    second_input = order.mark(all_tokens(order.then(tokens_ring)))
    gate_terms = halves_grad(second_input, all_tokens(order.then(gate_parts)))
    down_scatter = SeqScatter(lanes, [row_blocks(order.then(down_terms))], 0).step()
    order.mark(lanes.sent["seq"][-1])
    up_terms = halves_grad(second_input, all_tokens(order.then(up_parts)))
    down_scatter.items = order.then(down_scatter.items)
    down_grad = total_of(down_scatter.terms()[0])[:, :units]
    order.mark(lanes.sent["seq"][-1])
    both_scatter = SeqScatter(
        lanes, order.then([row_blocks(gate_terms), row_blocks(up_terms)]), 0
    ).step()
    order.mark(lanes.sent["seq"][-1])

    second_back = order.then(second_back).astype(f32)
    second_gain_term = jnp.sum(second_back * second_normed, axis=0)
    grad_own = take(out_grad, z, own, 1).reshape(tokens, width).astype(f32)
    grad_stream = grad_own + norm_back(second_back, second_normed, second_scale, second_gain)
    grad_attn = grad_stream.astype(bf16)

    grad_attended = jnp.concatenate(
        [matmul_nt(grad_attn, output_weight), matmul(grad_attn, output_rest)], axis=1
    ).astype(bf16)
    grad_query, kv_low, kv_high = attend_back_call(
        shift,
        query_rot,
        grad_attended.reshape(rows, own, q_all),
        cosine,
        sine,
        kv_all,
        key_pos,
        limit,
        logs,
    )
    order.mark(grad_query)
    grad_query = grad_query.reshape(tokens, q_all)
    gate_sum, up_sum = both_scatter.terms()
    kv_scatter = SeqScatter(
        lanes,
        [[[part] for half_of in (kv_low, kv_high) for part in split(half_of, n_seq // 2, 1)]],
        1,
    ).step(kv_high)
    query_terms = halves_grad(input_flat, grad_query)
    output_terms = halves_grad(grad_attn, attended)
    kv_scatter.items = order.then(kv_scatter.items)
    (kv_terms,) = kv_scatter.terms()
    order.mark(lanes.sent["seq"][-1])
    gate_grad, up_grad = (total_of(order.then(terms))[:, :units] for terms in (gate_sum, up_sum))

    kv_sum = total_of(order.then(kv_terms)).astype(bf16)
    kv_away = order.mark(
        [take(kv_sum, m, own, 1) for m in range(1, n_heads)]
    )
    kv_came = lanes.direct(kv_away, True)

    qo_scatter = SeqScatter(
        lanes, order.then([row_blocks(query_terms), row_blocks(output_terms)]), 0
    ).step()
    order.mark(lanes.sent["seq"][-1])
    first_scale = rms_scale(stream)
    first_normed = stream * first_scale
    first_gain = attn_gain.astype(f32)
    first_back = order.mark(
        matmul_nt(order.then(grad_query[:, :q_own]), query_weight)
        + matmul_nt(order.then(grad_query[:, q_own:]), query_rest)
    )
    grad_kv = turn_back_call(
        total_of([take(kv_sum, 0, own, 1)] + order.then(kv_came)).astype(bf16), cosine, sine
    )
    grad_kv = order.mark(grad_kv.reshape(tokens, 2 * kv_width))

    first_back = (
        first_back
        + matmul_nt(grad_kv[:, :kv_width], key_weight)
        + matmul_nt(grad_kv[:, kv_width:], value_weight)
    )
    first_gain_term = jnp.sum(first_back * first_normed, axis=0)

    small = jnp.concatenate(
        [
            first_gain_term,
            second_gain_term,
            jnp.roll(jnp.sum(grad_query.astype(f32), axis=0), z * q_own),
            jnp.sum(grad_kv.astype(f32), axis=0),
        ]
    )
    kv_cut = kv_width // n_heads
    packed = 2 * kv_width
    lines = -(-small.size // (packed * 16)) * 16
    small = as_sent(jnp.pad(small, (0, lines * packed - small.size)).reshape(lines, packed))

    def with_small(value):
        return jnp.concatenate([value, small.astype(bf16)], axis=0)

    def apart(value):
        return value[:-lines], value[-lines:].astype(f32)

    kv_mine, kv_other = (
        matmul_tn(take(input_flat, at, half, 1), grad_kv).astype(bf16) for at in (c, 1 - c)
    )
    kv_other, came_small = apart(lanes.core(with_small(kv_other)))
    small = as_sent(small + came_small)
    kv_terms = row_blocks([kv_mine, kv_other])
    while len(kv_terms) > 1:
        count = len(kv_terms) // 2
        message = join([low_total(terms) for terms in kv_terms[count:]], 0)
        came, came_small = apart(lanes.seq(with_small(message), count.bit_length() - 1))
        small = as_sent(small + came_small)
        kv_terms = [terms + [came[p * depth : (p + 1) * depth]] for p, terms in enumerate(kv_terms[:count])]
    kv_part = low_total(kv_terms[0])
    low_small = small.astype(bf16).reshape(-1, 2 * kv_cut)
    kv_pieces = [
        jnp.concatenate(
            [
                take(part, (z + m) % n_heads, kv_cut, 1)
                for part in (kv_part[:, :kv_width], kv_part[:, kv_width:])
            ],
            axis=1,
        )
        for m in range(n_heads)
    ]
    came = lanes.direct(
        [jnp.concatenate([part, low_small], axis=0) for part in kv_pieces[1:]], True
    )
    kv_total = total_of([kv_pieces[0]] + [part[:depth] for part in came])
    sums = total_of([low_small] + [part[depth:] for part in came])
    sums = sums.reshape(-1)
    residual_grad = grad_stream + norm_back(first_back, first_normed, first_scale, first_gain)

    query_sum, output_sum = (low_total(terms) for terms in qo_scatter.terms())
    qo_parts = [
        jnp.concatenate(pair, axis=1)
        for pair in zip(split(query_sum, n_heads, 1), split(output_sum, n_heads, 1))
    ]
    qo_grad = total_of(qo_parts[:1] + lanes.direct(qo_parts[1:], True))
    query_weight_grad = qo_grad[:, :q_own]
    output_weight_grad = qo_grad[:, q_own:].T

    gain_piece = width // (lax.axis_size("dp") * n_seq * n_heads)
    gain_at = (piece * n_heads + z) * gain_piece
    attn_gain_grad = lax.dynamic_slice_in_dim(sums, gain_at, gain_piece, 0)
    ffn_gain_grad = lax.dynamic_slice_in_dim(sums, width + gain_at, gain_piece, 0)
    query_bias_grad = lax.dynamic_slice_in_dim(sums, 2 * width + z * q_own, q_own, 0)
    kv_at = 2 * width + q_all + z * kv_cut
    key_bias_grad = lax.dynamic_slice_in_dim(sums, kv_at, kv_cut, 0)
    value_bias_grad = lax.dynamic_slice_in_dim(sums, kv_at + kv_width, kv_cut, 0)

    return (
        block_out.astype(bf16),
        residual_grad.reshape(rows, own, width),
        attn_gain_grad,
        query_weight_grad,
        query_bias_grad,
        kv_total[:, :kv_cut],
        key_bias_grad,
        kv_total[:, kv_cut:],
        value_bias_grad,
        output_weight_grad,
        ffn_gain_grad,
        gate_grad,
        up_grad,
        down_grad.T,
    )


def solution(mesh):
    in_specs = (
        P("dp", ("seq", "heads"), None),
        P("dp", "seq", None),
        P("dp"),
        P(),
        P(None, "heads"),
        P("heads"),
        P(),
        P(),
        P(),
        P(),
        P("heads", None),
        P(),
        P(("dp", "seq"), "heads"),
        P(("dp", "seq"), "heads"),
        P("heads", ("dp", "seq")),
    )
    out_specs = (
        P("dp", ("seq", "heads"), None),
        P("dp", ("seq", "heads"), None),
        P(("dp", "seq", "heads")),
        P(("dp", "seq"), "heads"),
        P("heads"),
        P(("dp", "seq"), "heads"),
        P("heads"),
        P(("dp", "seq"), "heads"),
        P("heads"),
        P("heads", ("dp", "seq")),
        P(("dp", "seq", "heads")),
        P(("dp", "seq"), "heads"),
        P(("dp", "seq"), "heads"),
        P("heads", ("dp", "seq")),
    )
    return jax.shard_map(local, mesh=mesh, in_specs=in_specs, out_specs=out_specs, check_vma=False)
```

time: 847 us -> 643 us (0.76)
  waiting for transfers between devices: 423 us -> 255 us
  starting transfers between devices: 79.8 us -> 36.5 us
  local copies, waits for them, and re-layouts: 77.1 us -> 91.7 us
    ppermute x0 -> x30, waiting for transfers between devices: none -> 220 us  [the longest x12 130 us: seq(): lax.ppermute(v, ('dp', 'seq'), pairs)]
    all_gather x4 -> x3, waiting for transfers between devices: 192 us -> 0.01 us  [local(): lax.all_gather(jnp.pad(part, ((0, 0), (0, spare))), both, axis=0, tiled=T...]
    ppermute x28 -> x8, waiting for transfers between devices: 124 us -> 2.27 us  [swap(): return lax.ppermute(value, axis, pairs)]
    reduce_scatter x4 -> x2, waiting for transfers between devices: 93.9 us -> 0.01 us  [the longest x1 0.01 us: local(): lax.psum_scatter(back_all, 'heads', scatter_dimension=0, tiled=True)]
    ppermute x28 -> x8, starting transfers between devices: 54.9 us -> 5.84 us  [swap(): return lax.ppermute(value, axis, pairs)]
    ppermute x0 -> x30, starting transfers between devices: none -> 29.3 us  [the longest x18 20.4 us: direct(): lax.ppermute(value, 'heads', [(i, (i + m if away else i - m) % size) for...]
    ppermute x15 -> x3, starting transfers between devices: 24.3 us -> 1.21 us  [rotate_down(): return lax.ppermute(value, axis, pairs)]
    ppermute x15 -> x3, waiting for transfers between devices: 11.3 us -> 32.9 us  [rotate_down(): return lax.ppermute(value, axis, pairs)]
  transfers between devices with their start and end apart: 52 -> 46, of which waited for: 27 -> 23; matrix products, arithmetic and copies ran while one was open for 25% -> 39% of each run, Pallas kernels for 3% -> 6%
where the time goes in v2:
time: 643 us; the launch traced here: 633 us
  waiting for transfers between devices  255 us (40%)
  matrix products  153 us (24%)
  local copies, waits for them, and re-layouts  91.7 us (14%)
  other arithmetic  44.2 us (7%)
  starting transfers between devices  36.5 us (6%)
  Pallas kernels  36.3 us (6%)
  between operations  15.8 us (2%)
    ppermute x12, waiting for transfers between devices, seq(): lax.ppermute(v, ('dp', 'seq'), pairs)  130 us
    ppermute x18, waiting for transfers between devices, direct(): lax.ppermute(value, 'heads', [(i, (i + m if away else i - m) % size) for...  89.6 us
    dot_general x13, matrix products, matmul(): return jnp.dot(left, right, preferred_element_type=f32)  67.3 us
    dot_general x12, matrix products, matmul_tn(): lax.dot_general(left, right, (((0,), (0,)), ((), ())), preferred_element_...  44.4 us
    dot_general x15, matrix products, matmul_nt(): lax.dot_general(left, right, (((1,), (1,)), ((), ())), preferred_element_...  41.6 us
    ppermute x3, waiting for transfers between devices, rotate_down(): return lax.ppermute(value, axis, pairs)  32.9 us
    unnamed x222, local copies, waits for them, and re-layouts  29.5 us
    pallas_call x1, Pallas kernels, attend_back_call(): pl.pallas_call(attend_back_kernel, grid_spec=pltpu.PrefetchScalarGridSpec...  21.1 us
  transfers between devices with their start and end apart: 46, of which 23 were waited for; matrix products, arithmetic and copies ran while one was open for 39% of the time, Pallas kernels for 6%

profile of v2, /device:TPU:9, one launch (start us, length us, event | category | flops | bytes accessed | tf_op | source)
XLA Modules:
  0.0 632.8 jit_solution(1752105322278077113)
XLA Ops:
  24.8 12.1 %collective-permute-done.1 = bf16[3,96,512]{2,1,0:T(8,128)(2,1)S(1)} collective-permute-done((bf16[3,96,512]{2,1,0:T(8,128)(2,1)S(1)}, bf16[3,96,512]{2,1,0:T(8,128)(2,1)S(1)}, u32[]{:S(2)}, u32[]{:S(2)}) %collective-permute-start.1) | collective-permute-done | bytes 294944 | tf_op jit(solution)/shard_map/ppermute | solution.py:68
  37.9 5.3 collective-permute-done.2
  52.6 19.1 %collective-permute-done.6 = bf16[3,384,512]{2,1,0:T(8,128)(2,1)} collective-permute-done((bf16[3,384,512]{2,1,0:T(8,128)(2,1)}, bf16[3,384,512]{2,1,0:T(8,128)(2,1)}, u32[]{:S(2)}, u32[]{:S(2)}) %collective-permute-start.6) | collective-permute-done | bytes 1179680 | tf_op jit(solution)/shard_map/ppermute | solution.py:58
  74.6 12.6 %collective-permute-done.4 = bf16[784,384]{1,0:T(8,128)(2,1)} collective-permute-done((bf16[784,384]{1,0:T(8,128)(2,1)S(1)}, bf16[784,384]{1,0:T(8,128)(2,1)}, u32[]{:S(2)}, u32[]{:S(2)}) %collective-permute-start.4) | collective-permute-done | bytes 602144 | tf_op jit(solution)/shard_map/ppermute | solution.py:68
  87.2 12.9 %collective-permute-done.5 = bf16[784,384]{1,0:T(8,128)(2,1)} collective-permute-done((bf16[784,384]{1,0:T(8,128)(2,1)S(1)}, bf16[784,384]{1,0:T(8,128)(2,1)}, u32[]{:S(2)}, u32[]{:S(2)}) %collective-permute-start.5) | collective-permute-done | bytes 602144 | tf_op jit(solution)/shard_map/ppermute | solution.py:68
  113.3 4.3 collective-permute-start.11
  126.1 20.1 %collective-permute-done.8 = bf16[3,768,512]{2,1,0:T(8,128)(2,1)} collective-permute-done((bf16[3,768,512]{2,1,0:T(8,128)(2,1)}, bf16[3,768,512]{2,1,0:T(8,128)(2,1)}, u32[]{:S(2)}, u32[]{:S(2)}) %collective-permute-start.8) | collective-permute-done | bytes 2359328 | tf_op jit(solution)/shard_map/ppermute | solution.py:58
  149.5 13.0 %attend.1 = (bf16[3,96,1536]{2,1,0:T(8,128)(2,1)S(1)}, bf16[3,96,1536]{2,1,0:T(8,128)(2,1)S(1)}, f32[3,2,1,576]{3,2,1,0:T(1,128)S(1)}) custom-call(s32[1]{0:T(128)} %bitcast.1.shift_ref, f32[3,96,1536]{2,1,0:T(8,128)S(1)} %maximum_add_fusion.q_ref, f32[96,128]{1,0:T(8,128)S(1)} %pad_maximum_fusion.16.cos_ref, f32[96,128]{1,0:T(8,128)S(1)} %pad_maximum_fusion.17.sin_ref, ...), custom_call_target="tpu_custom_call" | custom-call | flops 2717908992 | bytes 4718592 | tf_op jit(solution)/shard_map/attend/pallas_call | solution.py:308
  177.5 20.9 %collective-permute-done.13 = bf16[288,1536]{1,0:T(8,128)(2,1)} collective-permute-done((bf16[288,1536]{1,0:T(8,128)(2,1)S(1)}, bf16[288,1536]{1,0:T(8,128)(2,1)}, u32[]{:S(2)}, u32[]{:S(2)}) %collective-permute-start.13) | collective-permute-done | bytes 884768 | tf_op jit(solution)/shard_map/ppermute | solution.py:35
  199.8 4.0 copy.39
  207.4 12.0 %collective-permute-done.14 = bf16[288,1536]{1,0:T(8,128)(2,1)} collective-permute-done((bf16[288,1536]{1,0:T(8,128)(2,1)}, bf16[288,1536]{1,0:T(8,128)(2,1)}, u32[]{:S(2)}, u32[]{:S(2)}) %collective-permute-start.14) | collective-permute-done | bytes 884768 | tf_op jit(solution)/shard_map/ppermute | solution.py:35
  219.9 14.5 %fusion.70 = f32[1152,2304]{1,0:T(8,128)} fusion(bf16[1152,1536]{1,0:T(8,128)(2,1)} %bitcast.125, bf16[1536,2304]{1,0:T(8,128)(2,1)} %all-gather.4.cloned.1.call-done), kind=kOutput, calls=%fused_computation.290 | convolution fusion | flops 8153726976 | bytes 21233664 | tf_op jit(solution)/shard_map/dot_general | solution.py:461
  234.5 6.7 %fusion.71 = f32[288,2304]{1,0:T(8,128)} fusion(bf16[288,1536]{1,0:T(8,128)(2,1)S(1)} %copy-done.29, bf16[1536,2304]{1,0:T(8,128)(2,1)} %all-gather.8.cloned.1.call-done), kind=kOutput, calls=%fused_computation.291 | convolution fusion | flops 2038431744 | bytes 10616832 | tf_op jit(solution)/shard_map/dot_general | solution.py:461
  241.2 8.9 %multiply_convert_fusion.9 = (bf16[288,2304]{1,0:T(8,128)(2,1)S(1)}, bf16[288,2304]{1,0:T(8,128)(2,1)S(1)}, bf16[288,2304]{1,0:T(8,128)(2,1)}) fusion(f32[1152,2304]{1,0:T(8,128)} %fusion.70, s32[]{:T(128)S(6)} %select_n.261, f32[288,2304]{1,0:T(8,128)} %fusion.71, bf16[288,1536]{1,0:T(8,128)(2,1)S(1)} %copy-done.29, ...), kind=kOutput, calls=%fused_computation.38 | convolution fusion | flops 2048385024 | bytes 17252356 | tf_op jit(solution)/shard_map/dot_general | solution.py:461
  261.8 6.4 %multiply_convert_fusion.6 = (bf16[288,2304]{1,0:T(8,128)(2,1)S(1)}, bf16[288,2304]{1,0:T(8,128)(2,1)S(1)}, bf16[288,2304]{1,0:T(8,128)(2,1)}) fusion(f32[1152,2304]{1,0:T(8,128)} %fusion.70, s32[]{:T(128)S(6)} %select_n.263, f32[288,2304]{1,0:T(8,128)S(1)} %fusion.73, bf16[288,1536]{1,0:T(8,128)(2,1)} %collective-permute-done.13, ...), kind=kOutput, calls=%fused_computation.33 | convolution fusion | flops 2048385024 | bytes 17252356 | tf_op jit(solution)/shard_map/dot_general | solution.py:461
  277.3 6.4 %multiply_convert_fusion.3 = (bf16[288,2304]{1,0:T(8,128)(2,1)S(1)}, bf16[288,2304]{1,0:T(8,128)(2,1)S(1)}, bf16[288,2304]{1,0:T(8,128)(2,1)}) fusion(f32[1152,2304]{1,0:T(8,128)} %fusion.70, s32[]{:T(128)S(6)} %select_n.265, f32[288,2304]{1,0:T(8,128)S(1)} %fusion.75, bf16[288,1536]{1,0:T(8,128)(2,1)} %collective-permute-done.14, ...), kind=kOutput, calls=%fused_computation.28 | convolution fusion | flops 2048385024 | bytes 17252356 | tf_op jit(solution)/shard_map/dot_general | solution.py:461
  292.6 6.8 %multiply_convert_fusion = (bf16[288,2304]{1,0:T(8,128)(2,1)S(1)}, bf16[288,2304]{1,0:T(8,128)(2,1)S(1)}, bf16[288,2304]{1,0:T(8,128)(2,1)}) fusion(f32[1152,2304]{1,0:T(8,128)} %fusion.70, s32[]{:T(128)S(6)} %select_n.267, f32[288,2304]{1,0:T(8,128)S(1)} %fusion.77, bf16[288,1536]{1,0:T(8,128)(2,1)} %collective-permute-done.15, ...), kind=kOutput, calls=%fused_computation.23 | convolution fusion | flops 2048385024 | bytes 17252356 | tf_op jit(solution)/shard_map/dot_general | solution.py:461
  310.1 6.4 %convolution_convert_fusion.6 = bf16[768,2304]{1,0:T(8,128)(2,1)} fusion(bf16[1152,2304]{1,0:T(8,128)(2,1)S(1)} %constant_dynamic-update-slice_fusion.30, bf16[1152,1536]{1,0:T(8,128)(2,1)S(1)} %bitcast.126, s32[]{:T(128)S(6)} %select_n.256), kind=kOutput, calls=%fused_computation.6 | convolution fusion | flops 4078632960 | bytes 10616836 | tf_op jit(solution)/shard_map/dot_general | solution.py:469
  318.8 6.3 convolution_convert_fusion.5
  325.1 10.0 %convolution_convert_fusion = bf16[1152,1536]{1,0:T(8,128)(2,1)} fusion(bf16[1152,2304]{1,0:T(8,128)(2,1)S(1)} %constant_dynamic-update-slice_fusion.30, bf16[1536,2304]{1,0:T(8,128)(2,1)S(1)} %bitcast.134), kind=kOutput, calls=%fused_computation | convolution fusion | flops 8155496448 | bytes 15925248 | tf_op jit(solution)/shard_map/dot_general | solution.py:465
  344.5 6.5 %convolution_convert_fusion.4 = bf16[768,2304]{1,0:T(8,128)(2,1)} fusion(bf16[1152,2304]{1,0:T(8,128)(2,1)S(1)} %constant_dynamic-update-slice_fusion.22, bf16[1152,1536]{1,0:T(8,128)(2,1)S(1)} %constant_dynamic-update-slice_fusion.26, s32[]{:T(128)S(6)} %select_n.256), kind=kOutput, calls=%fused_computation.4 | convolution fusion | flops 4078632960 | bytes 10616836 | tf_op jit(solution)/shard_map/dot_general | solution.py:469
  351.2 7.9 %convolution_convert_fusion.3 = bf16[768,2304]{1,0:T(8,128)(2,1)S(1)} fusion(bf16[1152,2304]{1,0:T(8,128)(2,1)} %copy-done.25, bf16[1152,1536]{1,0:T(8,128)(2,1)} %copy-done.30, s32[]{:T(128)S(6)} %select_n.255), kind=kOutput, calls=%fused_computation.3 | convolution fusion | flops 4078632960 | bytes 10616836 | tf_op jit(solution)/shard_map/dot_general | solution.py:469
  369.0 5.1 convolution_convert_fusion.2
  378.1 5.3 convolution_convert_fusion.1
  402.9 21.1 %attend_back.1 = (bf16[3,96,1536]{2,1,0:T(8,128)(2,1)S(1)}, bf16[3,768,512]{2,1,0:T(8,128)(2,1)S(1)}, bf16[3,768,512]{2,1,0:T(8,128)(2,1)}) custom-call(s32[1]{0:T(128)} %bitcast.1.shift_ref, bf16[3,96,1536]{2,1,0:T(8,128)(2,1)S(1)} %copy-done.19, bf16[3,96,1536]{2,1,0:T(8,128)(2,1)S(1)} %pad_maximum_fusion.6.og_ref, f32[96,128]{1,0:T(8,128)S(1)} %copy-done.11, ...), custom_call_target="tpu_custom_call" | custom-call | flops 6794772480 | bytes 9437184 | tf_op jit(solution)/shard_map/attend_back/pallas_call | solution.py:398
  429.1 12.3 %collective-permute-done.22 = bf16[768,2304]{1,0:T(8,128)(2,1)} collective-permute-done((bf16[768,2304]{1,0:T(8,128)(2,1)}, bf16[768,2304]{1,0:T(8,128)(2,1)}, u32[]{:S(2)}, u32[]{:S(2)}) %collective-permute-start.22) | collective-permute-done | bytes 3538976 | tf_op jit(solution)/shard_map/ppermute | solution.py:58
  456.0 33.0 %collective-permute-done.24 = bf16[3,768,512]{2,1,0:T(8,128)(2,1)S(1)} collective-permute-done((bf16[3,768,512]{2,1,0:T(8,128)(2,1)S(1)}, bf16[3,768,512]{2,1,0:T(8,128)(2,1)S(1)}, u32[]{:S(2)}, u32[]{:S(2)}) %collective-permute-start.24) | collective-permute-done | bytes 2359328 | tf_op jit(solution)/shard_map/ppermute | solution.py:58
  496.0 10.4 %collective-permute-done.26 = bf16[3,384,512]{2,1,0:T(8,128)(2,1)S(1)} collective-permute-done((bf16[3,384,512]{2,1,0:T(8,128)(2,1)S(1)}, bf16[3,384,512]{2,1,0:T(8,128)(2,1)S(1)}, u32[]{:S(2)}, u32[]{:S(2)}) %collective-permute-start.26) | collective-permute-done | bytes 1179680 | tf_op jit(solution)/shard_map/ppermute | solution.py:58
  517.3 14.5 %collective-permute-done.28 = bf16[3,96,512]{2,1,0:T(8,128)(2,1)S(1)} collective-permute-done((bf16[3,96,512]{2,1,0:T(8,128)(2,1)S(1)}, bf16[3,96,512]{2,1,0:T(8,128)(2,1)S(1)}, u32[]{:S(2)}, u32[]{:S(2)}) %collective-permute-start.28) | collective-permute-done | bytes 294944 | tf_op jit(solution)/shard_map/ppermute | solution.py:68
  549.5 28.3 %collective-permute-done.31 = bf16[400,512]{1,0:T(8,128)(2,1)S(1)} collective-permute-done((bf16[400,512]{1,0:T(8,128)(2,1)S(1)}, bf16[400,512]{1,0:T(8,128)(2,1)S(1)}, u32[]{:S(2)}, u32[]{:S(2)}) %collective-permute-start.31) | collective-permute-done | bytes 409632 | tf_op jit(solution)/shard_map/ppermute | solution.py:58
  587.3 5.1 multiply_add_fusion
  604.3 16.9 %collective-permute-done.39 = bf16[192,768]{1,0:T(8,128)(2,1)S(1)} collective-permute-done((bf16[192,768]{1,0:T(8,128)(2,1)S(1)}, bf16[192,768]{1,0:T(8,128)(2,1)S(1)}, u32[]{:S(2)}, u32[]{:S(2)}) %collective-permute-start.39) | collective-permute-done | bytes 294944 | tf_op jit(solution)/shard_map/ppermute | solution.py:68
  (484 shorter events, 241.6 us)
Async XLA Ops:
  7.2 212.8 %all-gather.4.cloned.1.call-start = ((), (), s32[]{:S(2)}) async-start(), calls=%async_computation.2 | async-start | bytes 7962624 | tf_op jit(solution)/shard_map/all_gather | solution.py:550
  9.5 224.9 %all-gather.8.cloned.1.call-start = ((), (), s32[]{:S(2)}) async-start(), calls=%async_computation.4 | async-start | bytes 7962624 | tf_op jit(solution)/shard_map/all_gather | solution.py:550
  11.9 229.4 %all-gather.6.cloned.1.call-start = ((), (), s32[]{:S(2)}) async-start(), calls=%async_computation.3 | async-start | bytes 7962624 | tf_op jit(solution)/shard_map/all_gather | solution.py:550
  15.9 21.1 %collective-permute-start.1 = (bf16[3,96,512]{2,1,0:T(8,128)(2,1)S(1)}, bf16[3,96,512]{2,1,0:T(8,128)(2,1)S(1)}, u32[]{:S(2)}, u32[]{:S(2)}) collective-permute-start(bf16[3,96,512]{2,1,0:T(8,128)(2,1)S(1)} %get-tuple-element.149), channel_id=1, source_target_pairs={{0,2},{1,3},{2,0},{3,1},{4,6},{5,7},{6,4},{7,5},{8,10},{9,11},{10,... | collective-permute-start | bytes 884744 | tf_op jit(solution)/shard_map/ppermute | solution.py:68
  18.3 24.9 %collective-permute-start.2 = (bf16[3,96,512]{2,1,0:T(8,128)(2,1)S(1)}, bf16[3,96,512]{2,1,0:T(8,128)(2,1)S(1)}, u32[]{:S(2)}, u32[]{:S(2)}) collective-permute-start(bf16[3,96,512]{2,1,0:T(8,128)(2,1)S(1)} %get-tuple-element.149), channel_id=1, source_target_pairs={{0,1},{1,2},{2,3},{3,0},{4,5},{5,6},{6,7},{7,4},{8,9},{9,10},{10,1... | collective-permute-start | bytes 884744 | tf_op jit(solution)/shard_map/ppermute | solution.py:68
  44.3 27.4 %collective-permute-start.6 = (bf16[3,384,512]{2,1,0:T(8,128)(2,1)}, bf16[3,384,512]{2,1,0:T(8,128)(2,1)}, u32[]{:S(2)}, u32[]{:S(2)}) collective-permute-start(bf16[3,384,512]{2,1,0:T(8,128)(2,1)} %get-tuple-element.417), channel_id=1, source_target_pairs={{0,4},{4,0},{8,12},{12,8},{16,24},{20,28},{24,16},{28,20},{1,5},{5... | collective-permute-start | bytes 3538952 | tf_op jit(solution)/shard_map/ppermute | solution.py:58
  46.7 27.9 %collective-permute-start.3 = (bf16[784,384]{1,0:T(8,128)(2,1)S(1)}, bf16[784,384]{1,0:T(8,128)(2,1)S(1)}, u32[]{:S(2)}, u32[]{:S(2)}) collective-permute-start(bf16[784,384]{1,0:T(8,128)(2,1)S(1)} %fusion.27), channel_id=1, source_target_pairs={{0,3},{1,0},{2,1},{3,2},{4,7},{5,4},{6,5},{7,6},{8,11},{9,8},{10,9... | collective-permute-start | bytes 1806344 | tf_op jit(solution)/shard_map/ppermute | solution.py:68
  48.3 38.9 %collective-permute-start.4 = (bf16[784,384]{1,0:T(8,128)(2,1)S(1)}, bf16[784,384]{1,0:T(8,128)(2,1)}, u32[]{:S(2)}, u32[]{:S(2)}) collective-permute-start(bf16[784,384]{1,0:T(8,128)(2,1)S(1)} %fusion.27), channel_id=1, source_target_pairs={{0,2},{1,3},{2,0},{3,1},{4,6},{5,7},{6,4},{7,5},{8,10},{9,11},{10,... | collective-permute-start | bytes 1806344 | tf_op jit(solution)/shard_map/ppermute | solution.py:68
  50.3 49.9 %collective-permute-start.5 = (bf16[784,384]{1,0:T(8,128)(2,1)S(1)}, bf16[784,384]{1,0:T(8,128)(2,1)}, u32[]{:S(2)}, u32[]{:S(2)}) collective-permute-start(bf16[784,384]{1,0:T(8,128)(2,1)S(1)} %fusion.27), channel_id=1, source_target_pairs={{0,1},{1,2},{2,3},{3,0},{4,5},{5,6},{6,7},{7,4},{8,9},{9,10},{10,1... | collective-permute-start | bytes 1806344 | tf_op jit(solution)/shard_map/ppermute | solution.py:68
  52.5 343.4 %reduce-scatter.5.cloned.1.call-start = ((), (), s32[]{:S(2)}) async-start(), calls=%async_computation.6 | async-start | bytes 4423680 | tf_op jit(solution)/shard_map/reduce_scatter | solution.py:637
  107.2 39.0 %collective-permute-start.8 = (bf16[3,768,512]{2,1,0:T(8,128)(2,1)}, bf16[3,768,512]{2,1,0:T(8,128)(2,1)}, u32[]{:S(2)}, u32[]{:S(2)}) collective-permute-start(bf16[3,768,512]{2,1,0:T(8,128)(2,1)} %get-tuple-element.153), channel_id=1, source_target_pairs={{0,8},{4,12},{8,0},{12,4},{16,20},{20,16},{24,28},{28,24},{1,9},{5... | collective-permute-start | bytes 7077896 | tf_op jit(solution)/shard_map/ppermute | solution.py:58
  113.3 49.3 %collective-permute-start.10 = (bf16[768,384]{1,0:T(8,128)(2,1)}, bf16[768,384]{1,0:T(8,128)(2,1)S(1)}, u32[]{:S(2)}, u32[]{:S(2)}) collective-permute-start(bf16[768,384]{1,0:T(8,128)(2,1)} %bitcast.9), channel_id=1, source_target_pairs={{0,2},{1,3},{2,0},{3,1},{4,6},{5,7},{6,4},{7,5},{8,10},{9,11},{10,... | collective-permute-start | bytes 1769480 | tf_op jit(solution)/shard_map/ppermute | solution.py:68
  113.3 50.9 %collective-permute-start.11 = (bf16[768,384]{1,0:T(8,128)(2,1)}, bf16[768,384]{1,0:T(8,128)(2,1)S(1)}, u32[]{:S(2)}, u32[]{:S(2)}) collective-permute-start(bf16[768,384]{1,0:T(8,128)(2,1)} %bitcast.9), channel_id=1, source_target_pairs={{0,1},{1,2},{2,3},{3,0},{4,5},{5,6},{6,7},{7,4},{8,9},{9,10},{10,1... | collective-permute-start | bytes 1769480 | tf_op jit(solution)/shard_map/ppermute | solution.py:68
  117.6 50.0 %collective-permute-start.9 = (bf16[768,384]{1,0:T(8,128)(2,1)}, bf16[768,384]{1,0:T(8,128)(2,1)S(1)}, u32[]{:S(2)}, u32[]{:S(2)}) collective-permute-start(bf16[768,384]{1,0:T(8,128)(2,1)} %bitcast.9), channel_id=1, source_target_pairs={{0,3},{1,0},{2,1},{3,2},{4,7},{5,4},{6,5},{7,6},{8,11},{9,8},{10,9... | collective-permute-start | bytes 1769480 | tf_op jit(solution)/shard_map/ppermute | solution.py:68
  177.3 21.2 %collective-permute-start.13 = (bf16[288,1536]{1,0:T(8,128)(2,1)S(1)}, bf16[288,1536]{1,0:T(8,128)(2,1)}, u32[]{:S(2)}, u32[]{:S(2)}) collective-permute-start(bf16[288,1536]{1,0:T(8,128)(2,1)S(1)} %multiply_convert_fusion.12), channel_id=1, source_target_pairs={{0,3},{1,0},{2,1},{3,2},{4,7},{5,4},{6,5},{7,6},{8,11},{9,8},{10,9... | collective-permute-start | bytes 2654216 | tf_op jit(solution)/shard_map/ppermute | solution.py:35
  219.4 69.8 %collective-permute-start.15 = (bf16[288,1536]{1,0:T(8,128)(2,1)}, bf16[288,1536]{1,0:T(8,128)(2,1)}, u32[]{:S(2)}, u32[]{:S(2)}) collective-permute-start(bf16[288,1536]{1,0:T(8,128)(2,1)} %collective-permute-done.14), channel_id=1, source_target_pairs={{0,3},{1,0},{2,1},{3,2},{4,7},{5,4},{6,5},{7,6},{8,11},{9,8},{10,9... | collective-permute-start | bytes 2654216 | tf_op jit(solution)/shard_map/ppermute | solution.py:35
  304.9 282.3 %reduce-scatter.3.cloned.1.call-start = ((), (), s32[]{:S(2)}) async-start(), calls=%async_computation.5 | async-start | bytes 4423680 | tf_op jit(solution)/shard_map/reduce_scatter | solution.py:642
  316.5 44.0 %collective-permute-start.17 = (bf16[768,2304]{1,0:T(8,128)(2,1)}, bf16[768,2304]{1,0:T(8,128)(2,1)}, u32[]{:S(2)}, u32[]{:S(2)}) collective-permute-start(bf16[768,2304]{1,0:T(8,128)(2,1)} %convolution_convert_fusion.6), channel_id=1, source_target_pairs={{0,16},{16,0},{1,17},{17,1},{2,18},{18,2},{3,19},{19,3},{4,20},{20... | collective-permute-start | bytes 10616840 | tf_op jit(solution)/shard_map/ppermute | solution.py:29
  351.0 33.8 %collective-permute-start.16 = (bf16[768,2304]{1,0:T(8,128)(2,1)}, bf16[768,2304]{1,0:T(8,128)(2,1)}, u32[]{:S(2)}, u32[]{:S(2)}) collective-permute-start(bf16[768,2304]{1,0:T(8,128)(2,1)} %convolution_convert_fusion.4), channel_id=1, source_target_pairs={{0,16},{16,0},{1,17},{17,1},{2,18},{18,2},{3,19},{19,3},{4,20},{20... | collective-permute-start | bytes 10616840 | tf_op jit(solution)/shard_map/ppermute | solution.py:29
  363.8 24.5 %collective-permute-start.19 = (bf16[384,2304]{1,0:T(8,128)(2,1)S(1)}, bf16[384,2304]{1,0:T(8,128)(2,1)S(1)}, u32[]{:S(2)}, u32[]{:S(2)}) collective-permute-start(bf16[384,2304]{1,0:T(8,128)(2,1)S(1)} %pad_maximum_fusion.3), channel_id=1, source_target_pairs={{0,8},{4,12},{8,0},{12,4},{16,20},{20,16},{24,28},{28,24},{1,9},{5... | collective-permute-start | bytes 5308424 | tf_op jit(solution)/shard_map/ppermute | solution.py:58
  390.7 53.1 %collective-permute-start.23 = (bf16[192,2304]{1,0:T(8,128)(2,1)}, bf16[192,2304]{1,0:T(8,128)(2,1)}, u32[]{:S(2)}, u32[]{:S(2)}) collective-permute-start(bf16[192,2304]{1,0:T(8,128)(2,1)} %add_convert_fusion.8), channel_id=1, source_target_pairs={{0,4},{4,0},{8,12},{12,8},{16,24},{20,28},{24,16},{28,20},{1,5},{5... | collective-permute-start | bytes 2654216 | tf_op jit(solution)/shard_map/ppermute | solution.py:58
  395.9 45.5 %collective-permute-start.22 = (bf16[768,2304]{1,0:T(8,128)(2,1)}, bf16[768,2304]{1,0:T(8,128)(2,1)}, u32[]{:S(2)}, u32[]{:S(2)}) collective-permute-start(bf16[768,2304]{1,0:T(8,128)(2,1)} %pad_maximum_fusion), channel_id=1, source_target_pairs={{0,8},{4,12},{8,0},{12,4},{16,20},{20,16},{24,28},{28,24},{1,9},{5... | collective-permute-start | bytes 10616840 | tf_op jit(solution)/shard_map/ppermute | solution.py:58
  427.0 27.8 %collective-permute-start.20 = (bf16[768,1536]{1,0:T(8,128)(2,1)S(1)}, bf16[768,1536]{1,0:T(8,128)(2,1)S(1)}, u32[]{:S(2)}, u32[]{:S(2)}) collective-permute-start(bf16[768,1536]{1,0:T(8,128)(2,1)S(1)} %convolution_convert_fusion.10), channel_id=1, source_target_pairs={{0,16},{16,0},{1,17},{17,1},{2,18},{18,2},{3,19},{19,3},{4,20},{20... | collective-permute-start | bytes 7077896 | tf_op jit(solution)/shard_map/ppermute | solution.py:29
  428.8 24.8 %collective-permute-start.21 = (bf16[768,1536]{1,0:T(8,128)(2,1)S(1)}, bf16[768,1536]{1,0:T(8,128)(2,1)S(1)}, u32[]{:S(2)}, u32[]{:S(2)}) collective-permute-start(bf16[768,1536]{1,0:T(8,128)(2,1)S(1)} %convolution_convert_fusion.8), channel_id=1, source_target_pairs={{0,16},{16,0},{1,17},{17,1},{2,18},{18,2},{3,19},{19,3},{4,20},{20... | collective-permute-start | bytes 7077896 | tf_op jit(solution)/shard_map/ppermute | solution.py:29
  443.8 45.2 %collective-permute-start.24 = (bf16[3,768,512]{2,1,0:T(8,128)(2,1)S(1)}, bf16[3,768,512]{2,1,0:T(8,128)(2,1)S(1)}, u32[]{:S(2)}, u32[]{:S(2)}) collective-permute-start(bf16[3,768,512]{2,1,0:T(8,128)(2,1)S(1)} %copy-done.100), channel_id=1, source_target_pairs={{0,8},{4,12},{8,0},{12,4},{16,20},{20,16},{24,28},{28,24},{1,9},{5... | collective-permute-start | bytes 7077896 | tf_op jit(solution)/shard_map/ppermute | solution.py:58
  451.3 39.9 %collective-permute-start.25 = (bf16[384,2304]{1,0:T(8,128)(2,1)S(1)}, bf16[384,2304]{1,0:T(8,128)(2,1)S(1)}, u32[]{:S(2)}, u32[]{:S(2)}) collective-permute-start(bf16[384,2304]{1,0:T(8,128)(2,1)S(1)} %pad_maximum_fusion.4), channel_id=1, source_target_pairs={{0,4},{4,0},{8,12},{12,8},{16,24},{20,28},{24,16},{28,20},{1,5},{5... | collective-permute-start | bytes 5308424 | tf_op jit(solution)/shard_map/ppermute | solution.py:58
  508.2 23.6 %collective-permute-start.28 = (bf16[3,96,512]{2,1,0:T(8,128)(2,1)S(1)}, bf16[3,96,512]{2,1,0:T(8,128)(2,1)S(1)}, u32[]{:S(2)}, u32[]{:S(2)}) collective-permute-start(bf16[3,96,512]{2,1,0:T(8,128)(2,1)S(1)} %get-tuple-element.401), channel_id=1, source_target_pairs={{0,2},{1,3},{2,0},{3,1},{4,6},{5,7},{6,4},{7,5},{8,10},{9,11},{10,... | collective-permute-start | bytes 884744 | tf_op jit(solution)/shard_map/ppermute | solution.py:68
  511.0 24.8 %collective-permute-start.29 = (bf16[3,96,512]{2,1,0:T(8,128)(2,1)S(1)}, bf16[3,96,512]{2,1,0:T(8,128)(2,1)S(1)}, u32[]{:S(2)}, u32[]{:S(2)}) collective-permute-start(bf16[3,96,512]{2,1,0:T(8,128)(2,1)S(1)} %get-tuple-element.400), channel_id=1, source_target_pairs={{0,3},{1,0},{2,1},{3,2},{4,7},{5,4},{6,5},{7,6},{8,11},{9,8},{10,9... | collective-permute-start | bytes 884744 | tf_op jit(solution)/shard_map/ppermute | solution.py:68
  545.3 32.6 %collective-permute-start.32 = (bf16[768,1536]{1,0:T(8,128)(2,1)S(1)}, bf16[768,1536]{1,0:T(8,128)(2,1)S(1)}, u32[]{:S(2)}, u32[]{:S(2)}) collective-permute-start(bf16[768,1536]{1,0:T(8,128)(2,1)S(1)} %copy-done.57), channel_id=1, source_target_pairs={{0,8},{4,12},{8,0},{12,4},{16,20},{20,16},{24,28},{28,24},{1,9},{5... | collective-permute-start | bytes 7077896 | tf_op jit(solution)/shard_map/ppermute | solution.py:58
  546.7 31.0 %collective-permute-start.31 = (bf16[400,512]{1,0:T(8,128)(2,1)S(1)}, bf16[400,512]{1,0:T(8,128)(2,1)S(1)}, u32[]{:S(2)}, u32[]{:S(2)}) collective-permute-start(bf16[400,512]{1,0:T(8,128)(2,1)S(1)} %pad_maximum_fusion.8), channel_id=1, source_target_pairs={{0,8},{4,12},{8,0},{12,4},{16,20},{20,16},{24,28},{28,24},{1,9},{5... | collective-permute-start | bytes 1228808 | tf_op jit(solution)/shard_map/ppermute | solution.py:58
  598.3 22.9 %collective-permute-start.39 = (bf16[192,768]{1,0:T(8,128)(2,1)S(1)}, bf16[192,768]{1,0:T(8,128)(2,1)S(1)}, u32[]{:S(2)}, u32[]{:S(2)}) collective-permute-start(bf16[192,768]{1,0:T(8,128)(2,1)S(1)} %pad_maximum_fusion.10), channel_id=1, source_target_pairs={{0,2},{1,3},{2,0},{3,1},{4,6},{5,7},{6,4},{7,5},{8,10},{9,11},{10,... | collective-permute-start | bytes 884744 | tf_op jit(solution)/shard_map/ppermute | solution.py:68
  598.8 26.3 %collective-permute-start.40 = (bf16[192,768]{1,0:T(8,128)(2,1)S(1)}, bf16[192,768]{1,0:T(8,128)(2,1)S(1)}, u32[]{:S(2)}, u32[]{:S(2)}) collective-permute-start(bf16[192,768]{1,0:T(8,128)(2,1)S(1)} %pad_maximum_fusion.11), channel_id=1, source_target_pairs={{0,3},{1,0},{2,1},{3,2},{4,7},{5,4},{6,5},{7,6},{8,11},{9,8},{10,9... | collective-permute-start | bytes 884744 | tf_op jit(solution)/shard_map/ppermute | solution.py:68
  (120 other events, 1348.2 us)
Sparse Core Ops, SparseCore 0:
  10.5 56.3 all-gather.3
  68.8 54.7 all-gather.7
  125.5 55.7 all-gather.5
  305.1 65.5 reduce-scatter.4
  372.8 66.6 reduce-scatter.2

commit v3 on v2

--- a/solution.py
+++ b/solution.py
@@ -22,6 +22,10 @@
 
 def after(value, earlier):
     return lax.optimization_barrier((value, earlier))[0]
+
+
+def tie(*values):
+    return lax.optimization_barrier(values)
 
 
 def swap(value, axis, mask):
@@ -149,41 +153,31 @@
 
 
 class SeqScatter:
-    def __init__(self, lanes, items, dim):
-        self.lanes, self.items, self.dim = lanes, items, dim
+    def __init__(self, lanes, items, count, dim):
+        self.lanes, self.items, self.count, self.dim = lanes, items, count, dim
+        self.came = []
+
+    def at(self, i, p):
+        return self.items[i](p) + [came[i][p] for came in self.came]
 
     def step(self, message=None):
-        half = len(self.items[0]) // 2
+        half = self.count // 2
+        each = range(len(self.items))
         if message is None:
             message = join(
-                [low_total(terms) for held in self.items for terms in held[half:]], self.dim
+                [low_total(self.at(i, p)) for i in each for p in range(half, self.count)],
+                self.dim,
             )
         came = self.lanes.seq(message, half.bit_length() - 1)
         parts = split(came, half * len(self.items), self.dim)
-        self.items = [
-            [terms + [parts[i * half + p]] for p, terms in enumerate(held[:half])]
-            for i, held in enumerate(self.items)
-        ]
+        self.came.append([parts[i * half : (i + 1) * half] for i in each])
+        self.count = half
         return self
 
     def terms(self):
-        while len(self.items[0]) > 1:
+        while self.count > 1:
             self.step()
-        return [held[0] for held in self.items]
-
-
-def gather_ring(lanes, block):
-    held = [block]
-    for _ in range(lax.axis_size("heads") - 1):
-        held.append(lanes.ring(held[-1]))
-    return held
-
-
-def scatter_ring(lanes, blocks):
-    terms = blocks[1]
-    for block in blocks[2:] + blocks[:1]:
-        terms = [lanes.ring(low_total(terms))] + block
-    return terms
+        return [self.at(i, 0) for i in range(len(self.items))]
 
 
 def by_rows(value):
@@ -540,8 +534,12 @@
         ]
         return [terms[1], lanes.core(terms[0])]
 
-    def row_blocks(parts):
-        return [[take(part, place, depth, 0) for part in parts] for place in places]
+    def row_scatter(*arrays):
+        items = [
+            (lambda p, parts=parts: [take(part, places[p], depth, 0) for part in parts])
+            for parts in arrays
+        ]
+        return SeqScatter(lanes, items, len(places), 0)
 
     units = gate_weight.shape[1]
     spare = -units % 256
@@ -581,6 +579,10 @@
     shift = ((H - z * (q_own // HD)) % H).reshape(1)
 
     input_flat = first_input.reshape(tokens, width)
+    grad_flat = out_grad.reshape(rows, n_heads, own, width).transpose(1, 0, 2, 3)
+    grad_flat = grad_flat.reshape(n_heads * tokens, width)
+    grad_hidden_all = matmul(grad_flat, down_full)
+    input_flat, grad_hidden_all = tie(input_flat, grad_hidden_all)
     query_lin = jnp.concatenate(
         [matmul(input_flat, query_weight), matmul(input_flat, query_rest)], axis=1
     )
@@ -603,10 +605,7 @@
 
     order = Order()
     order.mark(second_own)
-    tokens_ring = gather_ring(lanes, second_own)
-    grad_flat = out_grad.reshape(rows, n_heads, own, width).transpose(1, 0, 2, 3)
-    grad_flat = grad_flat.reshape(n_heads * tokens, width)
-    grad_hidden_all = order.mark(matmul(order.then(grad_flat), down_full))
+    tokens_ring = [second_own, lanes.ring(second_own)]
 
     def all_tokens(parts):
         full = jnp.zeros((n_heads * tokens, parts[0].shape[1]), bf16)
@@ -615,8 +614,13 @@
         return by_rows(full)
 
     hidden_parts, gate_parts, up_parts, back_parts = [], [], [], []
-    for m, part in enumerate(tokens_ring):
-        part = order.then(part)
+    for m in range(n_heads):
+        part = order.then(tokens_ring[m])
+        if m > 0:
+            part, back_parts[m - 1] = tie(part, back_parts[m - 1])
+            tokens_ring[m] = part
+        if 0 < m < n_heads - 1:
+            tokens_ring.append(lanes.ring(part))
         grad_hidden = take(grad_hidden_all, (z + m) % n_heads, tokens, 0)
         gate_act = matmul(part, gate_full)
         up_act = matmul(part, up_full)
@@ -645,16 +649,12 @@
     block_out = (second_stream + ffn_own.astype(f32)).reshape(rows, own, width)
     second_input = order.mark(all_tokens(order.then(tokens_ring)))
     gate_terms = halves_grad(second_input, all_tokens(order.then(gate_parts)))
-    down_scatter = SeqScatter(lanes, [row_blocks(order.then(down_terms))], 0).step()
+    down_scatter = row_scatter(order.then(down_terms)).step()
     order.mark(lanes.sent["seq"][-1])
     up_terms = halves_grad(second_input, all_tokens(order.then(up_parts)))
-    down_scatter.items = order.then(down_scatter.items)
-    down_grad = total_of(down_scatter.terms()[0])[:, :units]
-    order.mark(lanes.sent["seq"][-1])
-    both_scatter = SeqScatter(
-        lanes, order.then([row_blocks(gate_terms), row_blocks(up_terms)]), 0
-    ).step()
-    order.mark(lanes.sent["seq"][-1])
+    (down_sum,) = down_scatter.terms()
+    down_grad = total_of(down_sum)[:, :units]
+    both_scatter = row_scatter(order.then(gate_terms), order.then(up_terms)).step()
 
     second_back = order.then(second_back).astype(f32)
     second_gain_term = jnp.sum(second_back * second_normed, axis=0)
@@ -678,18 +678,15 @@
     )
     order.mark(grad_query)
     grad_query = grad_query.reshape(tokens, q_all)
-    gate_sum, up_sum = both_scatter.terms()
     kv_scatter = SeqScatter(
         lanes,
-        [[[part] for half_of in (kv_low, kv_high) for part in split(half_of, n_seq // 2, 1)]],
+        [lambda p: [take((kv_low, kv_high)[p // (n_seq // 2)], p % (n_seq // 2), shard, 1)]],
+        n_seq,
         1,
     ).step(kv_high)
     query_terms = halves_grad(input_flat, grad_query)
     output_terms = halves_grad(grad_attn, attended)
-    kv_scatter.items = order.then(kv_scatter.items)
     (kv_terms,) = kv_scatter.terms()
-    order.mark(lanes.sent["seq"][-1])
-    gate_grad, up_grad = (total_of(order.then(terms))[:, :units] for terms in (gate_sum, up_sum))
 
     kv_sum = total_of(order.then(kv_terms)).astype(bf16)
     kv_away = order.mark(
@@ -697,10 +694,7 @@
     )
     kv_came = lanes.direct(kv_away, True)
 
-    qo_scatter = SeqScatter(
-        lanes, order.then([row_blocks(query_terms), row_blocks(output_terms)]), 0
-    ).step()
-    order.mark(lanes.sent["seq"][-1])
+    qo_scatter = row_scatter(order.then(query_terms), order.then(output_terms)).step()
     first_scale = rms_scale(stream)
     first_normed = stream * first_scale
     first_gain = attn_gain.astype(f32)
@@ -744,7 +738,7 @@
     )
     kv_other, came_small = apart(lanes.core(with_small(kv_other)))
     small = as_sent(small + came_small)
-    kv_terms = row_blocks([kv_mine, kv_other])
+    kv_terms = [[take(part, place, depth, 0) for part in (kv_mine, kv_other)] for place in places]
     while len(kv_terms) > 1:
         count = len(kv_terms) // 2
         message = join([low_total(terms) for terms in kv_terms[count:]], 0)
@@ -772,6 +766,7 @@
     residual_grad = grad_stream + norm_back(first_back, first_normed, first_scale, first_gain)
 
     query_sum, output_sum = (low_total(terms) for terms in qo_scatter.terms())
+    gate_grad, up_grad = (total_of(terms)[:, :units] for terms in both_scatter.terms())
     qo_parts = [
         jnp.concatenate(pair, axis=1)
         for pair in zip(split(query_sum, n_heads, 1), split(output_sum, n_heads, 1))

time: 643 us -> 563 us (0.88)
  waiting for transfers between devices: 255 us -> 167 us
  starting transfers between devices: 36.5 us -> 48.8 us
  other arithmetic: 44.2 us -> 56.3 us
  matrix products: 153 us -> 146 us
    ppermute x12, waiting for transfers between devices: 130 us -> 74.4 us  [seq(): lax.ppermute(v, ('dp', 'seq'), pairs)]
    ppermute x3, waiting for transfers between devices: 32.9 us -> 5.43 us  [rotate_down(): return lax.ppermute(value, axis, pairs)]
    dynamic_slice x16 -> x7, local copies, waits for them, and re-layouts: 19.8 us -> 3.51 us  [take(): return lax.dynamic_slice_in_dim(value, index * size, size, dim)]
    unnamed x222 -> x212, local copies, waits for them, and re-layouts: 29.5 us -> 38.6 us
    convert_element_type x17 -> x13, other arithmetic: 10.9 us -> 18.9 us  [low_total(): return parts[0] if len(parts) == 1 else total_of(parts).astype(bf16)]
  transfers between devices with their start and end apart: 46 -> 46, of which waited for: 23 -> 20; matrix products, arithmetic and copies ran while one was open for 39% -> 43% of each run, Pallas kernels for 6% -> 7%
where the time goes in v3:
time: 563 us; the launch traced here: 557 us
  waiting for transfers between devices  167 us (30%)
  matrix products  146 us (26%)
  local copies, waits for them, and re-layouts  87 us (15%)
  other arithmetic  56.3 us (10%)
  starting transfers between devices  48.8 us (9%)
  Pallas kernels  36.2 us (6%)
  between operations  15.8 us (3%)
    ppermute x18, waiting for transfers between devices, direct(): lax.ppermute(value, 'heads', [(i, (i + m if away else i - m) % size) for...  87.3 us
    ppermute x12, waiting for transfers between devices, seq(): lax.ppermute(v, ('dp', 'seq'), pairs)  74.4 us
    dot_general x13, matrix products, matmul(): return jnp.dot(left, right, preferred_element_type=f32)  62.7 us
    dot_general x12, matrix products, matmul_tn(): lax.dot_general(left, right, (((0,), (0,)), ((), ())), preferred_element_...  45.6 us
    unnamed x212, local copies, waits for them, and re-layouts  38.6 us
    dot_general x15, matrix products, matmul_nt(): lax.dot_general(left, right, (((1,), (1,)), ((), ())), preferred_element_...  37.5 us
    ppermute x18, starting transfers between devices, direct(): lax.ppermute(value, 'heads', [(i, (i + m if away else i - m) % size) for...  25 us
    pallas_call x1, Pallas kernels, attend_back_call(): pl.pallas_call(attend_back_kernel, grid_spec=pltpu.PrefetchScalarGridSpec...  21 us
  transfers between devices with their start and end apart: 46, of which 20 were waited for; matrix products, arithmetic and copies ran while one was open for 43% of the time, Pallas kernels for 7%

profile of v3, /device:TPU:9, one launch (start us, length us, event | category | flops | bytes accessed | tf_op | source)
XLA Modules:
  0.0 557.3 jit_solution(786208428150512271)
XLA Ops:
  25.5 12.1 %collective-permute-done.1 = bf16[3,96,512]{2,1,0:T(8,128)(2,1)S(1)} collective-permute-done((bf16[3,96,512]{2,1,0:T(8,128)(2,1)S(1)}, bf16[3,96,512]{2,1,0:T(8,128)(2,1)S(1)}, u32[]{:S(2)}, u32[]{:S(2)}) %collective-permute-start.1) | collective-permute-done | bytes 294944 | tf_op jit(solution)/shard_map/ppermute | solution.py:72
  38.6 5.3 collective-permute-done.2
  49.9 21.7 %collective-permute-done.6 = bf16[3,384,512]{2,1,0:T(8,128)(2,1)} collective-permute-done((bf16[3,384,512]{2,1,0:T(8,128)(2,1)}, bf16[3,384,512]{2,1,0:T(8,128)(2,1)}, u32[]{:S(2)}, u32[]{:S(2)}) %collective-permute-start.6) | collective-permute-done | bytes 1179680 | tf_op jit(solution)/shard_map/ppermute | solution.py:62
  75.7 11.2 %collective-permute-done.4 = bf16[784,384]{1,0:T(8,128)(2,1)S(1)} collective-permute-done((bf16[784,384]{1,0:T(8,128)(2,1)S(1)}, bf16[784,384]{1,0:T(8,128)(2,1)S(1)}, u32[]{:S(2)}, u32[]{:S(2)}) %collective-permute-start.4) | collective-permute-done | bytes 602144 | tf_op jit(solution)/shard_map/ppermute | solution.py:72
  86.9 12.9 %collective-permute-done.5 = bf16[784,384]{1,0:T(8,128)(2,1)S(1)} collective-permute-done((bf16[784,384]{1,0:T(8,128)(2,1)S(1)}, bf16[784,384]{1,0:T(8,128)(2,1)S(1)}, u32[]{:S(2)}, u32[]{:S(2)}) %collective-permute-start.5) | collective-permute-done | bytes 602144 | tf_op jit(solution)/shard_map/ppermute | solution.py:72
  105.5 4.0 copy.39
  113.7 4.0 collective-permute-start.11
  122.9 6.5 %collective-permute-done.8 = bf16[3,768,512]{2,1,0:T(8,128)(2,1)} collective-permute-done((bf16[3,768,512]{2,1,0:T(8,128)(2,1)}, bf16[3,768,512]{2,1,0:T(8,128)(2,1)}, u32[]{:S(2)}, u32[]{:S(2)}) %collective-permute-start.8) | collective-permute-done | bytes 2359328 | tf_op jit(solution)/shard_map/ppermute | solution.py:62
  132.6 14.6 %convolution_bitcast_fusion = f32[1152,2304]{1,0:T(8,128)} fusion(bf16[1152,1536]{1,0:T(8,128)(2,1)} %bitcast.127, bf16[1536,2304]{1,0:T(8,128)(2,1)} %all-gather.4.cloned.1.call-done), kind=kOutput, calls=%fused_computation | convolution fusion | flops 8153726976 | bytes 21233664 | tf_op jit(solution)/shard_map/dot_general | solution.py:455
  151.5 13.0 %attend.1 = (bf16[3,96,1536]{2,1,0:T(8,128)(2,1)S(1)}, bf16[3,96,1536]{2,1,0:T(8,128)(2,1)S(1)}, f32[3,2,1,576]{3,2,1,0:T(1,128)S(1)}) custom-call(s32[1]{0:T(128)} %bitcast.1.shift_ref, f32[3,96,1536]{2,1,0:T(8,128)S(1)} %maximum_add_fusion.q_ref, f32[96,128]{1,0:T(8,128)S(1)} %pad_maximum_fusion.16.cos_ref, f32[96,128]{1,0:T(8,128)S(1)} %pad_maximum_fusion.17.sin_ref, ...), custom_call_target="tpu_custom_call" | custom-call | flops 2717908992 | bytes 4718592 | tf_op jit(solution)/shard_map/attend/pallas_call | solution.py:302
  186.7 6.7 %fusion.65 = f32[288,2304]{1,0:T(8,128)} fusion(bf16[288,1536]{1,0:T(8,128)(2,1)S(1)} %multiply_convert_fusion.12, bf16[1536,2304]{1,0:T(8,128)(2,1)} %all-gather.8.cloned.1.call-done), kind=kOutput, calls=%fused_computation.250 | convolution fusion | flops 2038431744 | bytes 10616832 | tf_op jit(solution)/shard_map/dot_general | solution.py:455
  193.4 8.9 %multiply_convert_fusion.9 = (bf16[288,2304]{1,0:T(8,128)(2,1)S(1)}, bf16[288,2304]{1,0:T(8,128)(2,1)S(1)}, bf16[288,2304]{1,0:T(8,128)(2,1)}) fusion(f32[1152,2304]{1,0:T(8,128)} %convolution_bitcast_fusion, s32[]{:T(128)S(6)} %select_n.261, f32[288,2304]{1,0:T(8,128)} %fusion.65, bf16[288,1536]{1,0:T(8,128)(2,1)S(1)} %multiply_convert_fusion.12, ...), kind=kOutput, calls=%fused_computation.37 | convolution fusion | flops 2048385024 | bytes 17252356 | tf_op jit(solution)/shard_map/dot_general | solution.py:455
  215.0 6.4 %multiply_convert_fusion.6 = (bf16[288,2304]{1,0:T(8,128)(2,1)S(1)}, bf16[288,2304]{1,0:T(8,128)(2,1)S(1)}, bf16[288,2304]{1,0:T(8,128)(2,1)}) fusion(f32[1152,2304]{1,0:T(8,128)} %convolution_bitcast_fusion, s32[]{:T(128)S(6)} %select_n.263, f32[288,2304]{1,0:T(8,128)S(1)} %fusion.67, bf16[288,1536]{1,0:T(8,128)(2,1)} %collective-permute-done.13, ...), kind=kOutput, calls=%fused_computation.32 | convolution fusion | flops 2048385024 | bytes 17252356 | tf_op jit(solution)/shard_map/dot_general | solution.py:455
  235.0 6.2 %multiply_convert_fusion.3 = (bf16[288,2304]{1,0:T(8,128)(2,1)S(1)}, bf16[288,2304]{1,0:T(8,128)(2,1)S(1)}, bf16[288,2304]{1,0:T(8,128)(2,1)}) fusion(f32[1152,2304]{1,0:T(8,128)} %convolution_bitcast_fusion, s32[]{:T(128)S(6)} %select_n.265, f32[288,2304]{1,0:T(8,128)S(1)} %fusion.69, bf16[288,1536]{1,0:T(8,128)(2,1)S(1)} %collective-permute-done.14, ...), kind=kOutput, calls=%fused_computation.27 | convolution fusion | flops 2048385024 | bytes 17252356 | tf_op jit(solution)/shard_map/dot_general | solution.py:455
  246.6 3.8 collective-permute-done.15
  253.8 6.2 %multiply_convert_fusion = (bf16[288,2304]{1,0:T(8,128)(2,1)S(1)}, bf16[288,2304]{1,0:T(8,128)(2,1)S(1)}, bf16[288,2304]{1,0:T(8,128)(2,1)}) fusion(f32[1152,2304]{1,0:T(8,128)} %convolution_bitcast_fusion, s32[]{:T(128)S(6)} %select_n.267, f32[288,2304]{1,0:T(8,128)S(1)} %fusion.71, bf16[288,1536]{1,0:T(8,128)(2,1)S(1)} %collective-permute-done.15, ...), kind=kOutput, calls=%fused_computation.22 | convolution fusion | flops 2048385024 | bytes 17252356 | tf_op jit(solution)/shard_map/dot_general | solution.py:455
  270.8 6.4 %convolution_convert_fusion.6 = bf16[768,2304]{1,0:T(8,128)(2,1)} fusion(bf16[1152,2304]{1,0:T(8,128)(2,1)S(1)} %constant_dynamic-update-slice_fusion.30, bf16[1152,1536]{1,0:T(8,128)(2,1)S(1)} %bitcast.128, s32[]{:T(128)S(6)} %select_n.256), kind=kOutput, calls=%fused_computation.7 | convolution fusion | flops 4078632960 | bytes 10616836 | tf_op jit(solution)/shard_map/dot_general | solution.py:463
  277.3 6.4 %convolution_convert_fusion.5 = bf16[768,2304]{1,0:T(8,128)(2,1)} fusion(bf16[1152,2304]{1,0:T(8,128)(2,1)S(1)} %constant_dynamic-update-slice_fusion.30, bf16[1152,1536]{1,0:T(8,128)(2,1)S(1)} %bitcast.129, s32[]{:T(128)S(6)} %select_n.255), kind=kOutput, calls=%fused_computation.6 | convolution fusion | flops 4078632960 | bytes 10616836 | tf_op jit(solution)/shard_map/dot_general | solution.py:463
  283.7 10.0 %convolution_convert_fusion = bf16[1152,1536]{1,0:T(8,128)(2,1)} fusion(bf16[1152,2304]{1,0:T(8,128)(2,1)S(1)} %constant_dynamic-update-slice_fusion.30, bf16[1536,2304]{1,0:T(8,128)(2,1)S(1)} %bitcast.141), kind=kOutput, calls=%fused_computation.1 | convolution fusion | flops 8155496448 | bytes 15925248 | tf_op jit(solution)/shard_map/dot_general | solution.py:459
  302.1 6.4 %convolution_convert_fusion.4 = bf16[768,2304]{1,0:T(8,128)(2,1)} fusion(bf16[1152,2304]{1,0:T(8,128)(2,1)S(1)} %constant_dynamic-update-slice_fusion.22, bf16[1152,1536]{1,0:T(8,128)(2,1)S(1)} %constant_dynamic-update-slice_fusion.26, s32[]{:T(128)S(6)} %select_n.256), kind=kOutput, calls=%fused_computation.5 | convolution fusion | flops 4078632960 | bytes 10616836 | tf_op jit(solution)/shard_map/dot_general | solution.py:463
  308.5 5.5 convolution_convert_fusion.3
  319.0 6.4 %convolution_convert_fusion.2 = bf16[768,2304]{1,0:T(8,128)(2,1)} fusion(bf16[1152,2304]{1,0:T(8,128)(2,1)S(1)} %constant_dynamic-update-slice_fusion.18, bf16[1152,1536]{1,0:T(8,128)(2,1)S(1)} %constant_dynamic-update-slice_fusion.26, s32[]{:T(128)S(6)} %select_n.256), kind=kOutput, calls=%fused_computation.3 | convolution fusion | flops 4078632960 | bytes 10616836 | tf_op jit(solution)/shard_map/dot_general | solution.py:463
  327.5 6.5 %convolution_convert_fusion.1 = bf16[768,2304]{1,0:T(8,128)(2,1)} fusion(bf16[1152,2304]{1,0:T(8,128)(2,1)S(1)} %constant_dynamic-update-slice_fusion.18, bf16[1152,1536]{1,0:T(8,128)(2,1)S(1)} %constant_dynamic-update-slice_fusion.26, s32[]{:T(128)S(6)} %select_n.255), kind=kOutput, calls=%fused_computation.2 | convolution fusion | flops 4078632960 | bytes 10616836 | tf_op jit(solution)/shard_map/dot_general | solution.py:463
  351.9 21.0 %attend_back.1 = (bf16[3,96,1536]{2,1,0:T(8,128)(2,1)S(1)}, bf16[3,768,512]{2,1,0:T(8,128)(2,1)S(1)}, bf16[3,768,512]{2,1,0:T(8,128)(2,1)}) custom-call(s32[1]{0:T(128)} %bitcast.1.shift_ref, bf16[3,96,1536]{2,1,0:T(8,128)(2,1)S(1)} %copy-done.25, bf16[3,96,1536]{2,1,0:T(8,128)(2,1)S(1)} %pad_maximum_fusion.6.og_ref, f32[96,128]{1,0:T(8,128)S(1)} %copy-done.12, ...), custom_call_target="tpu_custom_call" | custom-call | flops 6794772480 | bytes 9437184 | tf_op jit(solution)/shard_map/attend_back/pallas_call | solution.py:392
  387.1 30.8 %collective-permute-done.21 = bf16[3,768,512]{2,1,0:T(8,128)(2,1)} collective-permute-done((bf16[3,768,512]{2,1,0:T(8,128)(2,1)}, bf16[3,768,512]{2,1,0:T(8,128)(2,1)}, u32[]{:S(2)}, u32[]{:S(2)}) %collective-permute-start.21) | collective-permute-done | bytes 2359328 | tf_op jit(solution)/shard_map/ppermute | solution.py:62
  423.3 4.5 add_convert_fusion.3
  427.8 7.2 %collective-permute-done.23 = bf16[3,384,512]{2,1,0:T(8,128)(2,1)S(1)} collective-permute-done((bf16[3,384,512]{2,1,0:T(8,128)(2,1)S(1)}, bf16[3,384,512]{2,1,0:T(8,128)(2,1)S(1)}, u32[]{:S(2)}, u32[]{:S(2)}) %collective-permute-start.23) | collective-permute-done | bytes 1179680 | tf_op jit(solution)/shard_map/ppermute | solution.py:62
  452.3 18.5 %collective-permute-done.25 = bf16[3,96,512]{2,1,0:T(8,128)(2,1)S(1)} collective-permute-done((bf16[3,96,512]{2,1,0:T(8,128)(2,1)S(1)}, bf16[3,96,512]{2,1,0:T(8,128)(2,1)S(1)}, u32[]{:S(2)}, u32[]{:S(2)}) %collective-permute-start.25) | collective-permute-done | bytes 294944 | tf_op jit(solution)/shard_map/ppermute | solution.py:72
  484.7 4.5 collective-permute-done.30
  500.1 5.0 multiply_add_fusion
  521.7 15.8 %collective-permute-done.38 = bf16[192,768]{1,0:T(8,128)(2,1)} collective-permute-done((bf16[192,768]{1,0:T(8,128)(2,1)}, bf16[192,768]{1,0:T(8,128)(2,1)}, u32[]{:S(2)}, u32[]{:S(2)}) %collective-permute-start.38) | collective-permute-done | bytes 294944 | tf_op jit(solution)/shard_map/ppermute | solution.py:72
  537.5 4.0 collective-permute-done.39
  (464 shorter events, 238.8 us)
Async XLA Ops:
  7.2 125.4 %all-gather.4.cloned.1.call-start = ((), (), s32[]{:S(2)}) async-start(), calls=%async_computation.2 | async-start | bytes 7962624 | tf_op jit(solution)/shard_map/all_gather | solution.py:548
  9.6 177.1 %all-gather.8.cloned.1.call-start = ((), (), s32[]{:S(2)}) async-start(), calls=%async_computation.4 | async-start | bytes 7962624 | tf_op jit(solution)/shard_map/all_gather | solution.py:548
  10.7 182.8 %all-gather.6.cloned.1.call-start = ((), (), s32[]{:S(2)}) async-start(), calls=%async_computation.3 | async-start | bytes 7962624 | tf_op jit(solution)/shard_map/all_gather | solution.py:548
  13.0 327.2 %reduce-scatter.5.cloned.1.call-start = ((), (), s32[]{:S(2)}) async-start(), calls=%async_computation.6 | async-start | bytes 4423680 | tf_op jit(solution)/shard_map/reduce_scatter | solution.py:641
  16.6 21.1 %collective-permute-start.1 = (bf16[3,96,512]{2,1,0:T(8,128)(2,1)S(1)}, bf16[3,96,512]{2,1,0:T(8,128)(2,1)S(1)}, u32[]{:S(2)}, u32[]{:S(2)}) collective-permute-start(bf16[3,96,512]{2,1,0:T(8,128)(2,1)S(1)} %get-tuple-element.115), channel_id=1, source_target_pairs={{0,2},{1,3},{2,0},{3,1},{4,6},{5,7},{6,4},{7,5},{8,10},{9,11},{10,... | collective-permute-start | bytes 884744 | tf_op jit(solution)/shard_map/ppermute | solution.py:72
  19.0 24.9 %collective-permute-start.2 = (bf16[3,96,512]{2,1,0:T(8,128)(2,1)S(1)}, bf16[3,96,512]{2,1,0:T(8,128)(2,1)S(1)}, u32[]{:S(2)}, u32[]{:S(2)}) collective-permute-start(bf16[3,96,512]{2,1,0:T(8,128)(2,1)S(1)} %get-tuple-element.115), channel_id=1, source_target_pairs={{0,1},{1,2},{2,3},{3,0},{4,5},{5,6},{6,7},{7,4},{8,9},{9,10},{10,1... | collective-permute-start | bytes 884744 | tf_op jit(solution)/shard_map/ppermute | solution.py:72
  44.9 26.7 %collective-permute-start.6 = (bf16[3,384,512]{2,1,0:T(8,128)(2,1)}, bf16[3,384,512]{2,1,0:T(8,128)(2,1)}, u32[]{:S(2)}, u32[]{:S(2)}) collective-permute-start(bf16[3,384,512]{2,1,0:T(8,128)(2,1)} %get-tuple-element.313), channel_id=1, source_target_pairs={{0,4},{4,0},{8,12},{12,8},{16,24},{20,28},{24,16},{28,20},{1,5},{5... | collective-permute-start | bytes 3538952 | tf_op jit(solution)/shard_map/ppermute | solution.py:62
  46.4 29.3 %collective-permute-start.3 = (bf16[784,384]{1,0:T(8,128)(2,1)S(1)}, bf16[784,384]{1,0:T(8,128)(2,1)S(1)}, u32[]{:S(2)}, u32[]{:S(2)}) collective-permute-start(bf16[784,384]{1,0:T(8,128)(2,1)S(1)} %fusion.23), channel_id=1, source_target_pairs={{0,3},{1,0},{2,1},{3,2},{4,7},{5,4},{6,5},{7,6},{8,11},{9,8},{10,9... | collective-permute-start | bytes 1806344 | tf_op jit(solution)/shard_map/ppermute | solution.py:72
  48.0 38.9 %collective-permute-start.4 = (bf16[784,384]{1,0:T(8,128)(2,1)S(1)}, bf16[784,384]{1,0:T(8,128)(2,1)S(1)}, u32[]{:S(2)}, u32[]{:S(2)}) collective-permute-start(bf16[784,384]{1,0:T(8,128)(2,1)S(1)} %fusion.23), channel_id=1, source_target_pairs={{0,2},{1,3},{2,0},{3,1},{4,6},{5,7},{6,4},{7,5},{8,10},{9,11},{10,... | collective-permute-start | bytes 1806344 | tf_op jit(solution)/shard_map/ppermute | solution.py:72
  49.9 49.9 %collective-permute-start.5 = (bf16[784,384]{1,0:T(8,128)(2,1)S(1)}, bf16[784,384]{1,0:T(8,128)(2,1)S(1)}, u32[]{:S(2)}, u32[]{:S(2)}) collective-permute-start(bf16[784,384]{1,0:T(8,128)(2,1)S(1)} %fusion.23), channel_id=1, source_target_pairs={{0,1},{1,2},{2,3},{3,0},{4,5},{5,6},{6,7},{7,4},{8,9},{9,10},{10,1... | collective-permute-start | bytes 1806344 | tf_op jit(solution)/shard_map/ppermute | solution.py:72
  74.6 54.8 %collective-permute-start.8 = (bf16[3,768,512]{2,1,0:T(8,128)(2,1)}, bf16[3,768,512]{2,1,0:T(8,128)(2,1)}, u32[]{:S(2)}, u32[]{:S(2)}) collective-permute-start(bf16[3,768,512]{2,1,0:T(8,128)(2,1)} %get-tuple-element.119), channel_id=1, source_target_pairs={{0,8},{4,12},{8,0},{12,4},{16,20},{20,16},{24,28},{28,24},{1,9},{5... | collective-permute-start | bytes 7077896 | tf_op jit(solution)/shard_map/ppermute | solution.py:62
  113.7 52.7 %collective-permute-start.10 = (bf16[768,384]{1,0:T(8,128)(2,1)}, bf16[768,384]{1,0:T(8,128)(2,1)}, u32[]{:S(2)}, u32[]{:S(2)}) collective-permute-start(bf16[768,384]{1,0:T(8,128)(2,1)} %bitcast.135), channel_id=1, source_target_pairs={{0,2},{1,3},{2,0},{3,1},{4,6},{5,7},{6,4},{7,5},{8,10},{9,11},{10,... | collective-permute-start | bytes 1769480 | tf_op jit(solution)/shard_map/ppermute | solution.py:72
  113.7 52.7 %collective-permute-start.11 = (bf16[768,384]{1,0:T(8,128)(2,1)}, bf16[768,384]{1,0:T(8,128)(2,1)}, u32[]{:S(2)}, u32[]{:S(2)}) collective-permute-start(bf16[768,384]{1,0:T(8,128)(2,1)} %bitcast.136), channel_id=1, source_target_pairs={{0,1},{1,2},{2,3},{3,0},{4,5},{5,6},{6,7},{7,4},{8,9},{9,10},{10,1... | collective-permute-start | bytes 1769480 | tf_op jit(solution)/shard_map/ppermute | solution.py:72
  117.7 50.5 %collective-permute-start.9 = (bf16[768,384]{1,0:T(8,128)(2,1)}, bf16[768,384]{1,0:T(8,128)(2,1)}, u32[]{:S(2)}, u32[]{:S(2)}) collective-permute-start(bf16[768,384]{1,0:T(8,128)(2,1)} %bitcast.137), channel_id=1, source_target_pairs={{0,3},{1,0},{2,1},{3,2},{4,7},{5,4},{6,5},{7,6},{8,11},{9,8},{10,9... | collective-permute-start | bytes 1769480 | tf_op jit(solution)/shard_map/ppermute | solution.py:72
  186.2 22.0 %collective-permute-start.13 = (bf16[288,1536]{1,0:T(8,128)(2,1)S(1)}, bf16[288,1536]{1,0:T(8,128)(2,1)}, u32[]{:S(2)}, u32[]{:S(2)}) collective-permute-start(bf16[288,1536]{1,0:T(8,128)(2,1)S(1)} %multiply_convert_fusion.12), channel_id=1, source_target_pairs={{0,3},{1,0},{2,1},{3,2},{4,7},{5,4},{6,5},{7,6},{8,11},{9,8},{10,9... | collective-permute-start | bytes 2654216 | tf_op jit(solution)/shard_map/ppermute | solution.py:39
  208.1 22.4 %collective-permute-start.14 = (bf16[288,1536]{1,0:T(8,128)(2,1)}, bf16[288,1536]{1,0:T(8,128)(2,1)S(1)}, u32[]{:S(2)}, u32[]{:S(2)}) collective-permute-start(bf16[288,1536]{1,0:T(8,128)(2,1)} %collective-permute-done.13), channel_id=1, source_target_pairs={{0,3},{1,0},{2,1},{3,2},{4,7},{5,4},{6,5},{7,6},{8,11},{9,8},{10,9... | collective-permute-start | bytes 2654216 | tf_op jit(solution)/shard_map/ppermute | solution.py:39
  265.6 234.5 %reduce-scatter.3.cloned.1.call-start = ((), (), s32[]{:S(2)}) async-start(), calls=%async_computation.5 | async-start | bytes 4423680 | tf_op jit(solution)/shard_map/reduce_scatter | solution.py:646
  293.7 20.4 %collective-permute-start.16 = (bf16[768,2304]{1,0:T(8,128)(2,1)}, bf16[768,2304]{1,0:T(8,128)(2,1)S(1)}, u32[]{:S(2)}, u32[]{:S(2)}) collective-permute-start(bf16[768,2304]{1,0:T(8,128)(2,1)} %convolution_convert_fusion.6), channel_id=1, source_target_pairs={{0,16},{16,0},{1,17},{17,1},{2,18},{18,2},{3,19},{19,3},{4,20},{20... | collective-permute-start | bytes 10616840 | tf_op jit(solution)/shard_map/ppermute | solution.py:33
  308.5 25.5 %collective-permute-start.17 = (bf16[768,2304]{1,0:T(8,128)(2,1)}, bf16[768,2304]{1,0:T(8,128)(2,1)S(1)}, u32[]{:S(2)}, u32[]{:S(2)}) collective-permute-start(bf16[768,2304]{1,0:T(8,128)(2,1)} %convolution_convert_fusion.4), channel_id=1, source_target_pairs={{0,16},{16,0},{1,17},{17,1},{2,18},{18,2},{3,19},{19,3},{4,20},{20... | collective-permute-start | bytes 10616840 | tf_op jit(solution)/shard_map/ppermute | solution.py:33
  314.7 21.8 %collective-permute-start.19 = (bf16[384,2304]{1,0:T(8,128)(2,1)S(1)}, bf16[384,2304]{1,0:T(8,128)(2,1)S(1)}, u32[]{:S(2)}, u32[]{:S(2)}) collective-permute-start(bf16[384,2304]{1,0:T(8,128)(2,1)S(1)} %pad_maximum_fusion.3), channel_id=1, source_target_pairs={{0,8},{4,12},{8,0},{12,4},{16,20},{20,16},{24,28},{28,24},{1,9},{5... | collective-permute-start | bytes 5308424 | tf_op jit(solution)/shard_map/ppermute | solution.py:62
  325.4 21.6 %collective-permute-start.18 = (bf16[768,2304]{1,0:T(8,128)(2,1)}, bf16[768,2304]{1,0:T(8,128)(2,1)}, u32[]{:S(2)}, u32[]{:S(2)}) collective-permute-start(bf16[768,2304]{1,0:T(8,128)(2,1)} %convolution_convert_fusion.2), channel_id=1, source_target_pairs={{0,16},{16,0},{1,17},{17,1},{2,18},{18,2},{3,19},{19,3},{4,20},{20... | collective-permute-start | bytes 10616840 | tf_op jit(solution)/shard_map/ppermute | solution.py:33
  338.0 36.3 %collective-permute-start.20 = (bf16[192,2304]{1,0:T(8,128)(2,1)}, bf16[192,2304]{1,0:T(8,128)(2,1)}, u32[]{:S(2)}, u32[]{:S(2)}) collective-permute-start(bf16[192,2304]{1,0:T(8,128)(2,1)} %add_convert_fusion.4), channel_id=1, source_target_pairs={{0,4},{4,0},{8,12},{12,8},{16,24},{20,28},{24,16},{28,20},{1,5},{5... | collective-permute-start | bytes 2654216 | tf_op jit(solution)/shard_map/ppermute | solution.py:62
  351.6 67.8 %collective-permute-start.22 = (bf16[768,2304]{1,0:T(8,128)(2,1)}, bf16[768,2304]{1,0:T(8,128)(2,1)}, u32[]{:S(2)}, u32[]{:S(2)}) collective-permute-start(bf16[768,2304]{1,0:T(8,128)(2,1)} %pad_maximum_fusion), channel_id=1, source_target_pairs={{0,8},{4,12},{8,0},{12,4},{16,20},{20,16},{24,28},{28,24},{1,9},{5... | collective-permute-start | bytes 10616840 | tf_op jit(solution)/shard_map/ppermute | solution.py:62
  374.3 43.5 %collective-permute-start.21 = (bf16[3,768,512]{2,1,0:T(8,128)(2,1)}, bf16[3,768,512]{2,1,0:T(8,128)(2,1)}, u32[]{:S(2)}, u32[]{:S(2)}) collective-permute-start(bf16[3,768,512]{2,1,0:T(8,128)(2,1)} %get-tuple-element.186), channel_id=1, source_target_pairs={{0,8},{4,12},{8,0},{12,4},{16,20},{20,16},{24,28},{28,24},{1,9},{5... | collective-permute-start | bytes 7077896 | tf_op jit(solution)/shard_map/ppermute | solution.py:62
  379.6 63.2 %collective-permute-start.27 = (bf16[768,1536]{1,0:T(8,128)(2,1)S(1)}, bf16[768,1536]{1,0:T(8,128)(2,1)S(1)}, u32[]{:S(2)}, u32[]{:S(2)}) collective-permute-start(bf16[768,1536]{1,0:T(8,128)(2,1)S(1)} %convolution_convert_fusion.10), channel_id=1, source_target_pairs={{0,16},{16,0},{1,17},{17,1},{2,18},{18,2},{3,19},{19,3},{4,20},{20... | collective-permute-start | bytes 7077896 | tf_op jit(solution)/shard_map/ppermute | solution.py:33
  382.9 60.0 %collective-permute-start.29 = (bf16[768,1536]{1,0:T(8,128)(2,1)S(1)}, bf16[768,1536]{1,0:T(8,128)(2,1)S(1)}, u32[]{:S(2)}, u32[]{:S(2)}) collective-permute-start(bf16[768,1536]{1,0:T(8,128)(2,1)S(1)} %convolution_convert_fusion.8), channel_id=1, source_target_pairs={{0,16},{16,0},{1,17},{17,1},{2,18},{18,2},{3,19},{19,3},{4,20},{20... | collective-permute-start | bytes 7077896 | tf_op jit(solution)/shard_map/ppermute | solution.py:33
  438.4 32.4 %collective-permute-start.25 = (bf16[3,96,512]{2,1,0:T(8,128)(2,1)S(1)}, bf16[3,96,512]{2,1,0:T(8,128)(2,1)S(1)}, u32[]{:S(2)}, u32[]{:S(2)}) collective-permute-start(bf16[3,96,512]{2,1,0:T(8,128)(2,1)S(1)} %get-tuple-element.297), channel_id=1, source_target_pairs={{0,2},{1,3},{2,0},{3,1},{4,6},{5,7},{6,4},{7,5},{8,10},{9,11},{10,... | collective-permute-start | bytes 884744 | tf_op jit(solution)/shard_map/ppermute | solution.py:72
  441.5 31.2 %collective-permute-start.26 = (bf16[3,96,512]{2,1,0:T(8,128)(2,1)S(1)}, bf16[3,96,512]{2,1,0:T(8,128)(2,1)S(1)}, u32[]{:S(2)}, u32[]{:S(2)}) collective-permute-start(bf16[3,96,512]{2,1,0:T(8,128)(2,1)S(1)} %get-tuple-element.296), channel_id=1, source_target_pairs={{0,3},{1,0},{2,1},{3,2},{4,7},{5,4},{6,5},{7,6},{8,11},{9,8},{10,9... | collective-permute-start | bytes 884744 | tf_op jit(solution)/shard_map/ppermute | solution.py:72
  446.6 42.7 %collective-permute-start.31 = (bf16[768,1536]{1,0:T(8,128)(2,1)}, bf16[768,1536]{1,0:T(8,128)(2,1)}, u32[]{:S(2)}, u32[]{:S(2)}) collective-permute-start(bf16[768,1536]{1,0:T(8,128)(2,1)} %pad_maximum_fusion.1), channel_id=1, source_target_pairs={{0,8},{4,12},{8,0},{12,4},{16,20},{20,16},{24,28},{28,24},{1,9},{5... | collective-permute-start | bytes 7077896 | tf_op jit(solution)/shard_map/ppermute | solution.py:62
  505.1 38.6 %collective-permute-start.40 = (bf16[384,2304]{1,0:T(8,128)(2,1)}, bf16[384,2304]{1,0:T(8,128)(2,1)S(1)}, u32[]{:S(2)}, u32[]{:S(2)}) collective-permute-start(bf16[384,2304]{1,0:T(8,128)(2,1)} %pad_maximum_fusion.4), channel_id=1, source_target_pairs={{0,4},{4,0},{8,12},{12,8},{16,24},{20,28},{24,16},{28,20},{1,5},{5... | collective-permute-start | bytes 5308424 | tf_op jit(solution)/shard_map/ppermute | solution.py:62
  514.4 23.1 %collective-permute-start.38 = (bf16[192,768]{1,0:T(8,128)(2,1)}, bf16[192,768]{1,0:T(8,128)(2,1)}, u32[]{:S(2)}, u32[]{:S(2)}) collective-permute-start(bf16[192,768]{1,0:T(8,128)(2,1)} %pad_maximum_fusion.10), channel_id=1, source_target_pairs={{0,2},{1,3},{2,0},{3,1},{4,6},{5,7},{6,4},{7,5},{8,10},{9,11},{10,... | collective-permute-start | bytes 884744 | tf_op jit(solution)/shard_map/ppermute | solution.py:72
  516.3 25.3 %collective-permute-start.39 = (bf16[192,768]{1,0:T(8,128)(2,1)}, bf16[192,768]{1,0:T(8,128)(2,1)}, u32[]{:S(2)}, u32[]{:S(2)}) collective-permute-start(bf16[192,768]{1,0:T(8,128)(2,1)} %pad_maximum_fusion.11), channel_id=1, source_target_pairs={{0,3},{1,0},{2,1},{3,2},{4,7},{5,4},{6,5},{7,6},{8,11},{9,8},{10,9... | collective-permute-start | bytes 884744 | tf_op jit(solution)/shard_map/ppermute | solution.py:72
  (116 other events, 1212.7 us)
Sparse Core Ops, SparseCore 0:
  10.5 56.0 all-gather.3
  69.1 65.0 all-gather.7
  136.0 48.8 all-gather.5
  265.8 72.5 reduce-scatter.4
  377.2 85.1 reduce-scatter.2

commit v4 on v3

--- a/solution.py
+++ b/solution.py
@@ -684,6 +684,7 @@
         n_seq,
         1,
     ).step(kv_high)
+    kv_scatter.came[0], both_scatter.came[0] = tie(kv_scatter.came[0], both_scatter.came[0])
     query_terms = halves_grad(input_flat, grad_query)
     output_terms = halves_grad(grad_attn, attended)
     (kv_terms,) = kv_scatter.terms()

time: 563 us -> 561 us (level)
    convert_element_type x13 -> x14, other arithmetic: 18.9 us -> 18.4 us  [low_total(): return parts[0] if len(parts) == 1 else total_of(parts).astype(bf16)]
  transfers between devices with their start and end apart: 46 -> 46, of which waited for: 20 -> 19; matrix products, arithmetic and copies ran while one was open for 43% -> 43% of each run, Pallas kernels for 7% -> 7%
where the time goes in v4:
time: 561 us; the launch traced here: 555 us
  waiting for transfers between devices  167 us (30%)
  matrix products  145 us (26%)
  local copies, waits for them, and re-layouts  88.1 us (16%)
  other arithmetic  55.7 us (10%)
  starting transfers between devices  47.6 us (8%)
  Pallas kernels  36.2 us (6%)
  between operations  15.8 us (3%)
    ppermute x18, waiting for transfers between devices, direct(): lax.ppermute(value, 'heads', [(i, (i + m if away else i - m) % size) for...  82.3 us
    ppermute x12, waiting for transfers between devices, seq(): lax.ppermute(v, ('dp', 'seq'), pairs)  78.4 us
    dot_general x13, matrix products, matmul(): return jnp.dot(left, right, preferred_element_type=f32)  62.7 us
    dot_general x12, matrix products, matmul_tn(): lax.dot_general(left, right, (((0,), (0,)), ((), ())), preferred_element_...  44.4 us
    unnamed x212, local copies, waits for them, and re-layouts  38.4 us
    dot_general x15, matrix products, matmul_nt(): lax.dot_general(left, right, (((1,), (1,)), ((), ())), preferred_element_...  37.5 us
    ppermute x18, starting transfers between devices, direct(): lax.ppermute(value, 'heads', [(i, (i + m if away else i - m) % size) for...  24.9 us
    pallas_call x1, Pallas kernels, attend_back_call(): pl.pallas_call(attend_back_kernel, grid_spec=pltpu.PrefetchScalarGridSpec...  20.9 us
  transfers between devices with their start and end apart: 46, of which 19 were waited for; matrix products, arithmetic and copies ran while one was open for 43% of the time, Pallas kernels for 7%

profile of v4, /device:TPU:9, one launch (start us, length us, event | category | flops | bytes accessed | tf_op | source)
XLA Modules:
  0.0 554.9 jit_solution(8974002954074514615)
XLA Ops:
  25.5 12.1 %collective-permute-done.1 = bf16[3,96,512]{2,1,0:T(8,128)(2,1)S(1)} collective-permute-done((bf16[3,96,512]{2,1,0:T(8,128)(2,1)S(1)}, bf16[3,96,512]{2,1,0:T(8,128)(2,1)S(1)}, u32[]{:S(2)}, u32[]{:S(2)}) %collective-permute-start.1) | collective-permute-done | bytes 294944 | tf_op jit(solution)/shard_map/ppermute | solution.py:72
  38.6 5.3 collective-permute-done.2
  49.9 21.8 %collective-permute-done.6 = bf16[3,384,512]{2,1,0:T(8,128)(2,1)} collective-permute-done((bf16[3,384,512]{2,1,0:T(8,128)(2,1)}, bf16[3,384,512]{2,1,0:T(8,128)(2,1)}, u32[]{:S(2)}, u32[]{:S(2)}) %collective-permute-start.6) | collective-permute-done | bytes 1179680 | tf_op jit(solution)/shard_map/ppermute | solution.py:62
  75.7 11.2 %collective-permute-done.4 = bf16[784,384]{1,0:T(8,128)(2,1)S(1)} collective-permute-done((bf16[784,384]{1,0:T(8,128)(2,1)S(1)}, bf16[784,384]{1,0:T(8,128)(2,1)S(1)}, u32[]{:S(2)}, u32[]{:S(2)}) %collective-permute-start.4) | collective-permute-done | bytes 602144 | tf_op jit(solution)/shard_map/ppermute | solution.py:72
  86.8 12.9 %collective-permute-done.5 = bf16[784,384]{1,0:T(8,128)(2,1)S(1)} collective-permute-done((bf16[784,384]{1,0:T(8,128)(2,1)S(1)}, bf16[784,384]{1,0:T(8,128)(2,1)S(1)}, u32[]{:S(2)}, u32[]{:S(2)}) %collective-permute-start.5) | collective-permute-done | bytes 602144 | tf_op jit(solution)/shard_map/ppermute | solution.py:72
  105.5 4.0 copy.39
  113.7 4.1 collective-permute-start.11
  123.0 6.4 %collective-permute-done.8 = bf16[3,768,512]{2,1,0:T(8,128)(2,1)} collective-permute-done((bf16[3,768,512]{2,1,0:T(8,128)(2,1)}, bf16[3,768,512]{2,1,0:T(8,128)(2,1)}, u32[]{:S(2)}, u32[]{:S(2)}) %collective-permute-start.8) | collective-permute-done | bytes 2359328 | tf_op jit(solution)/shard_map/ppermute | solution.py:62
  132.7 14.6 %convolution_bitcast_fusion = f32[1152,2304]{1,0:T(8,128)} fusion(bf16[1152,1536]{1,0:T(8,128)(2,1)} %bitcast.127, bf16[1536,2304]{1,0:T(8,128)(2,1)} %all-gather.4.cloned.1.call-done), kind=kOutput, calls=%fused_computation | convolution fusion | flops 8153726976 | bytes 21233664 | tf_op jit(solution)/shard_map/dot_general | solution.py:455
  151.5 13.0 %attend.1 = (bf16[3,96,1536]{2,1,0:T(8,128)(2,1)S(1)}, bf16[3,96,1536]{2,1,0:T(8,128)(2,1)S(1)}, f32[3,2,1,576]{3,2,1,0:T(1,128)S(1)}) custom-call(s32[1]{0:T(128)} %bitcast.1.shift_ref, f32[3,96,1536]{2,1,0:T(8,128)S(1)} %maximum_add_fusion.q_ref, f32[96,128]{1,0:T(8,128)S(1)} %pad_maximum_fusion.16.cos_ref, f32[96,128]{1,0:T(8,128)S(1)} %pad_maximum_fusion.17.sin_ref, ...), custom_call_target="tpu_custom_call" | custom-call | flops 2717908992 | bytes 4718592 | tf_op jit(solution)/shard_map/attend/pallas_call | solution.py:302
  186.2 6.7 %fusion.66 = f32[288,2304]{1,0:T(8,128)} fusion(bf16[288,1536]{1,0:T(8,128)(2,1)S(1)} %multiply_convert_fusion.12, bf16[1536,2304]{1,0:T(8,128)(2,1)} %all-gather.8.cloned.1.call-done), kind=kOutput, calls=%fused_computation.251 | convolution fusion | flops 2038431744 | bytes 10616832 | tf_op jit(solution)/shard_map/dot_general | solution.py:455
  192.9 8.9 %multiply_convert_fusion.9 = (bf16[288,2304]{1,0:T(8,128)(2,1)S(1)}, bf16[288,2304]{1,0:T(8,128)(2,1)S(1)}, bf16[288,2304]{1,0:T(8,128)(2,1)}) fusion(f32[1152,2304]{1,0:T(8,128)} %convolution_bitcast_fusion, s32[]{:T(128)S(6)} %select_n.261, f32[288,2304]{1,0:T(8,128)} %fusion.66, bf16[288,1536]{1,0:T(8,128)(2,1)S(1)} %multiply_convert_fusion.12, ...), kind=kOutput, calls=%fused_computation.37 | convolution fusion | flops 2048385024 | bytes 17252356 | tf_op jit(solution)/shard_map/dot_general | solution.py:455
  214.4 6.4 %multiply_convert_fusion.6 = (bf16[288,2304]{1,0:T(8,128)(2,1)S(1)}, bf16[288,2304]{1,0:T(8,128)(2,1)S(1)}, bf16[288,2304]{1,0:T(8,128)(2,1)}) fusion(f32[1152,2304]{1,0:T(8,128)} %convolution_bitcast_fusion, s32[]{:T(128)S(6)} %select_n.263, f32[288,2304]{1,0:T(8,128)S(1)} %fusion.68, bf16[288,1536]{1,0:T(8,128)(2,1)} %collective-permute-done.13, ...), kind=kOutput, calls=%fused_computation.32 | convolution fusion | flops 2048385024 | bytes 17252356 | tf_op jit(solution)/shard_map/dot_general | solution.py:455
  234.7 6.2 %multiply_convert_fusion.3 = (bf16[288,2304]{1,0:T(8,128)(2,1)S(1)}, bf16[288,2304]{1,0:T(8,128)(2,1)S(1)}, bf16[288,2304]{1,0:T(8,128)(2,1)}) fusion(f32[1152,2304]{1,0:T(8,128)} %convolution_bitcast_fusion, s32[]{:T(128)S(6)} %select_n.265, f32[288,2304]{1,0:T(8,128)S(1)} %fusion.70, bf16[288,1536]{1,0:T(8,128)(2,1)S(1)} %collective-permute-done.14, ...), kind=kOutput, calls=%fused_computation.27 | convolution fusion | flops 2048385024 | bytes 17252356 | tf_op jit(solution)/shard_map/dot_general | solution.py:455
  246.4 4.1 collective-permute-done.15
  253.8 6.2 %multiply_convert_fusion = (bf16[288,2304]{1,0:T(8,128)(2,1)S(1)}, bf16[288,2304]{1,0:T(8,128)(2,1)S(1)}, bf16[288,2304]{1,0:T(8,128)(2,1)}) fusion(f32[1152,2304]{1,0:T(8,128)} %convolution_bitcast_fusion, s32[]{:T(128)S(6)} %select_n.267, f32[288,2304]{1,0:T(8,128)S(1)} %fusion.72, bf16[288,1536]{1,0:T(8,128)(2,1)S(1)} %collective-permute-done.15, ...), kind=kOutput, calls=%fused_computation.22 | convolution fusion | flops 2048385024 | bytes 17252356 | tf_op jit(solution)/shard_map/dot_general | solution.py:455
  270.9 6.4 %convolution_convert_fusion.6 = bf16[768,2304]{1,0:T(8,128)(2,1)} fusion(bf16[1152,2304]{1,0:T(8,128)(2,1)S(1)} %constant_dynamic-update-slice_fusion.30, bf16[1152,1536]{1,0:T(8,128)(2,1)S(1)} %bitcast.128, s32[]{:T(128)S(6)} %select_n.256), kind=kOutput, calls=%fused_computation.7 | convolution fusion | flops 4078632960 | bytes 10616836 | tf_op jit(solution)/shard_map/dot_general | solution.py:463
  277.3 6.4 %convolution_convert_fusion.5 = bf16[768,2304]{1,0:T(8,128)(2,1)} fusion(bf16[1152,2304]{1,0:T(8,128)(2,1)S(1)} %constant_dynamic-update-slice_fusion.30, bf16[1152,1536]{1,0:T(8,128)(2,1)S(1)} %bitcast.129, s32[]{:T(128)S(6)} %select_n.255), kind=kOutput, calls=%fused_computation.6 | convolution fusion | flops 4078632960 | bytes 10616836 | tf_op jit(solution)/shard_map/dot_general | solution.py:463
  283.6 10.0 %convolution_convert_fusion = bf16[1152,1536]{1,0:T(8,128)(2,1)} fusion(bf16[1152,2304]{1,0:T(8,128)(2,1)S(1)} %constant_dynamic-update-slice_fusion.30, bf16[1536,2304]{1,0:T(8,128)(2,1)S(1)} %bitcast.141), kind=kOutput, calls=%fused_computation.1 | convolution fusion | flops 8155496448 | bytes 15925248 | tf_op jit(solution)/shard_map/dot_general | solution.py:459
  301.8 6.4 %convolution_convert_fusion.4 = bf16[768,2304]{1,0:T(8,128)(2,1)} fusion(bf16[1152,2304]{1,0:T(8,128)(2,1)S(1)} %constant_dynamic-update-slice_fusion.22, bf16[1152,1536]{1,0:T(8,128)(2,1)S(1)} %constant_dynamic-update-slice_fusion.26, s32[]{:T(128)S(6)} %select_n.256), kind=kOutput, calls=%fused_computation.5 | convolution fusion | flops 4078632960 | bytes 10616836 | tf_op jit(solution)/shard_map/dot_general | solution.py:463
  308.2 5.5 convolution_convert_fusion.3
  318.6 6.4 %convolution_convert_fusion.2 = bf16[768,2304]{1,0:T(8,128)(2,1)} fusion(bf16[1152,2304]{1,0:T(8,128)(2,1)S(1)} %constant_dynamic-update-slice_fusion.18, bf16[1152,1536]{1,0:T(8,128)(2,1)S(1)} %constant_dynamic-update-slice_fusion.26, s32[]{:T(128)S(6)} %select_n.256), kind=kOutput, calls=%fused_computation.3 | convolution fusion | flops 4078632960 | bytes 10616836 | tf_op jit(solution)/shard_map/dot_general | solution.py:463
  326.3 6.5 %convolution_convert_fusion.1 = bf16[768,2304]{1,0:T(8,128)(2,1)} fusion(bf16[1152,2304]{1,0:T(8,128)(2,1)S(1)} %constant_dynamic-update-slice_fusion.18, bf16[1152,1536]{1,0:T(8,128)(2,1)S(1)} %constant_dynamic-update-slice_fusion.26, s32[]{:T(128)S(6)} %select_n.255), kind=kOutput, calls=%fused_computation.2 | convolution fusion | flops 4078632960 | bytes 10616836 | tf_op jit(solution)/shard_map/dot_general | solution.py:463
  350.7 20.9 %attend_back.1 = (bf16[3,96,1536]{2,1,0:T(8,128)(2,1)S(1)}, bf16[3,768,512]{2,1,0:T(8,128)(2,1)S(1)}, bf16[3,768,512]{2,1,0:T(8,128)(2,1)}) custom-call(s32[1]{0:T(128)} %bitcast.1.shift_ref, bf16[3,96,1536]{2,1,0:T(8,128)(2,1)S(1)} %copy-done.25, bf16[3,96,1536]{2,1,0:T(8,128)(2,1)S(1)} %pad_maximum_fusion.6.og_ref, f32[96,128]{1,0:T(8,128)S(1)} %copy-done.12, ...), custom_call_target="tpu_custom_call" | custom-call | flops 6794772480 | bytes 9437184 | tf_op jit(solution)/shard_map/attend_back/pallas_call | solution.py:392
  385.5 31.1 %collective-permute-done.21 = bf16[3,768,512]{2,1,0:T(8,128)(2,1)} collective-permute-done((bf16[3,768,512]{2,1,0:T(8,128)(2,1)}, bf16[3,768,512]{2,1,0:T(8,128)(2,1)}, u32[]{:S(2)}, u32[]{:S(2)}) %collective-permute-start.21) | collective-permute-done | bytes 2359328 | tf_op jit(solution)/shard_map/ppermute | solution.py:62
  418.5 3.7 fusion.54
  428.1 9.9 %collective-permute-done.23 = bf16[3,384,512]{2,1,0:T(8,128)(2,1)S(1)} collective-permute-done((bf16[3,384,512]{2,1,0:T(8,128)(2,1)S(1)}, bf16[3,384,512]{2,1,0:T(8,128)(2,1)S(1)}, u32[]{:S(2)}, u32[]{:S(2)}) %collective-permute-start.23) | collective-permute-done | bytes 1179680 | tf_op jit(solution)/shard_map/ppermute | solution.py:62
  453.7 14.8 %collective-permute-done.25 = bf16[3,96,512]{2,1,0:T(8,128)(2,1)S(1)} collective-permute-done((bf16[3,96,512]{2,1,0:T(8,128)(2,1)S(1)}, bf16[3,96,512]{2,1,0:T(8,128)(2,1)S(1)}, u32[]{:S(2)}, u32[]{:S(2)}) %collective-permute-start.25) | collective-permute-done | bytes 294944 | tf_op jit(solution)/shard_map/ppermute | solution.py:72
  482.3 4.5 collective-permute-done.30
  497.8 5.0 multiply_add_fusion
  519.4 15.4 %collective-permute-done.38 = bf16[192,768]{1,0:T(8,128)(2,1)} collective-permute-done((bf16[192,768]{1,0:T(8,128)(2,1)}, bf16[192,768]{1,0:T(8,128)(2,1)}, u32[]{:S(2)}, u32[]{:S(2)}) %collective-permute-start.38) | collective-permute-done | bytes 294944 | tf_op jit(solution)/shard_map/ppermute | solution.py:72
  534.8 4.4 collective-permute-done.39
  (465 shorter events, 237.7 us)
Async XLA Ops:
  7.2 125.5 %all-gather.4.cloned.1.call-start = ((), (), s32[]{:S(2)}) async-start(), calls=%async_computation.2 | async-start | bytes 7962624 | tf_op jit(solution)/shard_map/all_gather | solution.py:548
  9.6 176.6 %all-gather.8.cloned.1.call-start = ((), (), s32[]{:S(2)}) async-start(), calls=%async_computation.4 | async-start | bytes 7962624 | tf_op jit(solution)/shard_map/all_gather | solution.py:548
  10.7 182.2 %all-gather.6.cloned.1.call-start = ((), (), s32[]{:S(2)}) async-start(), calls=%async_computation.3 | async-start | bytes 7962624 | tf_op jit(solution)/shard_map/all_gather | solution.py:548
  13.0 326.1 %reduce-scatter.5.cloned.1.call-start = ((), (), s32[]{:S(2)}) async-start(), calls=%async_computation.6 | async-start | bytes 4423680 | tf_op jit(solution)/shard_map/reduce_scatter | solution.py:641
  16.5 21.1 %collective-permute-start.1 = (bf16[3,96,512]{2,1,0:T(8,128)(2,1)S(1)}, bf16[3,96,512]{2,1,0:T(8,128)(2,1)S(1)}, u32[]{:S(2)}, u32[]{:S(2)}) collective-permute-start(bf16[3,96,512]{2,1,0:T(8,128)(2,1)S(1)} %get-tuple-element.121), channel_id=1, source_target_pairs={{0,2},{1,3},{2,0},{3,1},{4,6},{5,7},{6,4},{7,5},{8,10},{9,11},{10,... | collective-permute-start | bytes 884744 | tf_op jit(solution)/shard_map/ppermute | solution.py:72
  19.0 24.9 %collective-permute-start.2 = (bf16[3,96,512]{2,1,0:T(8,128)(2,1)S(1)}, bf16[3,96,512]{2,1,0:T(8,128)(2,1)S(1)}, u32[]{:S(2)}, u32[]{:S(2)}) collective-permute-start(bf16[3,96,512]{2,1,0:T(8,128)(2,1)S(1)} %get-tuple-element.121), channel_id=1, source_target_pairs={{0,1},{1,2},{2,3},{3,0},{4,5},{5,6},{6,7},{7,4},{8,9},{9,10},{10,1... | collective-permute-start | bytes 884744 | tf_op jit(solution)/shard_map/ppermute | solution.py:72
  44.9 26.7 %collective-permute-start.6 = (bf16[3,384,512]{2,1,0:T(8,128)(2,1)}, bf16[3,384,512]{2,1,0:T(8,128)(2,1)}, u32[]{:S(2)}, u32[]{:S(2)}) collective-permute-start(bf16[3,384,512]{2,1,0:T(8,128)(2,1)} %get-tuple-element.327), channel_id=1, source_target_pairs={{0,4},{4,0},{8,12},{12,8},{16,24},{20,28},{24,16},{28,20},{1,5},{5... | collective-permute-start | bytes 3538952 | tf_op jit(solution)/shard_map/ppermute | solution.py:62
  46.3 29.4 %collective-permute-start.3 = (bf16[784,384]{1,0:T(8,128)(2,1)S(1)}, bf16[784,384]{1,0:T(8,128)(2,1)S(1)}, u32[]{:S(2)}, u32[]{:S(2)}) collective-permute-start(bf16[784,384]{1,0:T(8,128)(2,1)S(1)} %fusion.23), channel_id=1, source_target_pairs={{0,3},{1,0},{2,1},{3,2},{4,7},{5,4},{6,5},{7,6},{8,11},{9,8},{10,9... | collective-permute-start | bytes 1806344 | tf_op jit(solution)/shard_map/ppermute | solution.py:72
  48.0 38.9 %collective-permute-start.4 = (bf16[784,384]{1,0:T(8,128)(2,1)S(1)}, bf16[784,384]{1,0:T(8,128)(2,1)S(1)}, u32[]{:S(2)}, u32[]{:S(2)}) collective-permute-start(bf16[784,384]{1,0:T(8,128)(2,1)S(1)} %fusion.23), channel_id=1, source_target_pairs={{0,2},{1,3},{2,0},{3,1},{4,6},{5,7},{6,4},{7,5},{8,10},{9,11},{10,... | collective-permute-start | bytes 1806344 | tf_op jit(solution)/shard_map/ppermute | solution.py:72
  49.9 49.9 %collective-permute-start.5 = (bf16[784,384]{1,0:T(8,128)(2,1)S(1)}, bf16[784,384]{1,0:T(8,128)(2,1)S(1)}, u32[]{:S(2)}, u32[]{:S(2)}) collective-permute-start(bf16[784,384]{1,0:T(8,128)(2,1)S(1)} %fusion.23), channel_id=1, source_target_pairs={{0,1},{1,2},{2,3},{3,0},{4,5},{5,6},{6,7},{7,4},{8,9},{9,10},{10,1... | collective-permute-start | bytes 1806344 | tf_op jit(solution)/shard_map/ppermute | solution.py:72
  74.6 54.8 %collective-permute-start.8 = (bf16[3,768,512]{2,1,0:T(8,128)(2,1)}, bf16[3,768,512]{2,1,0:T(8,128)(2,1)}, u32[]{:S(2)}, u32[]{:S(2)}) collective-permute-start(bf16[3,768,512]{2,1,0:T(8,128)(2,1)} %get-tuple-element.125), channel_id=1, source_target_pairs={{0,8},{4,12},{8,0},{12,4},{16,20},{20,16},{24,28},{28,24},{1,9},{5... | collective-permute-start | bytes 7077896 | tf_op jit(solution)/shard_map/ppermute | solution.py:62
  113.7 52.7 %collective-permute-start.10 = (bf16[768,384]{1,0:T(8,128)(2,1)}, bf16[768,384]{1,0:T(8,128)(2,1)}, u32[]{:S(2)}, u32[]{:S(2)}) collective-permute-start(bf16[768,384]{1,0:T(8,128)(2,1)} %bitcast.135), channel_id=1, source_target_pairs={{0,2},{1,3},{2,0},{3,1},{4,6},{5,7},{6,4},{7,5},{8,10},{9,11},{10,... | collective-permute-start | bytes 1769480 | tf_op jit(solution)/shard_map/ppermute | solution.py:72
  113.7 52.7 %collective-permute-start.11 = (bf16[768,384]{1,0:T(8,128)(2,1)}, bf16[768,384]{1,0:T(8,128)(2,1)}, u32[]{:S(2)}, u32[]{:S(2)}) collective-permute-start(bf16[768,384]{1,0:T(8,128)(2,1)} %bitcast.136), channel_id=1, source_target_pairs={{0,1},{1,2},{2,3},{3,0},{4,5},{5,6},{6,7},{7,4},{8,9},{9,10},{10,1... | collective-permute-start | bytes 1769480 | tf_op jit(solution)/shard_map/ppermute | solution.py:72
  117.8 50.4 %collective-permute-start.9 = (bf16[768,384]{1,0:T(8,128)(2,1)}, bf16[768,384]{1,0:T(8,128)(2,1)}, u32[]{:S(2)}, u32[]{:S(2)}) collective-permute-start(bf16[768,384]{1,0:T(8,128)(2,1)} %bitcast.137), channel_id=1, source_target_pairs={{0,3},{1,0},{2,1},{3,2},{4,7},{5,4},{6,5},{7,6},{8,11},{9,8},{10,9... | collective-permute-start | bytes 1769480 | tf_op jit(solution)/shard_map/ppermute | solution.py:72
  185.6 21.9 %collective-permute-start.13 = (bf16[288,1536]{1,0:T(8,128)(2,1)S(1)}, bf16[288,1536]{1,0:T(8,128)(2,1)}, u32[]{:S(2)}, u32[]{:S(2)}) collective-permute-start(bf16[288,1536]{1,0:T(8,128)(2,1)S(1)} %multiply_convert_fusion.12), channel_id=1, source_target_pairs={{0,3},{1,0},{2,1},{3,2},{4,7},{5,4},{6,5},{7,6},{8,11},{9,8},{10,9... | collective-permute-start | bytes 2654216 | tf_op jit(solution)/shard_map/ppermute | solution.py:39
  207.5 22.7 %collective-permute-start.14 = (bf16[288,1536]{1,0:T(8,128)(2,1)}, bf16[288,1536]{1,0:T(8,128)(2,1)S(1)}, u32[]{:S(2)}, u32[]{:S(2)}) collective-permute-start(bf16[288,1536]{1,0:T(8,128)(2,1)} %collective-permute-done.13), channel_id=1, source_target_pairs={{0,3},{1,0},{2,1},{3,2},{4,7},{5,4},{6,5},{7,6},{8,11},{9,8},{10,9... | collective-permute-start | bytes 2654216 | tf_op jit(solution)/shard_map/ppermute | solution.py:39
  230.2 20.3 %collective-permute-start.15 = (bf16[288,1536]{1,0:T(8,128)(2,1)S(1)}, bf16[288,1536]{1,0:T(8,128)(2,1)S(1)}, u32[]{:S(2)}, u32[]{:S(2)}) collective-permute-start(bf16[288,1536]{1,0:T(8,128)(2,1)S(1)} %collective-permute-done.14), channel_id=1, source_target_pairs={{0,3},{1,0},{2,1},{3,2},{4,7},{5,4},{6,5},{7,6},{8,11},{9,8},{10,9... | collective-permute-start | bytes 2654216 | tf_op jit(solution)/shard_map/ppermute | solution.py:39
  265.7 232.1 %reduce-scatter.3.cloned.1.call-start = ((), (), s32[]{:S(2)}) async-start(), calls=%async_computation.5 | async-start | bytes 4423680 | tf_op jit(solution)/shard_map/reduce_scatter | solution.py:646
  308.2 24.6 %collective-permute-start.17 = (bf16[768,2304]{1,0:T(8,128)(2,1)}, bf16[768,2304]{1,0:T(8,128)(2,1)S(1)}, u32[]{:S(2)}, u32[]{:S(2)}) collective-permute-start(bf16[768,2304]{1,0:T(8,128)(2,1)} %convolution_convert_fusion.4), channel_id=1, source_target_pairs={{0,16},{16,0},{1,17},{17,1},{2,18},{18,2},{3,19},{19,3},{4,20},{20... | collective-permute-start | bytes 10616840 | tf_op jit(solution)/shard_map/ppermute | solution.py:33
  314.3 21.8 %collective-permute-start.19 = (bf16[384,2304]{1,0:T(8,128)(2,1)S(1)}, bf16[384,2304]{1,0:T(8,128)(2,1)S(1)}, u32[]{:S(2)}, u32[]{:S(2)}) collective-permute-start(bf16[384,2304]{1,0:T(8,128)(2,1)S(1)} %pad_maximum_fusion.3), channel_id=1, source_target_pairs={{0,8},{4,12},{8,0},{12,4},{16,20},{20,16},{24,28},{28,24},{1,9},{5... | collective-permute-start | bytes 5308424 | tf_op jit(solution)/shard_map/ppermute | solution.py:62
  325.0 20.8 %collective-permute-start.18 = (bf16[768,2304]{1,0:T(8,128)(2,1)}, bf16[768,2304]{1,0:T(8,128)(2,1)}, u32[]{:S(2)}, u32[]{:S(2)}) collective-permute-start(bf16[768,2304]{1,0:T(8,128)(2,1)} %convolution_convert_fusion.2), channel_id=1, source_target_pairs={{0,16},{16,0},{1,17},{17,1},{2,18},{18,2},{3,19},{19,3},{4,20},{20... | collective-permute-start | bytes 10616840 | tf_op jit(solution)/shard_map/ppermute | solution.py:33
  337.6 35.3 %collective-permute-start.20 = (bf16[192,2304]{1,0:T(8,128)(2,1)}, bf16[192,2304]{1,0:T(8,128)(2,1)}, u32[]{:S(2)}, u32[]{:S(2)}) collective-permute-start(bf16[192,2304]{1,0:T(8,128)(2,1)} %add_convert_fusion.4), channel_id=1, source_target_pairs={{0,4},{4,0},{8,12},{12,8},{16,24},{20,28},{24,16},{28,20},{1,5},{5... | collective-permute-start | bytes 2654216 | tf_op jit(solution)/shard_map/ppermute | solution.py:62
  350.4 68.1 %collective-permute-start.22 = (bf16[768,2304]{1,0:T(8,128)(2,1)}, bf16[768,2304]{1,0:T(8,128)(2,1)}, u32[]{:S(2)}, u32[]{:S(2)}) collective-permute-start(bf16[768,2304]{1,0:T(8,128)(2,1)} %pad_maximum_fusion), channel_id=1, source_target_pairs={{0,8},{4,12},{8,0},{12,4},{16,20},{20,16},{24,28},{28,24},{1,9},{5... | collective-permute-start | bytes 10616840 | tf_op jit(solution)/shard_map/ppermute | solution.py:62
  373.0 43.6 %collective-permute-start.21 = (bf16[3,768,512]{2,1,0:T(8,128)(2,1)}, bf16[3,768,512]{2,1,0:T(8,128)(2,1)}, u32[]{:S(2)}, u32[]{:S(2)}) collective-permute-start(bf16[3,768,512]{2,1,0:T(8,128)(2,1)} %get-tuple-element.192), channel_id=1, source_target_pairs={{0,8},{4,12},{8,0},{12,4},{16,20},{20,16},{24,28},{28,24},{1,9},{5... | collective-permute-start | bytes 7077896 | tf_op jit(solution)/shard_map/ppermute | solution.py:62
  381.9 63.8 %collective-permute-start.27 = (bf16[768,1536]{1,0:T(8,128)(2,1)S(1)}, bf16[768,1536]{1,0:T(8,128)(2,1)S(1)}, u32[]{:S(2)}, u32[]{:S(2)}) collective-permute-start(bf16[768,1536]{1,0:T(8,128)(2,1)S(1)} %convolution_convert_fusion.10), channel_id=1, source_target_pairs={{0,16},{16,0},{1,17},{17,1},{2,18},{18,2},{3,19},{19,3},{4,20},{20... | collective-permute-start | bytes 7077896 | tf_op jit(solution)/shard_map/ppermute | solution.py:33
  385.4 60.4 %collective-permute-start.29 = (bf16[768,1536]{1,0:T(8,128)(2,1)S(1)}, bf16[768,1536]{1,0:T(8,128)(2,1)S(1)}, u32[]{:S(2)}, u32[]{:S(2)}) collective-permute-start(bf16[768,1536]{1,0:T(8,128)(2,1)S(1)} %convolution_convert_fusion.8), channel_id=1, source_target_pairs={{0,16},{16,0},{1,17},{17,1},{2,18},{18,2},{3,19},{19,3},{4,20},{20... | collective-permute-start | bytes 7077896 | tf_op jit(solution)/shard_map/ppermute | solution.py:33
  441.4 27.1 %collective-permute-start.25 = (bf16[3,96,512]{2,1,0:T(8,128)(2,1)S(1)}, bf16[3,96,512]{2,1,0:T(8,128)(2,1)S(1)}, u32[]{:S(2)}, u32[]{:S(2)}) collective-permute-start(bf16[3,96,512]{2,1,0:T(8,128)(2,1)S(1)} %get-tuple-element.311), channel_id=1, source_target_pairs={{0,2},{1,3},{2,0},{3,1},{4,6},{5,7},{6,4},{7,5},{8,10},{9,11},{10,... | collective-permute-start | bytes 884744 | tf_op jit(solution)/shard_map/ppermute | solution.py:72
  444.4 26.2 %collective-permute-start.26 = (bf16[3,96,512]{2,1,0:T(8,128)(2,1)S(1)}, bf16[3,96,512]{2,1,0:T(8,128)(2,1)S(1)}, u32[]{:S(2)}, u32[]{:S(2)}) collective-permute-start(bf16[3,96,512]{2,1,0:T(8,128)(2,1)S(1)} %get-tuple-element.310), channel_id=1, source_target_pairs={{0,3},{1,0},{2,1},{3,2},{4,7},{5,4},{6,5},{7,6},{8,11},{9,8},{10,9... | collective-permute-start | bytes 884744 | tf_op jit(solution)/shard_map/ppermute | solution.py:72
  449.5 37.5 %collective-permute-start.31 = (bf16[768,1536]{1,0:T(8,128)(2,1)}, bf16[768,1536]{1,0:T(8,128)(2,1)}, u32[]{:S(2)}, u32[]{:S(2)}) collective-permute-start(bf16[768,1536]{1,0:T(8,128)(2,1)} %pad_maximum_fusion.1), channel_id=1, source_target_pairs={{0,8},{4,12},{8,0},{12,4},{16,20},{20,16},{24,28},{28,24},{1,9},{5... | collective-permute-start | bytes 7077896 | tf_op jit(solution)/shard_map/ppermute | solution.py:62
  502.8 38.6 %collective-permute-start.40 = (bf16[384,2304]{1,0:T(8,128)(2,1)}, bf16[384,2304]{1,0:T(8,128)(2,1)S(1)}, u32[]{:S(2)}, u32[]{:S(2)}) collective-permute-start(bf16[384,2304]{1,0:T(8,128)(2,1)} %pad_maximum_fusion.4), channel_id=1, source_target_pairs={{0,4},{4,0},{8,12},{12,8},{16,24},{20,28},{24,16},{28,20},{1,5},{5... | collective-permute-start | bytes 5308424 | tf_op jit(solution)/shard_map/ppermute | solution.py:62
  512.0 22.8 %collective-permute-start.38 = (bf16[192,768]{1,0:T(8,128)(2,1)}, bf16[192,768]{1,0:T(8,128)(2,1)}, u32[]{:S(2)}, u32[]{:S(2)}) collective-permute-start(bf16[192,768]{1,0:T(8,128)(2,1)} %pad_maximum_fusion.10), channel_id=1, source_target_pairs={{0,2},{1,3},{2,0},{3,1},{4,6},{5,7},{6,4},{7,5},{8,10},{9,11},{10,... | collective-permute-start | bytes 884744 | tf_op jit(solution)/shard_map/ppermute | solution.py:72
  513.9 25.3 %collective-permute-start.39 = (bf16[192,768]{1,0:T(8,128)(2,1)}, bf16[192,768]{1,0:T(8,128)(2,1)}, u32[]{:S(2)}, u32[]{:S(2)}) collective-permute-start(bf16[192,768]{1,0:T(8,128)(2,1)} %pad_maximum_fusion.11), channel_id=1, source_target_pairs={{0,3},{1,0},{2,1},{3,2},{4,7},{5,4},{6,5},{7,6},{8,11},{9,8},{10,9... | collective-permute-start | bytes 884744 | tf_op jit(solution)/shard_map/ppermute | solution.py:72
  (116 other events, 1225.7 us)
Sparse Core Ops, SparseCore 0:
  10.5 56.0 all-gather.3
  69.1 65.0 all-gather.7
  136.1 48.8 all-gather.5
  265.8 71.2 reduce-scatter.4
  376.0 71.3 reduce-scatter.2
